TPU v7x, 32 devices: a whole 2x2x4 slice. The times are simulated.
32 devices in a mesh: pts: 8 (over z, x), nbr: 4 (over y, core).
Axes of the slice: x: 2, y: 2, z: 4, core: 2. Of those that a mesh axis runs over, the one named last changes fastest.
Arguments:
- points: bfloat16 [8, 4, 4096, 128], P('pts', 'nbr'), may hold values from -6 to 6
- dest_owner: int32 [8, 4, 4096, 1], P('pts', 'nbr'), may hold values from 0 to 31; in each aligned block of 4096 rows (0 to 4095, 4096 to 8191, ..., all dimensions but the last counted through in order) at most 256 rows name the same one
- dest_cell: int32 [8, 4, 4096], P('pts', 'nbr'), may hold values from 0 to 8191
- level_input: bfloat16 [64, 256, 16, 128], P('nbr', 'pts'), may hold values from -6 to 6
- w_res: bfloat16 [27, 128, 128], replicated, may hold values from -0.109375 to 0.109375
- w_down: bfloat16 [27, 128, 256], replicated, may hold values from -0.109375 to 0.109375
Outputs:
- lowered: bfloat16 [32, 128, 8, 256], P('nbr', 'pts')
Inputs may be any that keep to these rules, and one draw needn't show every extreme that they name: `dest_owner`: at most 256 points of one device go to one owner, and some device sends exactly 256 points to some owner.
All inputs are finite; a program needn't handle non-finite values.
Results may differ from a plain program's by a relative error of at most 0.0048.
Values may be sent and summed in bfloat16 or wider, within the bound.
No kernel may reach another device: no remote copies, remote signals or barrier semaphores. Data moves between devices by JAX's collectives and lax.ppermute only.
A program may use at most 64 MiB of HBM per device.

v0:
```python
import functools
import jax
import jax.numpy as jnp
from jax import lax
from jax.experimental import pallas as pl
from jax.experimental.pallas import tpu as pltpu
from jax.sharding import PartitionSpec as P

LANES = 128
EXTRA = 8


def pack_kernel(devices, cap, owner_ref, cell_ref, rows_ref, out_ref,
                wide, spread, slot_vmem, slot_smem, sem):
    p_local, channels = rows_ref.shape
    blocks = p_local // LANES
    stride = cap + EXTRA
    upper = (lax.broadcasted_iota(jnp.int32, (LANES, LANES), 0)
             <= lax.broadcasted_iota(jnp.int32, (LANES, LANES), 1)).astype(jnp.bfloat16)
    ids = lax.broadcasted_iota(jnp.int32, (devices, LANES), 0)
    spots = lax.broadcasted_iota(jnp.int32, (cap, LANES), 0)
    base = jnp.zeros((devices, 1), jnp.float32)
    table = jnp.zeros((2 * devices, cap), jnp.float32)
    for b in range(blocks):
        own = owner_ref[b:b + 1, :]
        cell = cell_ref[b:b + 1, :]
        hit = ids == own
        hot = hit.astype(jnp.float32)
        run = jnp.dot(hot.astype(jnp.bfloat16), upper, preferred_element_type=jnp.float32)
        place = jnp.sum(hot * (run + base), axis=0, keepdims=True).astype(jnp.int32) - 1
        base = base + run[:, LANES - 1:LANES]
        slot_vmem[b:b + 1, :] = own * stride + place
        high = jnp.where(hit, (cell // LANES + 1).astype(jnp.float32), 0.0)
        low = jnp.where(hit, (cell % LANES).astype(jnp.float32), 0.0)
        left = jnp.concatenate([high, low], axis=0).astype(jnp.bfloat16)
        right = (spots == place).astype(jnp.float32).astype(jnp.bfloat16)
        table = table + lax.dot_general(left, right, (((1,), (1,)), ((), ())),
                                        preferred_element_type=jnp.float32)
    copy = pltpu.make_async_copy(slot_vmem, slot_smem, sem)
    copy.start()
    wide[...] = rows_ref[...].astype(jnp.float32)
    per = -(-cap // LANES)
    for part in range(2):
        for j in range(per):
            width = min(LANES, cap - j * LANES)
            piece = table[part * devices:(part + 1) * devices, j * LANES:j * LANES + width]
            if width < LANES:
                piece = jnp.concatenate(
                    [piece, jnp.zeros((devices, LANES - width), jnp.float32)], axis=1)
            spread[pl.ds(cap + part * per + j, devices, stride=stride), :] = piece
    copy.wait()

    def step(b, carry):
        for u in range(LANES):
            spread[pl.ds(slot_smem[b, u], 1), :] = wide[pl.ds(b * LANES + u, 1), :]
        return carry

    lax.fori_loop(0, blocks, step, 0)
    out_ref[...] = spread[...].astype(jnp.bfloat16)


def pack(owner, cell, rows, devices, cap):
    p_local, channels = rows.shape
    blocks = p_local // LANES
    total = devices * (cap + EXTRA)
    vm = pl.BlockSpec(memory_space=pltpu.VMEM)
    return pl.pallas_call(
        functools.partial(pack_kernel, devices, cap),
        out_shape=jax.ShapeDtypeStruct((total, channels), jnp.bfloat16),
        in_specs=[vm, vm, vm],
        out_specs=vm,
        scratch_shapes=[
            pltpu.VMEM((p_local, channels), jnp.float32),
            pltpu.VMEM((total, channels), jnp.float32),
            pltpu.VMEM((blocks, LANES), jnp.int32),
            pltpu.SMEM((blocks, LANES), jnp.int32),
            pltpu.SemaphoreType.DMA,
        ],
        name="pack",
        cost_estimate=pl.CostEstimate(flops=10**8, bytes_accessed=4 * 10**6, transcendentals=0),
    )(owner.reshape(blocks, LANES), cell.reshape(blocks, LANES), rows)


WAYS = 4


def add_kernel(devices, cap, cells, got_ref, base_hbm, out_ref, wide, slot_vmem, slot_smem,
               sem, sem2, *sums):
    channels = got_ref.shape[-1]
    stride = cap + EXTRA
    per = -(-cap // LANES)
    first = pltpu.make_async_copy(base_hbm, sums[0].at[pl.ds(0, cells)], sem2)
    first.start()
    wide[...] = got_ref[...].astype(jnp.float32)
    for j in range(per):
        width = min(LANES, cap - j * LANES)
        high = wide[pl.ds(cap + j, devices, stride=stride), :].astype(jnp.int32)
        low = wide[pl.ds(cap + per + j, devices, stride=stride), :].astype(jnp.int32)
        spot = jnp.where(high > 0, (high - 1) * LANES + low, cells)
        slot_vmem[:, j * LANES:j * LANES + width] = spot[:, :width]
    copy = pltpu.make_async_copy(slot_vmem, slot_smem, sem)
    copy.start()
    for s in sums[1:]:
        s[...] = jnp.zeros_like(s)
    copy.wait()
    first.wait()

    def step(o, carry):
        def inner(q, carry):
            for u in range(32):
                at = slot_smem[o, q * 32 + u]
                s = sums[u % len(sums)]
                s[pl.ds(at, 1), :] += wide[pl.ds(o * stride + q * 32 + u, 1), :]
            return carry
        return lax.fori_loop(0, cap // 32, inner, carry)

    lax.fori_loop(0, devices, step, 0)
    total = sums[0][pl.ds(0, cells), :]
    for s in sums[1:]:
        total = total + s[pl.ds(0, cells), :]
    out_ref[...] = total.astype(jnp.bfloat16)


def add_rows(got, base, devices, cap):
    cells, channels = base.shape
    vm = pl.BlockSpec(memory_space=pltpu.VMEM)
    total = devices * (cap + EXTRA)
    return pl.pallas_call(
        functools.partial(add_kernel, devices, cap, cells),
        out_shape=jax.ShapeDtypeStruct((cells, channels), jnp.bfloat16),
        in_specs=[vm, pl.BlockSpec(memory_space=pl.ANY)],
        out_specs=vm,
        scratch_shapes=[
            pltpu.VMEM((total, channels), jnp.float32),
            pltpu.VMEM((devices, cap), jnp.int32),
            pltpu.SMEM((devices, cap), jnp.int32),
            pltpu.SemaphoreType.DMA,
            pltpu.SemaphoreType.DMA,
        ] + [pltpu.VMEM((cells + 8, channels), jnp.float32)] * WAYS,
        name="add_rows",
        cost_estimate=pl.CostEstimate(flops=10**8, bytes_accessed=8 * 10**6, transcendentals=0),
    )(got, base)

def extended_2(block, sides, width):
    for axis, dim in sides:
        count = lax.axis_size(axis)
        forward = [(i, i + 1) for i in range(count - 1)]
        backward = [(target, source) for source, target in forward]
        low = lax.ppermute(
            lax.slice_in_dim(block, block.shape[dim] - width, None, axis=dim), axis, forward
        )
        high = lax.ppermute(lax.slice_in_dim(block, 0, width, axis=dim), axis, backward)
        block = jnp.concatenate([low, block, high], axis=dim)
    return block


def passed_along(array, axis, by):
    count = lax.axis_size(axis)
    pairs = [(i, i + by) for i in range(count) if 0 <= i + by < count]
    return lax.ppermute(array, axis, pairs)


def conv_valid(source, kernel, stride):
    return lax.conv_general_dilated(
        source[None],
        kernel,
        (stride, stride, stride),
        "VALID",
        dimension_numbers=("NDHWC", "DHWIO", "NDHWC"),
        preferred_element_type=jnp.float32,
    )[0]


def body(points, dest_owner, dest_cell, level_input, w_res, w_down):
    devices = lax.axis_size("pts") * lax.axis_size("nbr")
    channels = points.shape[-1]
    rows = points.reshape(-1, channels)
    capacity = 2 * rows.shape[0] // devices
    outgoing = pack(dest_owner.reshape(-1), dest_cell.reshape(-1), rows, devices, capacity)
    got = lax.all_to_all(
        outgoing.reshape(devices, capacity + EXTRA, channels),
        ("pts", "nbr"),
        split_axis=0,
        concat_axis=0,
        tiled=True,
    ).reshape(outgoing.shape)
    span_x, span_y, span_z = level_input.shape[:3]
    cells = span_x * span_y * span_z
    padded = extended_2(level_input, (("pts", 1), ("nbr", 0)), 1)
    padded = jnp.pad(padded, ((0, 0), (0, 0), (1, 1), (0, 0)))
    kernel = w_res.reshape(3, 3, 3, channels, channels)
    residual = conv_valid(padded, kernel, 1).reshape(cells, channels)
    base = level_input.reshape(cells, channels).astype(jnp.float32) + jnp.maximum(residual, 0.0)
    joined = add_rows(got, base, devices, capacity)
    joined = joined.reshape(span_x, span_y, span_z, channels)
    front = passed_along(joined[-1:], "nbr", 1)
    extended = jnp.concatenate([front, joined], axis=0)
    side = passed_along(extended[:, -1:], "pts", 1)
    extended = jnp.concatenate([side, extended], axis=1)
    extended = jnp.pad(extended, ((0, 0), (0, 0), (1, 0), (0, 0)))
    down_kernel = w_down.reshape(3, 3, 3, channels, w_down.shape[-1])
    lowered = conv_valid(extended, down_kernel, 2)
    return lowered.astype(jnp.bfloat16)


def solution(mesh):
    return jax.shard_map(
        body,
        mesh=mesh,
        in_specs=(
            P("pts", "nbr", None, None),
            P("pts", "nbr", None, None),
            P("pts", "nbr", None),
            P("nbr", "pts", None, None),
            P(),
            P(),
        ),
        out_specs=P("nbr", "pts", None, None),
        check_vma=False,
    )
```

profile of v0, /device:TPU:12, one launch (start us, length us, event | category | flops | bytes accessed | tf_op | source)
XLA Modules:
  0.0 136.9 jit_solution(1353919708783447455)
XLA Ops:
  0.0 2.3 %copy.7 = bf16[16,32,16,128]{3,1,2,0:T(8,128)(2,1)S(1)} copy(bf16[16,32,16,128]{3,2,1,0:T(8,128)(2,1)} %param.9) | data formatting | bytes 4194304 | tf_op args[3]
  2.3 0.2 fusion.32
  2.5 3.4 %collective-permute-start = (bf16[16,1,16,128]{3,1,2,0:T(2,128)(2,1)S(1)}, bf16[16,1,16,128]{3,1,2,0:T(2,128)(2,1)S(1)}, u32[]{:S(2)}, u32[]{:S(2)}) collective-permute-start(bf16[16,1,16,128]{3,1,2,0:T(2,128)(2,1)S(1)} %get-tuple-element.7), channel_id=1, source_target_pairs={{0,4},{4,8},{8,12},{12,16},{16,20},{20,24},{24,28},{1,5},{5,9},{9,... | collective-permute-start | bytes 196616 | tf_op jit(solution)/shard_map/ppermute | solution.py:149
  5.9 3.3 %collective-permute-start.1 = (bf16[16,1,16,128]{3,1,2,0:T(2,128)(2,1)S(1)}, bf16[16,1,16,128]{3,1,2,0:T(2,128)(2,1)S(1)}, u32[]{:S(2)}, u32[]{:S(2)}) collective-permute-start(bf16[16,1,16,128]{3,1,2,0:T(2,128)(2,1)S(1)} %get-tuple-element.8), channel_id=1, source_target_pairs={{4,0},{8,4},{12,8},{16,12},{20,16},{24,20},{28,24},{5,1},{9,5},{13... | collective-permute-start | bytes 196616 | tf_op jit(solution)/shard_map/ppermute | solution.py:152
  9.3 1.3 collective-permute-done
  10.6 2.7 %collective-permute-done.1 = bf16[16,1,16,128]{3,1,2,0:T(2,128)(2,1)S(1)} collective-permute-done((bf16[16,1,16,128]{3,1,2,0:T(2,128)(2,1)S(1)}, bf16[16,1,16,128]{3,1,2,0:T(2,128)(2,1)S(1)}, u32[]{:S(2)}, u32[]{:S(2)}) %collective-permute-start.1) | collective-permute-done | bytes 65568 | tf_op jit(solution)/shard_map/ppermute | solution.py:152
  13.3 0.2 pad_maximum_fusion.2
  13.5 1.9 %collective-permute-start.2 = (bf16[1,34,16,128]{3,1,2,0:T(8,128)(2,1)S(1)}, bf16[1,34,16,128]{3,1,2,0:T(8,128)(2,1)S(1)}, u32[]{:S(2)}, u32[]{:S(2)}) collective-permute-start(bf16[1,34,16,128]{3,1,2,0:T(8,128)(2,1)S(1)} %get-tuple-element.5), channel_id=1, source_target_pairs={{0,1},{1,2},{2,3},{4,5},{5,6},{6,7},{8,9},{9,10},{10,11},{12,13},{... | collective-permute-start | bytes 417800 | tf_op jit(solution)/shard_map/ppermute | solution.py:149
  15.4 3.6 %collective-permute-start.3 = (bf16[1,34,16,128]{3,1,2,0:T(8,128)(2,1)S(1)}, bf16[1,34,16,128]{3,1,2,0:T(8,128)(2,1)S(1)}, u32[]{:S(2)}, u32[]{:S(2)}) collective-permute-start(bf16[1,34,16,128]{3,1,2,0:T(8,128)(2,1)S(1)} %get-tuple-element.6), channel_id=1, source_target_pairs={{1,0},{2,1},{3,2},{5,4},{6,5},{7,6},{9,8},{10,9},{11,10},{13,12},{... | collective-permute-start | bytes 417800 | tf_op jit(solution)/shard_map/ppermute | solution.py:152
  19.1 9.2 %pack.1 = bf16[8448,128]{1,0:T(8,128)(2,1)} custom-call(s32[32,128]{1,0:T(8,128)} %bitcast.37, s32[32,128]{1,0:T(8,128)} %bitcast.38, bf16[4096,128]{1,0:T(8,128)(2,1)} %bitcast.35), custom_call_target="tpu_custom_call" | custom-call | flops 100000000 | bytes 4000000 | tf_op jit(solution)/shard_map/pack/pallas_call | solution.py:67
  28.3 5.4 %all-to-all-start = ((bf16[32,264,128]{2,1,0:T(8,128)(2,1)}), bf16[32,264,128]{2,1,0:T(8,128)(2,1)}, u32[]{:S(2)}, u32[]{:S(2)}) async-start(bf16[32,264,128]{2,1,0:T(8,128)(2,1)} %bitcast.32), calls=%async_computation | async-start | bytes 4325376 | tf_op jit(solution)/shard_map/all_to_all | solution.py:180
  33.7 0.0 copy-start.4
  33.7 4.5 %fusion.21 = bf16[1,18,34,18,128]{4,2,3,1,0:T(8,128)(2,1)S(1)} fusion(bf16[1,34,16,128]{3,1,2,0:T(8,128)(2,1)S(1)} %collective-permute-done.3, bf16[1,34,16,128]{3,1,2,0:T(8,128)(2,1)S(1)} %collective-permute-done.2, bf16[16,1,16,128]{3,1,2,0:T(2,128)(2,1)S(1)} %collective-permute-done.1, bf16[16,32,16,128]{3,1,2,0:T(8,128)(2,1)} %copy-done.1, ...), kind=kLoop, calls=%fused_computation.24 | loop fusion | flops 25380864 | bytes 5326848 | tf_op jit(solution)/shard_map/broadcast_in_dim | solution.py:165
  38.2 0.0 copy-start.3
  38.3 44.0 %fusion.14 = f32[1,16,32,16,128]{4,0,3,2,1:T(1,128)S(1)} fusion(bf16[3,3,3,128,128]{4,3,2,1,0:T(8,128)(2,1)S(1)} %bitcast.39, bf16[1,18,34,18,128]{4,2,3,1,0:T(8,128)(2,1)S(1)} %fusion.21), kind=kOutput, calls=%fused_computation.18 | convolution fusion | flops 7248805888 | bytes 7899136 | tf_op jit(solution)/shard_map/conv_general_dilated | solution.py:164
  82.3 2.4 %convert_add_fusion.base_hbm = f32[8192,128]{1,0:T(8,128)} fusion(f32[8192,128]{1,0:T(8,128)S(1)} %bitcast.33, bf16[16,32,16,128]{3,2,1,0:T(8,128)(2,1)S(1)} %copy-done.3), kind=kLoop, calls=%fused_computation.17 | loop fusion | flops 2097152 | bytes 10485760 | tf_op jit(solution)/shard_map/add | solution.py:193
  84.7 27.4 %add_rows.1 = bf16[8192,128]{1,0:T(8,128)(2,1)} custom-call(bf16[8448,128]{1,0:T(8,128)(2,1)} %bitcast.4.got_ref, f32[8192,128]{1,0:T(8,128)} %convert_add_fusion.base_hbm), custom_call_target="tpu_custom_call" | custom-call | flops 100000000 | bytes 8000000 | tf_op jit(solution)/shard_map/add_rows/pallas_call | solution.py:128
  112.2 1.1 slice.32
  113.2 2.0 %collective-permute-start.4 = (bf16[1,32,16,128]{3,2,1,0:T(8,128)(2,1)S(1)}, bf16[1,32,16,128]{3,2,1,0:T(8,128)(2,1)S(1)}, u32[]{:S(2)}, u32[]{:S(2)}) collective-permute-start(bf16[1,32,16,128]{3,2,1,0:T(8,128)(2,1)S(1)} %bitcast.36), channel_id=1, source_target_pairs={{0,1},{1,2},{2,3},{4,5},{5,6},{6,7},{8,9},{9,10},{10,11},{12,13},{... | collective-permute-start | bytes 393224 | tf_op jit(solution)/shard_map/ppermute | solution.py:160
  115.3 4.3 %collective-permute-done.4 = bf16[1,32,16,128]{3,2,1,0:T(8,128)(2,1)S(1)} collective-permute-done((bf16[1,32,16,128]{3,2,1,0:T(8,128)(2,1)S(1)}, bf16[1,32,16,128]{3,2,1,0:T(8,128)(2,1)S(1)}, u32[]{:S(2)}, u32[]{:S(2)}) %collective-permute-start.4) | collective-permute-done | bytes 131104 | tf_op jit(solution)/shard_map/ppermute | solution.py:160
  119.5 0.8 pad_maximum_fusion.3
  120.4 3.4 %collective-permute-start.5 = (bf16[17,1,16,128]{3,2,1,0:T(8,128)(2,1)S(1)}, bf16[17,1,16,128]{3,2,1,0:T(8,128)(2,1)S(1)}, u32[]{:S(2)}, u32[]{:S(2)}) collective-permute-start(bf16[17,1,16,128]{3,2,1,0:T(8,128)(2,1)S(1)} %pad_maximum_fusion.3), channel_id=1, source_target_pairs={{0,4},{4,8},{8,12},{12,16},{16,20},{20,24},{24,28},{1,5},{5,9},{9,... | collective-permute-start | bytes 208904 | tf_op jit(solution)/shard_map/ppermute | solution.py:160
  123.7 3.7 %collective-permute-done.5 = bf16[17,1,16,128]{3,2,1,0:T(8,128)(2,1)S(1)} collective-permute-done((bf16[17,1,16,128]{3,2,1,0:T(8,128)(2,1)S(1)}, bf16[17,1,16,128]{3,2,1,0:T(8,128)(2,1)S(1)}, u32[]{:S(2)}, u32[]{:S(2)}) %collective-permute-start.5) | collective-permute-done | bytes 69664 | tf_op jit(solution)/shard_map/ppermute | solution.py:160
  127.5 1.7 %fusion.18 = bf16[17,33,1,17,128]{4,3,1,0,2:T(8,128)(2,1)S(1)} fusion(bf16[17,1,16,128]{3,2,1,0:T(8,128)(2,1)S(1)} %collective-permute-done.5, bf16[16,32,16,128]{3,2,1,0:T(8,128)(2,1)S(1)} %bitcast.30, bf16[1,32,16,128]{3,2,1,0:T(8,128)(2,1)S(1)} %collective-permute-done.4), kind=kLoop, calls=%fused_computation.20 | loop fusion | flops 12207360 | bytes 4739328 | tf_op jit(solution)/shard_map/broadcast_in_dim | solution.py:165
  129.2 0.7 pad.10
  129.9 0.8 copy.12
  130.7 0.0 copy-start.5
  130.7 0.6 slice.33
  131.3 0.0 copy-done.5
  131.3 4.2 %select_convert_fusion = bf16[8,16,8,2,256]{4,2,3,1,0:T(8,128)(2,1)S(1)} fusion(bf16[3,3,3,128,256]{4,3,2,1,0:T(8,128)(2,1)S(1)} %bitcast.28, bf16[17,33,1,7,2,128]{5,3,4,1,0,2:T(8,128)(2,1)S(1)} %slice.33, bf16[17,33,1,8,4,128]{5,3,4,1,0,2:T(8,128)(2,1)S(1)} %copy.12, pred[8,2]{0,1:T(4,128)(4,1)S(1)} %copy-done.5), kind=kOutput, calls=%fused_computation.31 | convolution fusion | flops 3645607936 | bytes 9424400 | tf_op jit(solution)/shard_map/conv_general_dilated | solution.py:164
  135.5 0.4 copy.13
  136.0 1.0 copy.14
  (12 shorter events, 0.1 us)
Async XLA Ops:
  0.0 131.3 %copy-start = (bf16[27,128,256]{2,1,0:T(8,128)(2,1)S(1)}, bf16[27,128,256]{2,1,0:T(8,128)(2,1)}, u32[]{:S(2)}) copy-start(bf16[27,128,256]{2,1,0:T(8,128)(2,1)} %param.11) | copy-start | bytes 5308420
  2.3 11.1 %copy-start.1 = (bf16[16,32,16,128]{3,1,2,0:T(8,128)(2,1)}, bf16[16,32,16,128]{3,1,2,0:T(8,128)(2,1)S(1)}, u32[]{:S(2)}) copy-start(bf16[16,32,16,128]{3,1,2,0:T(8,128)(2,1)S(1)} %copy.7) | copy-start | bytes 6291460
  2.5 8.1 %collective-permute-start = (bf16[16,1,16,128]{3,1,2,0:T(2,128)(2,1)S(1)}, bf16[16,1,16,128]{3,1,2,0:T(2,128)(2,1)S(1)}, u32[]{:S(2)}, u32[]{:S(2)}) collective-permute-start(bf16[16,1,16,128]{3,1,2,0:T(2,128)(2,1)S(1)} %get-tuple-element.7), channel_id=1, source_target_pairs={{0,4},{4,8},{8,12},{12,16},{16,20},{20,24},{24,28},{1,5},{5,9},{9,... | collective-permute-start | bytes 196616 | tf_op jit(solution)/shard_map/ppermute | solution.py:149
  5.9 7.4 %collective-permute-start.1 = (bf16[16,1,16,128]{3,1,2,0:T(2,128)(2,1)S(1)}, bf16[16,1,16,128]{3,1,2,0:T(2,128)(2,1)S(1)}, u32[]{:S(2)}, u32[]{:S(2)}) collective-permute-start(bf16[16,1,16,128]{3,1,2,0:T(2,128)(2,1)S(1)} %get-tuple-element.8), channel_id=1, source_target_pairs={{4,0},{8,4},{12,8},{16,12},{20,16},{24,20},{28,24},{5,1},{9,5},{13... | collective-permute-start | bytes 196616 | tf_op jit(solution)/shard_map/ppermute | solution.py:152
  13.5 20.2 %collective-permute-start.2 = (bf16[1,34,16,128]{3,1,2,0:T(8,128)(2,1)S(1)}, bf16[1,34,16,128]{3,1,2,0:T(8,128)(2,1)S(1)}, u32[]{:S(2)}, u32[]{:S(2)}) collective-permute-start(bf16[1,34,16,128]{3,1,2,0:T(8,128)(2,1)S(1)} %get-tuple-element.5), channel_id=1, source_target_pairs={{0,1},{1,2},{2,3},{4,5},{5,6},{6,7},{8,9},{9,10},{10,11},{12,13},{... | collective-permute-start | bytes 417800 | tf_op jit(solution)/shard_map/ppermute | solution.py:149
  15.4 18.3 %collective-permute-start.3 = (bf16[1,34,16,128]{3,1,2,0:T(8,128)(2,1)S(1)}, bf16[1,34,16,128]{3,1,2,0:T(8,128)(2,1)S(1)}, u32[]{:S(2)}, u32[]{:S(2)}) collective-permute-start(bf16[1,34,16,128]{3,1,2,0:T(8,128)(2,1)S(1)} %get-tuple-element.6), channel_id=1, source_target_pairs={{1,0},{2,1},{3,2},{5,4},{6,5},{7,6},{9,8},{10,9},{11,10},{13,12},{... | collective-permute-start | bytes 417800 | tf_op jit(solution)/shard_map/ppermute | solution.py:152
  28.3 56.4 %all-to-all-start = ((bf16[32,264,128]{2,1,0:T(8,128)(2,1)}), bf16[32,264,128]{2,1,0:T(8,128)(2,1)}, u32[]{:S(2)}, u32[]{:S(2)}) async-start(bf16[32,264,128]{2,1,0:T(8,128)(2,1)} %bitcast.32), calls=%async_computation | async-start | bytes 4325376 | tf_op jit(solution)/shard_map/all_to_all | solution.py:180
  33.7 4.5 %copy-start.4 = (bf16[27,128,128]{2,1,0:T(8,128)(2,1)S(1)}, bf16[27,128,128]{2,1,0:T(8,128)(2,1)}, u32[]{:S(2)}) copy-start(bf16[27,128,128]{2,1,0:T(8,128)(2,1)} %param.10) | copy-start | bytes 2654212
  38.2 44.0 %copy-start.3 = (bf16[16,32,16,128]{3,2,1,0:T(8,128)(2,1)S(1)}, bf16[16,32,16,128]{3,2,1,0:T(8,128)(2,1)}, u32[]{:S(2)}) copy-start(bf16[16,32,16,128]{3,2,1,0:T(8,128)(2,1)} %param.9) | copy-start | bytes 6291460
  112.1 15.3 %copy-start.2 = (bf16[8192,128]{1,0:T(8,128)(2,1)S(1)}, bf16[8192,128]{1,0:T(8,128)(2,1)}, u32[]{:S(2)}) copy-start(bf16[8192,128]{1,0:T(8,128)(2,1)} %add_rows.1) | copy-start | bytes 6291460
  113.2 6.3 %collective-permute-start.4 = (bf16[1,32,16,128]{3,2,1,0:T(8,128)(2,1)S(1)}, bf16[1,32,16,128]{3,2,1,0:T(8,128)(2,1)S(1)}, u32[]{:S(2)}, u32[]{:S(2)}) collective-permute-start(bf16[1,32,16,128]{3,2,1,0:T(8,128)(2,1)S(1)} %bitcast.36), channel_id=1, source_target_pairs={{0,1},{1,2},{2,3},{4,5},{5,6},{6,7},{8,9},{9,10},{10,11},{12,13},{... | collective-permute-start | bytes 393224 | tf_op jit(solution)/shard_map/ppermute | solution.py:160
  120.4 7.1 %collective-permute-start.5 = (bf16[17,1,16,128]{3,2,1,0:T(8,128)(2,1)S(1)}, bf16[17,1,16,128]{3,2,1,0:T(8,128)(2,1)S(1)}, u32[]{:S(2)}, u32[]{:S(2)}) collective-permute-start(bf16[17,1,16,128]{3,2,1,0:T(8,128)(2,1)S(1)} %pad_maximum_fusion.3), channel_id=1, source_target_pairs={{0,4},{4,8},{8,12},{12,16},{16,20},{20,24},{24,28},{1,5},{5,9},{9,... | collective-permute-start | bytes 208904 | tf_op jit(solution)/shard_map/ppermute | solution.py:160
  130.7 0.7 copy-start.5
where the time goes:
time: 137 us
  matrix products  48.2 us (35%)
  Pallas kernels  36.6 us (27%)
  starting transfers between devices  23.1 us (17%)
  waiting for transfers between devices  12.1 us (9%)
  other arithmetic  9.63 us (7%)
  local copies, waits for them, and re-layouts  7.11 us (5%)
    conv_general_dilated x2, matrix products, conv_valid(): lax.conv_general_dilated(source[None], kernel, (stride, stride, stride),...  48.2 us
    pallas_call x1, Pallas kernels, add_rows(): pl.pallas_call(functools.partial(add_kernel, devices, cap, cells), out_sh...  27.4 us
    pallas_call x1, Pallas kernels, pack(): pl.pallas_call(functools.partial(pack_kernel, devices, cap), out_shape=ja...  9.19 us
    ppermute x2, waiting for transfers between devices, passed_along(): return lax.ppermute(array, axis, pairs)  7.98 us
    ppermute x2, starting transfers between devices, extended_2(): lax.ppermute(lax.slice_in_dim(block, 0, width, axis=dim), axis, backward)  6.98 us
    broadcast_in_dim x2, other arithmetic, conv_valid(): source[None]  6.19 us
    all_to_all x1, starting transfers between devices, body(): lax.all_to_all(outgoing.reshape(devices, capacity + EXTRA, channels), ('p...  5.42 us
    ppermute x2, starting transfers between devices, passed_along(): return lax.ppermute(array, axis, pairs)  5.38 us
  transfers between devices with their start and end apart: 7, of which 4 were waited for; matrix products, arithmetic and copies ran while one was open for 37% of the time, Pallas kernels for 7%

commit v1 on v0

--- a/solution.py
+++ b/solution.py
@@ -141,42 +141,187 @@
         cost_estimate=pl.CostEstimate(flops=10**8, bytes_accessed=8 * 10**6, transcendentals=0),
     )(got, base)
 
-def extended_2(block, sides, width):
-    for axis, dim in sides:
-        count = lax.axis_size(axis)
-        forward = [(i, i + 1) for i in range(count - 1)]
-        backward = [(target, source) for source, target in forward]
-        low = lax.ppermute(
-            lax.slice_in_dim(block, block.shape[dim] - width, None, axis=dim), axis, forward
-        )
-        high = lax.ppermute(lax.slice_in_dim(block, 0, width, axis=dim), axis, backward)
-        block = jnp.concatenate([low, block, high], axis=dim)
-    return block
+
+def residual_kernel(group, level_ref, ylow_ref, yhigh_ref, xlow_ref, xhigh_ref, w_ref, out_ref,
+                    plane, taps, wide, result):
+    span_x, span_y, span_z, channels = level_ref.shape
+    half = (span_y + 2) // 2
+    lines = half * span_z
+    three = 3 * channels
+    for a in range(3):
+        for d in range(2):
+            for par in range(2):
+                for c in range(3):
+                    at = ((a * 2 + d) * 2 + par) * three + c * channels
+                    for s in range(2):
+                        b = 2 * d + par - s
+                        if 0 <= b <= 2:
+                            tile = w_ref[9 * a + 3 * b + c]
+                        else:
+                            tile = jnp.zeros((channels, channels), jnp.bfloat16)
+                        wide[at:at + channels, s * channels:(s + 1) * channels] = tile
+    spot = lax.broadcasted_iota(jnp.int32, ((span_y + 2) * span_z, channels), 0) % span_z
+    count = (span_y + 2) * span_z
+    plane[0:8, :] = jnp.zeros((8, channels), jnp.float32)
+    plane[8 + count:16 + count, :] = jnp.zeros((8, channels), jnp.float32)
+
+    def spread(x):
+        middle = plane[8:8 + count, :]
+        low = jnp.where(spot == 0, 0.0, plane[7:7 + count, :])
+        high = jnp.where(spot == span_z - 1, 0.0, plane[9:9 + count, :])
+        for c, value in enumerate((low, middle, high)):
+            value = value.astype(jnp.bfloat16).reshape(half, 2, span_z, channels)
+            for par in range(2):
+                taps[pl.ds(pl.multiple_of(x * lines, 16), lines),
+                     par * three + c * channels:par * three + (c + 1) * channels] = (
+                    value[:, par].reshape(lines, channels))
+
+    for x, ref in ((0, xlow_ref), (span_x + 1, xhigh_ref)):
+        plane[8:8 + count, :] = ref[...].reshape(count, channels).astype(jnp.float32)
+        spread(x)
+
+    def fill(x, carry):
+        plane[8:8 + span_z, :] = ylow_ref[x].reshape(span_z, channels).astype(jnp.float32)
+        plane[8 + span_z:8 + count - span_z, :] = level_ref[x].reshape(
+            span_y * span_z, channels).astype(jnp.float32)
+        plane[8 + count - span_z:8 + count, :] = yhigh_ref[x].reshape(
+            span_z, channels).astype(jnp.float32)
+        spread(x + 1)
+        return carry
+
+    lax.fori_loop(0, span_x, fill, 0)
+    height = group * lines - span_z
+
+    def multiply(g, carry):
+        total = None
+        for a in range(3):
+            for d in range(2):
+                start = pl.multiple_of((g * group + a) * lines + d * span_z, 16)
+                at = (a * 2 + d) * 2 * three
+                part = jnp.dot(taps[pl.ds(start, height), :], wide[at:at + 2 * three, :],
+                               preferred_element_type=jnp.float32)
+                total = part if total is None else total + part
+        result[0:height, :] = total
+        for i in range(group):
+            x = g * group + i
+            for s in range(2):
+                value = result[i * lines:i * lines + span_y // 2 * span_z,
+                               s * channels:(s + 1) * channels]
+                value = jnp.maximum(value, 0.0).reshape(span_y // 2, span_z, channels)
+                here = level_ref[x].reshape(span_y // 2, 2, span_z, channels)[:, s]
+                out_ref[x, :, s] = value + here.astype(jnp.float32)
+        return carry
+
+    lax.fori_loop(0, span_x // group, multiply, 0)
+
+
+def residual_base(level, ylow, yhigh, xlow, xhigh, w_res, group=4):
+    span_x, span_y, span_z, channels = level.shape
+    lines = (span_y + 2) // 2 * span_z
+    vm = pl.BlockSpec(memory_space=pltpu.VMEM)
+    flops = 2 * span_x * span_y * span_z * 27 * channels * channels
+    out = pl.pallas_call(
+        functools.partial(residual_kernel, group),
+        out_shape=jax.ShapeDtypeStruct((span_x, span_y // 2, 2, span_z, channels), jnp.float32),
+        in_specs=[vm] * 6,
+        out_specs=vm,
+        scratch_shapes=[
+            pltpu.VMEM(((span_y + 2) * span_z + 16, channels), jnp.float32),
+            pltpu.VMEM(((span_x + 2) * lines, 6 * channels), jnp.bfloat16),
+            pltpu.VMEM((36 * channels, 2 * channels), jnp.bfloat16),
+            pltpu.VMEM((group * lines, 2 * channels), jnp.float32),
+        ],
+        name="residual",
+        cost_estimate=pl.CostEstimate(flops=flops, bytes_accessed=8 * 10**6, transcendentals=0),
+    )(level, ylow, yhigh, xlow, xhigh, w_res)
+    return out.reshape(span_x * span_y * span_z, channels)
+
+
+def lower_kernel(joined_ref, front_ref, side_ref, corner_ref, w_ref, out_ref, plane, taps):
+    span_x, span_y, span_z, channels = joined_ref.shape
+    half_y, half_z = span_y // 2, span_z // 2
+    lines = half_y * half_z
+    count = (span_y + 1) * span_z
+    zero = lax.broadcasted_iota(jnp.int32, ((span_y + 1) * half_z, channels), 0) % half_z == 0
+    plane[0:8, :] = jnp.zeros((8, channels), jnp.float32)
+
+    def spread(x):
+        rows = (span_y + 1) * half_z
+        low = jnp.where(zero, 0.0, plane[pl.ds(7, rows, stride=2), :])
+        for c, value in enumerate((low, plane[pl.ds(8, rows, stride=2), :],
+                                   plane[pl.ds(9, rows, stride=2), :])):
+            value = value.reshape(span_y + 1, half_z, channels)
+            evens = value[0:span_y].reshape(half_y, 2, half_z, channels)
+            odds = value[1:].reshape(half_y, 2, half_z, channels)
+            for b, piece in enumerate((evens[:, 0], evens[:, 1], odds[:, 1])):
+                at = (b * 3 + c) * channels
+                taps[x, :, at:at + channels] = piece.reshape(lines, channels).astype(jnp.bfloat16)
+
+    plane[8:8 + span_z, :] = corner_ref[...].reshape(span_z, channels).astype(jnp.float32)
+    plane[8 + span_z:8 + count, :] = front_ref[...].reshape(
+        span_y * span_z, channels).astype(jnp.float32)
+    spread(0)
+
+    def fill(x, carry):
+        plane[8:8 + span_z, :] = side_ref[x].reshape(span_z, channels).astype(jnp.float32)
+        plane[8 + span_z:8 + count, :] = joined_ref[x].reshape(
+            span_y * span_z, channels).astype(jnp.float32)
+        spread(x + 1)
+        return carry
+
+    lax.fori_loop(0, span_x, fill, 0)
+    depth = 9 * channels
+
+    def multiply(i, carry):
+        total = None
+        for a in range(3):
+            part = jnp.dot(taps[2 * i + a], w_ref[a * depth:(a + 1) * depth, :],
+                           preferred_element_type=jnp.float32)
+            total = part if total is None else total + part
+        out_ref[i] = total.reshape(half_y, half_z, w_ref.shape[-1]).astype(jnp.bfloat16)
+        return carry
+
+    lax.fori_loop(0, span_x // 2, multiply, 0)
+
+
+def lower(joined, front, side, corner, w_down):
+    span_x, span_y, span_z, channels = joined.shape
+    wide = w_down.shape[-1]
+    vm = pl.BlockSpec(memory_space=pltpu.VMEM)
+    flops = 2 * span_x * span_y * span_z // 8 * 27 * channels * wide
+    return pl.pallas_call(
+        lower_kernel,
+        out_shape=jax.ShapeDtypeStruct((span_x // 2, span_y // 2, span_z // 2, wide),
+                                       jnp.bfloat16),
+        in_specs=[vm] * 5,
+        out_specs=vm,
+        scratch_shapes=[
+            pltpu.VMEM(((span_y + 1) * span_z + 16, channels), jnp.float32),
+            pltpu.VMEM((span_x + 1, span_y * span_z // 4, 9 * channels), jnp.bfloat16),
+        ],
+        name="lower",
+        cost_estimate=pl.CostEstimate(flops=flops, bytes_accessed=5 * 10**6, transcendentals=0),
+    )(joined, front, side, corner, w_down.reshape(-1, wide))
+
+
+def pairs_of(axis, by):
+    count = lax.axis_size(axis)
+    return [(i, i + by) for i in range(count) if 0 <= i + by < count]
 
 
 def passed_along(array, axis, by):
-    count = lax.axis_size(axis)
-    pairs = [(i, i + by) for i in range(count) if 0 <= i + by < count]
-    return lax.ppermute(array, axis, pairs)
-
-
-def conv_valid(source, kernel, stride):
-    return lax.conv_general_dilated(
-        source[None],
-        kernel,
-        (stride, stride, stride),
-        "VALID",
-        dimension_numbers=("NDHWC", "DHWIO", "NDHWC"),
-        preferred_element_type=jnp.float32,
-    )[0]
+    return lax.ppermute(array, axis, pairs_of(axis, by))
 
 
 def body(points, dest_owner, dest_cell, level_input, w_res, w_down):
-    devices = lax.axis_size("pts") * lax.axis_size("nbr")
+    count_pts = lax.axis_size("pts")
+    count_nbr = lax.axis_size("nbr")
+    devices = count_pts * count_nbr
     channels = points.shape[-1]
     rows = points.reshape(-1, channels)
     capacity = 2 * rows.shape[0] // devices
     outgoing = pack(dest_owner.reshape(-1), dest_cell.reshape(-1), rows, devices, capacity)
+    outgoing, level = lax.optimization_barrier((outgoing, level_input))
     got = lax.all_to_all(
         outgoing.reshape(devices, capacity + EXTRA, channels),
         ("pts", "nbr"),
@@ -185,22 +330,24 @@
         tiled=True,
     ).reshape(outgoing.shape)
     span_x, span_y, span_z = level_input.shape[:3]
-    cells = span_x * span_y * span_z
-    padded = extended_2(level_input, (("pts", 1), ("nbr", 0)), 1)
-    padded = jnp.pad(padded, ((0, 0), (0, 0), (1, 1), (0, 0)))
-    kernel = w_res.reshape(3, 3, 3, channels, channels)
-    residual = conv_valid(padded, kernel, 1).reshape(cells, channels)
-    base = level_input.reshape(cells, channels).astype(jnp.float32) + jnp.maximum(residual, 0.0)
+    low_y = passed_along(level[:, -1:], "pts", 1)
+    high_y = passed_along(level[:, :1], "pts", -1)
+    last = jnp.concatenate([low_y[-1:], level[-1:], high_y[-1:]], axis=1)
+    first = jnp.concatenate([low_y[:1], level[:1], high_y[:1]], axis=1)
+    low_x = passed_along(last, "nbr", 1)
+    high_x = passed_along(first, "nbr", -1)
+    base = residual_base(level, low_y, high_y, low_x, high_x, w_res)
     joined = add_rows(got, base, devices, capacity)
     joined = joined.reshape(span_x, span_y, span_z, channels)
     front = passed_along(joined[-1:], "nbr", 1)
-    extended = jnp.concatenate([front, joined], axis=0)
-    side = passed_along(extended[:, -1:], "pts", 1)
-    extended = jnp.concatenate([side, extended], axis=1)
-    extended = jnp.pad(extended, ((0, 0), (0, 0), (1, 0), (0, 0)))
-    down_kernel = w_down.reshape(3, 3, 3, channels, w_down.shape[-1])
-    lowered = conv_valid(extended, down_kernel, 2)
-    return lowered.astype(jnp.bfloat16)
+    side = passed_along(joined[:, -1:], "pts", 1)
+    diagonal = [
+        (i * count_nbr + j, (i + 1) * count_nbr + j + 1)
+        for i in range(count_pts - 1)
+        for j in range(count_nbr - 1)
+    ]
+    corner = lax.ppermute(joined[-1:, -1:], ("pts", "nbr"), diagonal)
+    return lower(joined, front, side, corner, w_down)
 
 
 def solution(mesh):

time: 137 us -> 144 us (1.051)
  matrix products: 48.2 us -> 0 us
  waiting for transfers between devices: 12.1 us -> 38.6 us
  Pallas kernels: 36.6 us -> 61.1 us
  starting transfers between devices: 23.1 us -> 35.4 us
  other arithmetic: 9.63 us -> 0.05 us
    conv_general_dilated x2 -> x0, matrix products: 48.2 us -> none  [conv_valid(): lax.conv_general_dilated(source[None], kernel, (stride, stride, stride),...]
    ppermute x6 -> x7, waiting for transfers between devices: 12.1 us -> 38.6 us  [the longest x6 33.8 us: passed_along(): return lax.ppermute(array, axis, pairs_of(axis, by))]
    pallas_call x0 -> x2, Pallas kernels: none -> 24.5 us  [the longest x1 17 us: residual_base(): pl.pallas_call(functools.partial(residual_kernel, group), out_shape=jax.S...]
    ppermute x6 -> x7, starting transfers between devices: 17.7 us -> 29.4 us  [the longest x6 27.5 us: passed_along(): return lax.ppermute(array, axis, pairs_of(axis, by))]
    broadcast_in_dim x2 -> x0, other arithmetic: 6.19 us -> none  [conv_valid(): source[None]]
    slice x1 -> x6, local copies, waits for them, and re-layouts: 0.21 us -> 3.42 us  [the longest x3 0.99 us: body(): first = jnp.concatenate([low_y[:1], level[:1], high_y[:1]], axis=1)]
    add x1 -> x0, other arithmetic: 2.43 us -> none  [body(): level_input.reshape(cells, channels).astype(jnp.float32)]
    unnamed x13 -> x16, local copies, waits for them, and re-layouts: 2.33 us -> 3.2 us
  transfers between devices with their start and end apart: 7 -> 8, of which waited for: 4 -> 5; matrix products, arithmetic and copies ran while one was open for 37% -> 2% of each run, Pallas kernels for 7% -> 12%
where the time goes in v1:
time: 144 us; the launch traced here: 143 us
  Pallas kernels  61.1 us (42%)
  waiting for transfers between devices  38.6 us (27%)
  starting transfers between devices  35.4 us (25%)
  local copies, waits for them, and re-layouts  7.54 us (5%)
    ppermute x6, waiting for transfers between devices, passed_along(): return lax.ppermute(array, axis, pairs_of(axis, by))  33.8 us
    ppermute x6, starting transfers between devices, passed_along(): return lax.ppermute(array, axis, pairs_of(axis, by))  27.5 us
    pallas_call x1, Pallas kernels, add_rows(): pl.pallas_call(functools.partial(add_kernel, devices, cap, cells), out_sh...  27.4 us
    pallas_call x1, Pallas kernels, residual_base(): pl.pallas_call(functools.partial(residual_kernel, group), out_shape=jax.S...  17 us
    pallas_call x1, Pallas kernels, pack(): pl.pallas_call(functools.partial(pack_kernel, devices, cap), out_shape=ja...  9.15 us
    pallas_call x1, Pallas kernels, lower(): pl.pallas_call(lower_kernel, out_shape=jax.ShapeDtypeStruct((span_x // 2,...  7.5 us
    all_to_all x1, starting transfers between devices, body(): lax.all_to_all(outgoing.reshape(devices, capacity + EXTRA, channels), ('p...  6 us
    ppermute x1, waiting for transfers between devices, body(): corner = lax.ppermute(joined[-1:, -1:], ('pts', 'nbr'), diagonal)  4.8 us
  transfers between devices with their start and end apart: 8, of which 5 were waited for; matrix products, arithmetic and copies ran while one was open for 2% of the time, Pallas kernels for 12%

profile of v1, /device:TPU:12, one launch (start us, length us, event | category | flops | bytes accessed | tf_op | source)
XLA Modules:
  0.0 142.8 jit_solution(12720955406331648213)
XLA Ops:
  0.0 9.1 %pack.1 = bf16[8448,128]{1,0:T(8,128)(2,1)} custom-call(s32[32,128]{1,0:T(8,128)} %bitcast.17, s32[32,128]{1,0:T(8,128)} %bitcast.18, bf16[4096,128]{1,0:T(8,128)(2,1)} %bitcast.15), custom_call_target="tpu_custom_call" | custom-call | flops 100000000 | bytes 4000000 | tf_op jit(solution)/shard_map/pack/pallas_call | solution.py:67
  9.2 6.0 %all-to-all-start = ((bf16[32,264,128]{2,1,0:T(8,128)(2,1)}), bf16[32,264,128]{2,1,0:T(8,128)(2,1)S(1)}, u32[]{:S(2)}, u32[]{:S(2)}) async-start(bf16[32,264,128]{2,1,0:T(8,128)(2,1)} %bitcast.10), calls=%async_computation | async-start | bytes 4325376 | tf_op jit(solution)/shard_map/all_to_all | solution.py:325
  15.2 0.9 fusion.1
  16.1 3.4 %collective-permute-start.1 = (bf16[16,1,16,128]{3,2,1,0:T(8,128)(2,1)S(1)}, bf16[16,1,16,128]{3,2,1,0:T(8,128)(2,1)S(1)}, u32[]{:S(2)}, u32[]{:S(2)}) collective-permute-start(bf16[16,1,16,128]{3,2,1,0:T(8,128)(2,1)S(1)} %get-tuple-element.11), channel_id=1, source_target_pairs={{4,0},{8,4},{12,8},{16,12},{20,16},{24,20},{28,24},{5,1},{9,5},{13... | collective-permute-start | bytes 196616 | tf_op jit(solution)/shard_map/ppermute | solution.py:313
  19.4 2.5 %collective-permute-start = (bf16[16,1,16,128]{3,2,1,0:T(8,128)(2,1)S(1)}, bf16[16,1,16,128]{3,2,1,0:T(8,128)(2,1)S(1)}, u32[]{:S(2)}, u32[]{:S(2)}) collective-permute-start(bf16[16,1,16,128]{3,2,1,0:T(8,128)(2,1)S(1)} %get-tuple-element.12), channel_id=1, source_target_pairs={{0,4},{4,8},{8,12},{12,16},{16,20},{20,24},{24,28},{1,5},{5,9},{9,... | collective-permute-start | bytes 196616 | tf_op jit(solution)/shard_map/ppermute | solution.py:313
  21.9 1.0 fusion
  22.9 17.9 %collective-permute-done.1.yhigh_ref = bf16[16,1,16,128]{3,2,1,0:T(8,128)(2,1)S(1)} collective-permute-done((bf16[16,1,16,128]{3,2,1,0:T(8,128)(2,1)S(1)}, bf16[16,1,16,128]{3,2,1,0:T(8,128)(2,1)S(1)}, u32[]{:S(2)}, u32[]{:S(2)}) %collective-permute-start.1) | collective-permute-done | bytes 65568 | tf_op jit(solution)/shard_map/ppermute | solution.py:313
  40.8 13.2 %collective-permute-done.ylow_ref = bf16[16,1,16,128]{3,2,1,0:T(8,128)(2,1)S(1)} collective-permute-done((bf16[16,1,16,128]{3,2,1,0:T(8,128)(2,1)S(1)}, bf16[16,1,16,128]{3,2,1,0:T(8,128)(2,1)S(1)}, u32[]{:S(2)}, u32[]{:S(2)}) %collective-permute-start) | collective-permute-done | bytes 65568 | tf_op jit(solution)/shard_map/ppermute | solution.py:313
  54.0 1.9 %collective-permute-start.2 = (bf16[1,34,16,128]{3,2,1,0:T(8,128)(2,1)S(1)}, bf16[1,34,16,128]{3,2,1,0:T(8,128)(2,1)S(1)}, u32[]{:S(2)}, u32[]{:S(2)}) collective-permute-start(bf16[1,34,16,128]{3,2,1,0:T(8,128)(2,1)S(1)} %pad_maximum_fusion), channel_id=1, source_target_pairs={{0,1},{1,2},{2,3},{4,5},{5,6},{6,7},{8,9},{9,10},{10,11},{12,13},{... | collective-permute-start | bytes 417800 | tf_op jit(solution)/shard_map/ppermute | solution.py:313
  56.0 3.6 %collective-permute-start.3 = (bf16[1,34,16,128]{3,2,1,0:T(8,128)(2,1)S(1)}, bf16[1,34,16,128]{3,2,1,0:T(8,128)(2,1)S(1)}, u32[]{:S(2)}, u32[]{:S(2)}) collective-permute-start(bf16[1,34,16,128]{3,2,1,0:T(8,128)(2,1)S(1)} %pad_maximum_fusion.1), channel_id=1, source_target_pairs={{1,0},{2,1},{3,2},{5,4},{6,5},{7,6},{9,8},{10,9},{11,10},{13,12},{... | collective-permute-start | bytes 417800 | tf_op jit(solution)/shard_map/ppermute | solution.py:313
  59.6 2.6 %collective-permute-done.2.xlow_ref = bf16[1,34,16,128]{3,2,1,0:T(8,128)(2,1)S(1)} collective-permute-done((bf16[1,34,16,128]{3,2,1,0:T(8,128)(2,1)S(1)}, bf16[1,34,16,128]{3,2,1,0:T(8,128)(2,1)S(1)}, u32[]{:S(2)}, u32[]{:S(2)}) %collective-permute-start.2) | collective-permute-done | bytes 139296 | tf_op jit(solution)/shard_map/ppermute | solution.py:313
  62.2 0.1 collective-permute-done.3.xhigh_ref
  62.3 0.5 copy-done.3
  62.9 0.7 copy-done.4
  63.5 17.0 %residual.1 = f32[16,16,2,16,128]{4,3,2,1,0:T(8,128)} custom-call(bf16[16,32,16,128]{3,2,1,0:T(8,128)(2,1)} %level_ref, bf16[16,1,16,128]{3,2,1,0:T(8,128)(2,1)} %copy-done.2, bf16[16,1,16,128]{3,2,1,0:T(8,128)(2,1)} %copy-done.1, bf16[1,34,16,128]{3,2,1,0:T(8,128)(2,1)} %copy-done.3, bf16[1,34,16,128]{3,2,1,0:T(8,128)(2,1)} %copy-done.4, ...), custom_call_target="tpu_custom_call" | custom-call | flops 7247757312 | bytes 8000000 | tf_op jit(solution)/shard_map/residual/pallas_call | solution.py:223
  80.5 0.0 all-to-all-done
  80.5 1.4 copy-done
  81.9 27.4 %add_rows.1 = bf16[8192,128]{1,0:T(8,128)(2,1)} custom-call(bf16[8448,128]{1,0:T(8,128)(2,1)} %bitcast.9, f32[8192,128]{1,0:T(8,128)} %bitcast.11), custom_call_target="tpu_custom_call" | custom-call | flops 100000000 | bytes 8000000 | tf_op jit(solution)/shard_map/add_rows/pallas_call | solution.py:128
  109.3 0.9 slice.52
  110.3 1.9 %collective-permute-start.4 = (bf16[1,32,16,128]{3,2,1,0:T(8,128)(2,1)S(1)}, bf16[1,32,16,128]{3,2,1,0:T(8,128)(2,1)S(1)}, u32[]{:S(2)}, u32[]{:S(2)}) collective-permute-start(bf16[1,32,16,128]{3,2,1,0:T(8,128)(2,1)S(1)} %bitcast.16), channel_id=1, source_target_pairs={{0,1},{1,2},{2,3},{4,5},{5,6},{6,7},{8,9},{9,10},{10,11},{12,13},{... | collective-permute-start | bytes 393224 | tf_op jit(solution)/shard_map/ppermute | solution.py:313
  112.2 0.9 slice.53
  113.0 14.2 %collective-permute-start.5 = (bf16[16,1,16,128]{3,2,1,0:T(8,128)(2,1)S(1)}, bf16[16,1,16,128]{3,2,1,0:T(8,128)(2,1)S(1)}, u32[]{:S(2)}, u32[]{:S(2)}) collective-permute-start(bf16[16,1,16,128]{3,2,1,0:T(8,128)(2,1)S(1)} %slice.53), channel_id=1, source_target_pairs={{0,4},{4,8},{8,12},{12,16},{16,20},{20,24},{24,28},{1,5},{5,9},{9,... | collective-permute-start | bytes 196616 | tf_op jit(solution)/shard_map/ppermute | solution.py:313
  127.3 0.7 slice.54
  127.9 1.9 %collective-permute-start.6 = (bf16[1,1,16,128]{3,2,1,0:T(8,128)(2,1)S(1)}, bf16[1,1,16,128]{3,2,1,0:T(8,128)(2,1)S(1)}, u32[]{:S(2)}, u32[]{:S(2)}) collective-permute-start(bf16[1,1,16,128]{3,2,1,0:T(8,128)(2,1)S(1)} %slice.54), channel_id=1, source_target_pairs={{0,5},{1,6},{2,7},{4,9},{5,10},{6,11},{8,13},{9,14},{10,15},{12,17... | collective-permute-start | bytes 12296 | tf_op jit(solution)/shard_map/ppermute | solution.py:349
  129.9 4.8 %collective-permute-done.6.corner_ref = bf16[1,1,16,128]{3,2,1,0:T(8,128)(2,1)S(1)} collective-permute-done((bf16[1,1,16,128]{3,2,1,0:T(8,128)(2,1)S(1)}, bf16[1,1,16,128]{3,2,1,0:T(8,128)(2,1)S(1)}, u32[]{:S(2)}, u32[]{:S(2)}) %collective-permute-start.6) | collective-permute-done | bytes 4128 | tf_op jit(solution)/shard_map/ppermute | solution.py:349
  134.7 0.0 collective-permute-done.5.side_ref
  134.7 0.0 collective-permute-done.4.front_ref
  134.7 0.0 copy-start.5
  134.7 0.6 copy-done.7
  135.2 0.0 copy-done.6
  135.3 0.0 copy-done.5
  135.3 7.5 %lower.1 = bf16[8,16,8,256]{3,2,1,0:T(8,128)(2,1)} custom-call(bf16[16,32,16,128]{3,2,1,0:T(8,128)(2,1)} %bitcast.14, bf16[1,32,16,128]{3,2,1,0:T(8,128)(2,1)} %copy-done.5, bf16[16,1,16,128]{3,2,1,0:T(8,128)(2,1)} %copy-done.6, bf16[1,1,16,128]{3,2,1,0:T(8,128)(2,1)} %copy-done.7, bf16[3456,256]{1,0:T(8,128)(2,1)} %bitcast.19), custom_call_target="tpu_custom_call" | custom-call | flops 1811939328 | bytes 5000000 | tf_op jit(solution)/shard_map/lower/pallas_call | solution.py:292
  (13 shorter events, 0.1 us)
Async XLA Ops:
  9.2 71.4 %all-to-all-start = ((bf16[32,264,128]{2,1,0:T(8,128)(2,1)}), bf16[32,264,128]{2,1,0:T(8,128)(2,1)S(1)}, u32[]{:S(2)}, u32[]{:S(2)}) async-start(bf16[32,264,128]{2,1,0:T(8,128)(2,1)} %bitcast.10), calls=%async_computation | async-start | bytes 4325376 | tf_op jit(solution)/shard_map/all_to_all | solution.py:325
  16.1 24.7 %collective-permute-start.1 = (bf16[16,1,16,128]{3,2,1,0:T(8,128)(2,1)S(1)}, bf16[16,1,16,128]{3,2,1,0:T(8,128)(2,1)S(1)}, u32[]{:S(2)}, u32[]{:S(2)}) collective-permute-start(bf16[16,1,16,128]{3,2,1,0:T(8,128)(2,1)S(1)} %get-tuple-element.11), channel_id=1, source_target_pairs={{4,0},{8,4},{12,8},{16,12},{20,16},{24,20},{28,24},{5,1},{9,5},{13... | collective-permute-start | bytes 196616 | tf_op jit(solution)/shard_map/ppermute | solution.py:313
  19.4 34.6 %collective-permute-start = (bf16[16,1,16,128]{3,2,1,0:T(8,128)(2,1)S(1)}, bf16[16,1,16,128]{3,2,1,0:T(8,128)(2,1)S(1)}, u32[]{:S(2)}, u32[]{:S(2)}) collective-permute-start(bf16[16,1,16,128]{3,2,1,0:T(8,128)(2,1)S(1)} %get-tuple-element.12), channel_id=1, source_target_pairs={{0,4},{4,8},{8,12},{12,16},{16,20},{20,24},{24,28},{1,5},{5,9},{9,... | collective-permute-start | bytes 196616 | tf_op jit(solution)/shard_map/ppermute | solution.py:313
  40.8 21.6 %copy-start.1 = (bf16[16,1,16,128]{3,2,1,0:T(8,128)(2,1)}, bf16[16,1,16,128]{3,2,1,0:T(8,128)(2,1)S(1)}, u32[]{:S(2)}) copy-start(bf16[16,1,16,128]{3,2,1,0:T(8,128)(2,1)S(1)} %collective-permute-done.1.yhigh_ref) | copy-start | bytes 196612
  54.0 8.4 %copy-start.2 = (bf16[16,1,16,128]{3,2,1,0:T(8,128)(2,1)}, bf16[16,1,16,128]{3,2,1,0:T(8,128)(2,1)S(1)}, u32[]{:S(2)}) copy-start(bf16[16,1,16,128]{3,2,1,0:T(8,128)(2,1)S(1)} %collective-permute-done.ylow_ref) | copy-start | bytes 196612
  54.0 8.2 %collective-permute-start.2 = (bf16[1,34,16,128]{3,2,1,0:T(8,128)(2,1)S(1)}, bf16[1,34,16,128]{3,2,1,0:T(8,128)(2,1)S(1)}, u32[]{:S(2)}, u32[]{:S(2)}) collective-permute-start(bf16[1,34,16,128]{3,2,1,0:T(8,128)(2,1)S(1)} %pad_maximum_fusion), channel_id=1, source_target_pairs={{0,1},{1,2},{2,3},{4,5},{5,6},{6,7},{8,9},{9,10},{10,11},{12,13},{... | collective-permute-start | bytes 417800 | tf_op jit(solution)/shard_map/ppermute | solution.py:313
  56.0 6.4 %collective-permute-start.3 = (bf16[1,34,16,128]{3,2,1,0:T(8,128)(2,1)S(1)}, bf16[1,34,16,128]{3,2,1,0:T(8,128)(2,1)S(1)}, u32[]{:S(2)}, u32[]{:S(2)}) collective-permute-start(bf16[1,34,16,128]{3,2,1,0:T(8,128)(2,1)S(1)} %pad_maximum_fusion.1), channel_id=1, source_target_pairs={{1,0},{2,1},{3,2},{5,4},{6,5},{7,6},{9,8},{10,9},{11,10},{13,12},{... | collective-permute-start | bytes 417800 | tf_op jit(solution)/shard_map/ppermute | solution.py:313
  62.2 0.7 copy-start.3
  62.9 0.7 copy-start.4
  80.5 1.4 copy-start
  110.3 24.4 %collective-permute-start.4 = (bf16[1,32,16,128]{3,2,1,0:T(8,128)(2,1)S(1)}, bf16[1,32,16,128]{3,2,1,0:T(8,128)(2,1)S(1)}, u32[]{:S(2)}, u32[]{:S(2)}) collective-permute-start(bf16[1,32,16,128]{3,2,1,0:T(8,128)(2,1)S(1)} %bitcast.16), channel_id=1, source_target_pairs={{0,1},{1,2},{2,3},{4,5},{5,6},{6,7},{8,9},{9,10},{10,11},{12,13},{... | collective-permute-start | bytes 393224 | tf_op jit(solution)/shard_map/ppermute | solution.py:313
  113.0 21.6 %collective-permute-start.5 = (bf16[16,1,16,128]{3,2,1,0:T(8,128)(2,1)S(1)}, bf16[16,1,16,128]{3,2,1,0:T(8,128)(2,1)S(1)}, u32[]{:S(2)}, u32[]{:S(2)}) collective-permute-start(bf16[16,1,16,128]{3,2,1,0:T(8,128)(2,1)S(1)} %slice.53), channel_id=1, source_target_pairs={{0,4},{4,8},{8,12},{12,16},{16,20},{20,24},{24,28},{1,5},{5,9},{9,... | collective-permute-start | bytes 196616 | tf_op jit(solution)/shard_map/ppermute | solution.py:313
  127.9 6.7 %collective-permute-start.6 = (bf16[1,1,16,128]{3,2,1,0:T(8,128)(2,1)S(1)}, bf16[1,1,16,128]{3,2,1,0:T(8,128)(2,1)S(1)}, u32[]{:S(2)}, u32[]{:S(2)}) collective-permute-start(bf16[1,1,16,128]{3,2,1,0:T(8,128)(2,1)S(1)} %slice.54), channel_id=1, source_target_pairs={{0,5},{1,6},{2,7},{4,9},{5,10},{6,11},{8,13},{9,14},{10,15},{12,17... | collective-permute-start | bytes 12296 | tf_op jit(solution)/shard_map/ppermute | solution.py:349
  134.7 0.6 copy-start.7
  134.7 0.6 copy-start.6
  134.7 0.7 copy-start.5

commit v2 on v1

--- a/solution.py
+++ b/solution.py
@@ -6,13 +6,14 @@
 from jax.experimental.pallas import tpu as pltpu
 from jax.sharding import PartitionSpec as P
 
+
 LANES = 128
 EXTRA = 8
 
 
 def pack_kernel(devices, cap, owner_ref, cell_ref, rows_ref, out_ref,
                 wide, spread, slot_vmem, slot_smem, sem):
-    p_local, channels = rows_ref.shape
+    p_local, _ = rows_ref.shape
     blocks = p_local // LANES
     stride = cap + EXTRA
     upper = (lax.broadcasted_iota(jnp.int32, (LANES, LANES), 0)
@@ -81,62 +82,100 @@
     )(owner.reshape(blocks, LANES), cell.reshape(blocks, LANES), rows)
 
 
-WAYS = 4
-
-
-def add_kernel(devices, cap, cells, got_ref, base_hbm, out_ref, wide, slot_vmem, slot_smem,
-               sem, sem2, *sums):
-    channels = got_ref.shape[-1]
-    stride = cap + EXTRA
-    per = -(-cap // LANES)
-    first = pltpu.make_async_copy(base_hbm, sums[0].at[pl.ds(0, cells)], sem2)
+WAYS = 6
+PIECES = 4
+LIMIT = 48 * 2**20
+
+
+def add_kernel(capacity, got_hbm, base_hbm, out_ref, front_ref, side_ref, corner_ref,
+               landed, wide, slot_vmem, slot_smem, sems, *sums):
+    span_x, span_y, span_z, channels = out_ref.shape
+    cells = span_x * span_y * span_z
+    total, _ = landed.shape
+    stride = capacity + EXTRA
+    devices = total // stride
+    per = -(-capacity // LANES)
+    width = min(LANES, capacity)
+    piece = total // PIECES
+    copies = [
+        pltpu.make_async_copy(got_hbm.at[pl.ds(i * piece, piece)],
+                              landed.at[pl.ds(i * piece, piece)], sems.at[i])
+        for i in range(PIECES)
+    ]
+    for copy in copies:
+        copy.start()
+    first = pltpu.make_async_copy(base_hbm, sums[0].at[pl.ds(0, cells)], sems.at[PIECES])
     first.start()
-    wide[...] = got_ref[...].astype(jnp.float32)
+    half = len(sums) // 2
+    for s in sums[1:half]:
+        s[...] = jnp.zeros_like(s)
+    for i, copy in enumerate(copies):
+        copy.wait()
+        wide[i * piece:(i + 1) * piece, :] = landed[i * piece:(i + 1) * piece, :].astype(
+            jnp.float32)
     for j in range(per):
-        width = min(LANES, cap - j * LANES)
-        high = wide[pl.ds(cap + j, devices, stride=stride), :].astype(jnp.int32)
-        low = wide[pl.ds(cap + per + j, devices, stride=stride), :].astype(jnp.int32)
-        spot = jnp.where(high > 0, (high - 1) * LANES + low, cells)
-        slot_vmem[:, j * LANES:j * LANES + width] = spot[:, :width]
-    copy = pltpu.make_async_copy(slot_vmem, slot_smem, sem)
+        high = wide[pl.ds(capacity + j, devices, stride=stride), :].astype(jnp.int32)
+        low = wide[pl.ds(capacity + per + j, devices, stride=stride), :].astype(jnp.int32)
+        slot_vmem[j * devices:(j + 1) * devices, :] = jnp.where(
+            high > 0, (high - 1) * LANES + low, cells)
+    copy = pltpu.make_async_copy(slot_vmem, slot_smem, sems.at[PIECES + 1])
     copy.start()
-    for s in sums[1:]:
+    for s in sums[max(half, 1):]:
         s[...] = jnp.zeros_like(s)
     copy.wait()
     first.wait()
-
-    def step(o, carry):
-        def inner(q, carry):
-            for u in range(32):
-                at = slot_smem[o, q * 32 + u]
+    for j in range(per):
+        def step(o, carry):
+            start = pl.multiple_of(o * stride + j * LANES, 8)
+            for u in range(width):
+                at = slot_smem[j * devices + o, u]
                 s = sums[u % len(sums)]
-                s[pl.ds(at, 1), :] += wide[pl.ds(o * stride + q * 32 + u, 1), :]
+                s[pl.ds(at, 1), :] += wide[pl.ds(start + u, 1), :]
             return carry
-        return lax.fori_loop(0, cap // 32, inner, carry)
-
-    lax.fori_loop(0, devices, step, 0)
-    total = sums[0][pl.ds(0, cells), :]
-    for s in sums[1:]:
-        total = total + s[pl.ds(0, cells), :]
-    out_ref[...] = total.astype(jnp.bfloat16)
-
-
-def add_rows(got, base, devices, cap):
-    cells, channels = base.shape
+
+        lax.fori_loop(0, devices, step, 0)
+
+    def finish(x, carry):
+        at = pl.ds(pl.multiple_of(x * (span_y * span_z), 8), span_y * span_z)
+        value = sums[0][at, :]
+        for s in sums[1:]:
+            value = value + s[at, :]
+        value = value.astype(jnp.bfloat16).reshape(span_y, span_z, channels)
+        out_ref[x] = value
+        side_ref[x] = value[span_y - 1:]
+        return carry
+
+    lax.fori_loop(0, span_x, finish, 0)
+    front_ref[...] = out_ref[span_x - 1:]
+    corner_ref[...] = out_ref[span_x - 1:, span_y - 1:]
+
+
+def add_rows(got, base, shape, capacity):
+    span_x, span_y, span_z, channels = shape
+    cells = span_x * span_y * span_z
+    total = got.shape[0]
+    devices = total // (capacity + EXTRA)
+    per = -(-capacity // LANES)
     vm = pl.BlockSpec(memory_space=pltpu.VMEM)
-    total = devices * (cap + EXTRA)
+    hbm = pl.BlockSpec(memory_space=pl.ANY)
     return pl.pallas_call(
-        functools.partial(add_kernel, devices, cap, cells),
-        out_shape=jax.ShapeDtypeStruct((cells, channels), jnp.bfloat16),
-        in_specs=[vm, pl.BlockSpec(memory_space=pl.ANY)],
-        out_specs=vm,
+        functools.partial(add_kernel, capacity),
+        out_shape=[
+            jax.ShapeDtypeStruct(shape, jnp.bfloat16),
+            jax.ShapeDtypeStruct((1, span_y, span_z, channels), jnp.bfloat16),
+            jax.ShapeDtypeStruct((span_x, 1, span_z, channels), jnp.bfloat16),
+            jax.ShapeDtypeStruct((1, 1, span_z, channels), jnp.bfloat16),
+        ],
+        in_specs=[hbm, hbm],
+        out_specs=[vm] * 4,
         scratch_shapes=[
+            pltpu.VMEM((total, channels), jnp.bfloat16),
             pltpu.VMEM((total, channels), jnp.float32),
-            pltpu.VMEM((devices, cap), jnp.int32),
-            pltpu.SMEM((devices, cap), jnp.int32),
-            pltpu.SemaphoreType.DMA,
-            pltpu.SemaphoreType.DMA,
+            pltpu.VMEM((devices * per, LANES), jnp.int32),
+            pltpu.SMEM((devices * per, LANES), jnp.int32),
+            pltpu.SemaphoreType.DMA((PIECES + 2,)),
         ] + [pltpu.VMEM((cells + 8, channels), jnp.float32)] * WAYS,
+        compiler_params=pltpu.CompilerParams(vmem_limit_bytes=LIMIT),
         name="add_rows",
         cost_estimate=pl.CostEstimate(flops=10**8, bytes_accessed=8 * 10**6, transcendentals=0),
     )(got, base)
@@ -231,6 +270,7 @@
             pltpu.VMEM((36 * channels, 2 * channels), jnp.bfloat16),
             pltpu.VMEM((group * lines, 2 * channels), jnp.float32),
         ],
+        compiler_params=pltpu.CompilerParams(vmem_limit_bytes=36 * 2**20),
         name="residual",
         cost_estimate=pl.CostEstimate(flops=flops, bytes_accessed=8 * 10**6, transcendentals=0),
     )(level, ylow, yhigh, xlow, xhigh, w_res)
@@ -299,6 +339,7 @@
             pltpu.VMEM(((span_y + 1) * span_z + 16, channels), jnp.float32),
             pltpu.VMEM((span_x + 1, span_y * span_z // 4, 9 * channels), jnp.bfloat16),
         ],
+        compiler_params=pltpu.CompilerParams(vmem_limit_bytes=28 * 2**20),
         name="lower",
         cost_estimate=pl.CostEstimate(flops=flops, bytes_accessed=5 * 10**6, transcendentals=0),
     )(joined, front, side, corner, w_down.reshape(-1, wide))
@@ -320,8 +361,15 @@
     channels = points.shape[-1]
     rows = points.reshape(-1, channels)
     capacity = 2 * rows.shape[0] // devices
+    level = level_input
+    low_y = passed_along(level[:, -1:], "pts", 1)
+    high_y = passed_along(level[:, :1], "pts", -1)
     outgoing = pack(dest_owner.reshape(-1), dest_cell.reshape(-1), rows, devices, capacity)
-    outgoing, level = lax.optimization_barrier((outgoing, level_input))
+    last = jnp.concatenate([low_y[-1:], level[-1:], high_y[-1:]], axis=1)
+    first = jnp.concatenate([low_y[:1], level[:1], high_y[:1]], axis=1)
+    outgoing, last, first = lax.optimization_barrier((outgoing, last, first))
+    low_x = passed_along(last, "nbr", 1)
+    high_x = passed_along(first, "nbr", -1)
     got = lax.all_to_all(
         outgoing.reshape(devices, capacity + EXTRA, channels),
         ("pts", "nbr"),
@@ -329,24 +377,16 @@
         concat_axis=0,
         tiled=True,
     ).reshape(outgoing.shape)
-    span_x, span_y, span_z = level_input.shape[:3]
-    low_y = passed_along(level[:, -1:], "pts", 1)
-    high_y = passed_along(level[:, :1], "pts", -1)
-    last = jnp.concatenate([low_y[-1:], level[-1:], high_y[-1:]], axis=1)
-    first = jnp.concatenate([low_y[:1], level[:1], high_y[:1]], axis=1)
-    low_x = passed_along(last, "nbr", 1)
-    high_x = passed_along(first, "nbr", -1)
     base = residual_base(level, low_y, high_y, low_x, high_x, w_res)
-    joined = add_rows(got, base, devices, capacity)
-    joined = joined.reshape(span_x, span_y, span_z, channels)
-    front = passed_along(joined[-1:], "nbr", 1)
-    side = passed_along(joined[:, -1:], "pts", 1)
+    joined, front, side, corner = add_rows(got, base, level.shape, capacity)
     diagonal = [
         (i * count_nbr + j, (i + 1) * count_nbr + j + 1)
         for i in range(count_pts - 1)
         for j in range(count_nbr - 1)
     ]
-    corner = lax.ppermute(joined[-1:, -1:], ("pts", "nbr"), diagonal)
+    front = passed_along(front, "nbr", 1)
+    side = passed_along(side, "pts", 1)
+    corner = lax.ppermute(corner, ("pts", "nbr"), diagonal)
     return lower(joined, front, side, corner, w_down)
 
 

time: 144 us -> 103 us (0.72)
  Pallas kernels: 61.1 us -> 40.5 us
  starting transfers between devices: 35.4 us -> 24.7 us
  waiting for transfers between devices: 38.6 us -> 30.4 us
  local copies, waits for them, and re-layouts: 7.54 us -> 5.43 us
    ppermute x6, waiting for transfers between devices: 33.8 us -> 8.6 us  [passed_along(): return lax.ppermute(array, axis, pairs_of(axis, by))]
    all_to_all x1, waiting for transfers between devices: 0.01 us -> 17 us  [body(): lax.all_to_all(outgoing.reshape(devices, capacity + EXTRA, channels), ('p...]
    pallas_call x1, Pallas kernels: 27.4 us -> 13 us  [add_rows(): pl.pallas_call(functools.partial(add_kernel, capacity), out_shape=[jax.Sh...]
    ppermute x6, starting transfers between devices: 27.5 us -> 17.7 us  [passed_along(): return lax.ppermute(array, axis, pairs_of(axis, by))]
    pallas_call x1, Pallas kernels: 17 us -> 13 us  [residual_base(): pl.pallas_call(functools.partial(residual_kernel, group), out_shape=jax.S...]
    slice x4 -> x1, local copies, waits for them, and re-layouts: 3.34 us -> 0.88 us  [body(): low_y = passed_along(level[:, -1:], 'pts', 1)]
    pallas_call x1, Pallas kernels: 7.5 us -> 5.29 us  [lower(): pl.pallas_call(lower_kernel, out_shape=jax.ShapeDtypeStruct((span_x // 2,...]
    unnamed x16 -> x8, local copies, waits for them, and re-layouts: 3.2 us -> 3.55 us
  transfers between devices with their start and end apart: 8 -> 8, of which waited for: 5 -> 3; matrix products, arithmetic and copies ran while one was open for 2% -> 1% of each run, Pallas kernels for 12% -> 22%
where the time goes in v2:
time: 103 us; the launch traced here: 101 us
  Pallas kernels  40.5 us (39%)
  waiting for transfers between devices  30.4 us (30%)
  starting transfers between devices  24.7 us (24%)
  local copies, waits for them, and re-layouts  5.43 us (5%)
    ppermute x6, starting transfers between devices, passed_along(): return lax.ppermute(array, axis, pairs_of(axis, by))  17.7 us
    all_to_all x1, waiting for transfers between devices, body(): lax.all_to_all(outgoing.reshape(devices, capacity + EXTRA, channels), ('p...  17 us
    pallas_call x1, Pallas kernels, residual_base(): pl.pallas_call(functools.partial(residual_kernel, group), out_shape=jax.S...  13 us
    pallas_call x1, Pallas kernels, add_rows(): pl.pallas_call(functools.partial(add_kernel, capacity), out_shape=[jax.Sh...  13 us
    pallas_call x1, Pallas kernels, pack(): pl.pallas_call(functools.partial(pack_kernel, devices, cap), out_shape=ja...  9.16 us
    ppermute x6, waiting for transfers between devices, passed_along(): return lax.ppermute(array, axis, pairs_of(axis, by))  8.6 us
    pallas_call x1, Pallas kernels, lower(): pl.pallas_call(lower_kernel, out_shape=jax.ShapeDtypeStruct((span_x // 2,...  5.29 us
    all_to_all x1, starting transfers between devices, body(): lax.all_to_all(outgoing.reshape(devices, capacity + EXTRA, channels), ('p...  5.1 us
  transfers between devices with their start and end apart: 8, of which 3 were waited for; matrix products, arithmetic and copies ran while one was open for 1% of the time, Pallas kernels for 22%

profile of v2, /device:TPU:12, one launch (start us, length us, event | category | flops | bytes accessed | tf_op | source)
XLA Modules:
  0.0 101.2 jit_solution(10418129460812415187)
XLA Ops:
  0.0 0.9 fusion.1
  0.9 3.4 %collective-permute-start = (bf16[16,1,16,128]{3,2,1,0:T(8,128)(2,1)S(1)}, bf16[16,1,16,128]{3,2,1,0:T(8,128)(2,1)S(1)}, u32[]{:S(2)}, u32[]{:S(2)}) collective-permute-start(bf16[16,1,16,128]{3,2,1,0:T(8,128)(2,1)S(1)} %get-tuple-element.21), channel_id=1, source_target_pairs={{0,4},{4,8},{8,12},{12,16},{16,20},{20,24},{24,28},{1,5},{5,9},{9,... | collective-permute-start | bytes 196616 | tf_op jit(solution)/shard_map/ppermute | solution.py:354
  4.3 3.3 %collective-permute-start.1 = (bf16[16,1,16,128]{3,2,1,0:T(8,128)(2,1)S(1)}, bf16[16,1,16,128]{3,2,1,0:T(8,128)(2,1)S(1)}, u32[]{:S(2)}, u32[]{:S(2)}) collective-permute-start(bf16[16,1,16,128]{3,2,1,0:T(8,128)(2,1)S(1)} %get-tuple-element.22), channel_id=1, source_target_pairs={{4,0},{8,4},{12,8},{16,12},{20,16},{24,20},{28,24},{5,1},{9,5},{13... | collective-permute-start | bytes 196616 | tf_op jit(solution)/shard_map/ppermute | solution.py:354
  7.6 1.0 fusion
  8.6 9.2 %pack.1 = bf16[8448,128]{1,0:T(8,128)(2,1)} custom-call(s32[32,128]{1,0:T(8,128)} %bitcast.12, s32[32,128]{1,0:T(8,128)} %bitcast.13, bf16[4096,128]{1,0:T(8,128)(2,1)} %bitcast.11), custom_call_target="tpu_custom_call" | custom-call | flops 100000000 | bytes 4000000 | tf_op jit(solution)/shard_map/pack/pallas_call | solution.py:68
  17.8 0.0 collective-permute-done.ylow_ref
  17.8 0.0 collective-permute-done.1.yhigh_ref
  17.9 0.0 copy-start.3
  17.9 5.1 %all-to-all-start = ((bf16[32,264,128]{2,1,0:T(8,128)(2,1)}), bf16[32,264,128]{2,1,0:T(8,128)(2,1)S(1)}, u32[]{:S(2)}, u32[]{:S(2)}) async-start(bf16[32,264,128]{2,1,0:T(8,128)(2,1)} %bitcast.10), calls=%async_computation | async-start | bytes 4325376 | tf_op jit(solution)/shard_map/all_to_all | solution.py:373
  23.0 2.0 %collective-permute-start.2 = (bf16[1,34,16,128]{3,2,1,0:T(8,128)(2,1)S(1)}, bf16[1,34,16,128]{3,2,1,0:T(8,128)(2,1)S(1)}, u32[]{:S(2)}, u32[]{:S(2)}) collective-permute-start(bf16[1,34,16,128]{3,2,1,0:T(8,128)(2,1)S(1)} %get-tuple-element.13), channel_id=1, source_target_pairs={{0,1},{1,2},{2,3},{4,5},{5,6},{6,7},{8,9},{9,10},{10,11},{12,13},{... | collective-permute-start | bytes 417800 | tf_op jit(solution)/shard_map/ppermute | solution.py:354
  25.0 3.5 %collective-permute-start.3 = (bf16[1,34,16,128]{3,2,1,0:T(8,128)(2,1)S(1)}, bf16[1,34,16,128]{3,2,1,0:T(8,128)(2,1)S(1)}, u32[]{:S(2)}, u32[]{:S(2)}) collective-permute-start(bf16[1,34,16,128]{3,2,1,0:T(8,128)(2,1)S(1)} %get-tuple-element.14), channel_id=1, source_target_pairs={{1,0},{2,1},{3,2},{5,4},{6,5},{7,6},{9,8},{10,9},{11,10},{13,12},{... | collective-permute-start | bytes 417800 | tf_op jit(solution)/shard_map/ppermute | solution.py:354
  28.6 8.6 %collective-permute-done.2.xlow_ref = bf16[1,34,16,128]{3,2,1,0:T(8,128)(2,1)S(1)} collective-permute-done((bf16[1,34,16,128]{3,2,1,0:T(8,128)(2,1)S(1)}, bf16[1,34,16,128]{3,2,1,0:T(8,128)(2,1)S(1)}, u32[]{:S(2)}, u32[]{:S(2)}) %collective-permute-start.2) | collective-permute-done | bytes 139296 | tf_op jit(solution)/shard_map/ppermute | solution.py:354
  37.2 0.0 collective-permute-done.3.xhigh_ref
  37.2 0.0 copy-done.3
  37.2 0.0 copy-start.1
  37.2 1.6 %copy-done.1 = bf16[16,32,16,128]{3,2,1,0:T(8,128)(2,1)S(1)} copy-done((bf16[16,32,16,128]{3,2,1,0:T(8,128)(2,1)S(1)}, bf16[16,32,16,128]{3,2,1,0:T(8,128)(2,1)}, u32[]{:S(2)}) %copy-start.1) | copy-done | bytes 2097176
  38.8 13.0 %residual.1 = f32[16,16,2,16,128]{4,3,2,1,0:T(8,128)S(1)} custom-call(bf16[16,32,16,128]{3,2,1,0:T(8,128)(2,1)S(1)} %copy-done.1, bf16[16,1,16,128]{3,2,1,0:T(8,128)(2,1)S(1)} %collective-permute-done.ylow_ref, bf16[16,1,16,128]{3,2,1,0:T(8,128)(2,1)S(1)} %collective-permute-done.1.yhigh_ref, bf16[1,34,16,128]{3,2,1,0:T(8,128)(2,1)S(1)} %collective-permute-done.2.xlow_ref, ...), custom_call_target="tpu_custom_call" | custom-call | flops 7247757312 | bytes 8000000 | tf_op jit(solution)/shard_map/residual/pallas_call | solution.py:262
  51.8 0.0 copy-start
  51.8 1.9 %copy-done = f32[16,16,2,16,128]{4,3,2,1,0:T(8,128)} copy-done((f32[16,16,2,16,128]{4,3,2,1,0:T(8,128)}, f32[16,16,2,16,128]{4,3,2,1,0:T(8,128)S(1)}, u32[]{:S(2)}) %copy-start) | copy-done | bytes 4194328
  53.8 17.0 %all-to-all-done = bf16[32,264,128]{2,1,0:T(8,128)(2,1)S(1)} async-done(((bf16[32,264,128]{2,1,0:T(8,128)(2,1)}), bf16[32,264,128]{2,1,0:T(8,128)(2,1)S(1)}, u32[]{:S(2)}, u32[]{:S(2)}) %all-to-all-start) | async-done | bytes 2162720 | tf_op jit(solution)/shard_map/all_to_all | solution.py:373
  70.8 0.0 copy-start.2
  70.8 13.0 %add_rows.1 = (bf16[16,32,16,128]{3,2,1,0:T(8,128)(2,1)S(1)}, bf16[1,32,16,128]{3,2,1,0:T(8,128)(2,1)S(1)}, bf16[16,1,16,128]{3,2,1,0:T(8,128)(2,1)S(1)}, bf16[1,1,16,128]{3,2,1,0:T(8,128)(2,1)S(1)}) custom-call(bf16[8448,128]{1,0:T(8,128)(2,1)S(1)} %bitcast.7, f32[8192,128]{1,0:T(8,128)} %bitcast.8), custom_call_target="tpu_custom_call" | custom-call | flops 100000000 | bytes 8000000 | tf_op jit(solution)/shard_map/add_rows/pallas_call | solution.py:161
  83.8 2.9 %collective-permute-start.4 = (bf16[1,32,16,128]{3,2,1,0:T(8,128)(2,1)S(1)}, bf16[1,32,16,128]{3,2,1,0:T(8,128)(2,1)S(1)}, u32[]{:S(2)}, u32[]{:S(2)}) collective-permute-start(bf16[1,32,16,128]{3,2,1,0:T(8,128)(2,1)S(1)} %get-tuple-element.16), channel_id=1, source_target_pairs={{0,1},{1,2},{2,3},{4,5},{5,6},{6,7},{8,9},{9,10},{10,11},{12,13},{... | collective-permute-start | bytes 393224 | tf_op jit(solution)/shard_map/ppermute | solution.py:354
  86.7 2.4 %collective-permute-start.5 = (bf16[16,1,16,128]{3,2,1,0:T(8,128)(2,1)S(1)}, bf16[16,1,16,128]{3,2,1,0:T(8,128)(2,1)S(1)}, u32[]{:S(2)}, u32[]{:S(2)}) collective-permute-start(bf16[16,1,16,128]{3,2,1,0:T(8,128)(2,1)S(1)} %get-tuple-element.17), channel_id=1, source_target_pairs={{0,4},{4,8},{8,12},{12,16},{16,20},{20,24},{24,28},{1,5},{5,9},{9,... | collective-permute-start | bytes 196616 | tf_op jit(solution)/shard_map/ppermute | solution.py:354
  89.2 1.9 %collective-permute-start.6 = (bf16[1,1,16,128]{3,2,1,0:T(8,128)(2,1)S(1)}, bf16[1,1,16,128]{3,2,1,0:T(8,128)(2,1)S(1)}, u32[]{:S(2)}, u32[]{:S(2)}) collective-permute-start(bf16[1,1,16,128]{3,2,1,0:T(8,128)(2,1)S(1)} %get-tuple-element.18), channel_id=1, source_target_pairs={{0,5},{1,6},{2,7},{4,9},{5,10},{6,11},{8,13},{9,14},{10,15},{12,17... | collective-permute-start | bytes 12296 | tf_op jit(solution)/shard_map/ppermute | solution.py:389
  91.1 4.8 %collective-permute-done.6.corner_ref = bf16[1,1,16,128]{3,2,1,0:T(8,128)(2,1)S(1)} collective-permute-done((bf16[1,1,16,128]{3,2,1,0:T(8,128)(2,1)S(1)}, bf16[1,1,16,128]{3,2,1,0:T(8,128)(2,1)S(1)}, u32[]{:S(2)}, u32[]{:S(2)}) %collective-permute-start.6) | collective-permute-done | bytes 4128 | tf_op jit(solution)/shard_map/ppermute | solution.py:389
  95.9 0.0 collective-permute-done.5.side_ref
  95.9 0.0 collective-permute-done.4.front_ref
  95.9 0.0 copy-done.2
  95.9 5.3 %lower.1 = bf16[8,16,8,256]{3,2,1,0:T(8,128)(2,1)} custom-call(bf16[16,32,16,128]{3,2,1,0:T(8,128)(2,1)S(1)} %get-tuple-element.15.joined_ref, bf16[1,32,16,128]{3,2,1,0:T(8,128)(2,1)S(1)} %collective-permute-done.4.front_ref, bf16[16,1,16,128]{3,2,1,0:T(8,128)(2,1)S(1)} %collective-permute-done.5.side_ref, ...), custom_call_target="tpu_custom_call" | custom-call | flops 1811939328 | bytes 5000000 | tf_op jit(solution)/shard_map/lower/pallas_call | solution.py:332
  (3 shorter events, 0.0 us)
Async XLA Ops:
  0.9 16.9 %collective-permute-start = (bf16[16,1,16,128]{3,2,1,0:T(8,128)(2,1)S(1)}, bf16[16,1,16,128]{3,2,1,0:T(8,128)(2,1)S(1)}, u32[]{:S(2)}, u32[]{:S(2)}) collective-permute-start(bf16[16,1,16,128]{3,2,1,0:T(8,128)(2,1)S(1)} %get-tuple-element.21), channel_id=1, source_target_pairs={{0,4},{4,8},{8,12},{12,16},{16,20},{20,24},{24,28},{1,5},{5,9},{9,... | collective-permute-start | bytes 196616 | tf_op jit(solution)/shard_map/ppermute | solution.py:354
  4.3 13.5 %collective-permute-start.1 = (bf16[16,1,16,128]{3,2,1,0:T(8,128)(2,1)S(1)}, bf16[16,1,16,128]{3,2,1,0:T(8,128)(2,1)S(1)}, u32[]{:S(2)}, u32[]{:S(2)}) collective-permute-start(bf16[16,1,16,128]{3,2,1,0:T(8,128)(2,1)S(1)} %get-tuple-element.22), channel_id=1, source_target_pairs={{4,0},{8,4},{12,8},{16,12},{20,16},{24,20},{28,24},{5,1},{9,5},{13... | collective-permute-start | bytes 196616 | tf_op jit(solution)/shard_map/ppermute | solution.py:354
  17.9 19.3 %copy-start.3 = (bf16[27,128,128]{2,1,0:T(8,128)(2,1)S(1)}, bf16[27,128,128]{2,1,0:T(8,128)(2,1)}, u32[]{:S(2)}) copy-start(bf16[27,128,128]{2,1,0:T(8,128)(2,1)} %w_ref.1) | copy-start | bytes 2654212
  17.9 52.9 %all-to-all-start = ((bf16[32,264,128]{2,1,0:T(8,128)(2,1)}), bf16[32,264,128]{2,1,0:T(8,128)(2,1)S(1)}, u32[]{:S(2)}, u32[]{:S(2)}) async-start(bf16[32,264,128]{2,1,0:T(8,128)(2,1)} %bitcast.10), calls=%async_computation | async-start | bytes 4325376 | tf_op jit(solution)/shard_map/all_to_all | solution.py:373
  23.0 14.2 %collective-permute-start.2 = (bf16[1,34,16,128]{3,2,1,0:T(8,128)(2,1)S(1)}, bf16[1,34,16,128]{3,2,1,0:T(8,128)(2,1)S(1)}, u32[]{:S(2)}, u32[]{:S(2)}) collective-permute-start(bf16[1,34,16,128]{3,2,1,0:T(8,128)(2,1)S(1)} %get-tuple-element.13), channel_id=1, source_target_pairs={{0,1},{1,2},{2,3},{4,5},{5,6},{6,7},{8,9},{9,10},{10,11},{12,13},{... | collective-permute-start | bytes 417800 | tf_op jit(solution)/shard_map/ppermute | solution.py:354
  25.0 12.1 %collective-permute-start.3 = (bf16[1,34,16,128]{3,2,1,0:T(8,128)(2,1)S(1)}, bf16[1,34,16,128]{3,2,1,0:T(8,128)(2,1)S(1)}, u32[]{:S(2)}, u32[]{:S(2)}) collective-permute-start(bf16[1,34,16,128]{3,2,1,0:T(8,128)(2,1)S(1)} %get-tuple-element.14), channel_id=1, source_target_pairs={{1,0},{2,1},{3,2},{5,4},{6,5},{7,6},{9,8},{10,9},{11,10},{13,12},{... | collective-permute-start | bytes 417800 | tf_op jit(solution)/shard_map/ppermute | solution.py:354
  37.2 1.6 %copy-start.1 = (bf16[16,32,16,128]{3,2,1,0:T(8,128)(2,1)S(1)}, bf16[16,32,16,128]{3,2,1,0:T(8,128)(2,1)}, u32[]{:S(2)}) copy-start(bf16[16,32,16,128]{3,2,1,0:T(8,128)(2,1)} %level_ref.1) | copy-start | bytes 6291460
  51.8 2.0 %copy-start = (f32[16,16,2,16,128]{4,3,2,1,0:T(8,128)}, f32[16,16,2,16,128]{4,3,2,1,0:T(8,128)S(1)}, u32[]{:S(2)}) copy-start(f32[16,16,2,16,128]{4,3,2,1,0:T(8,128)S(1)} %residual.1) | copy-start | bytes 12582916
  70.8 25.1 %copy-start.2 = (bf16[27,128,256]{2,1,0:T(8,128)(2,1)S(1)}, bf16[27,128,256]{2,1,0:T(8,128)(2,1)}, u32[]{:S(2)}) copy-start(bf16[27,128,256]{2,1,0:T(8,128)(2,1)} %param.11) | copy-start | bytes 5308420
  83.8 12.1 %collective-permute-start.4 = (bf16[1,32,16,128]{3,2,1,0:T(8,128)(2,1)S(1)}, bf16[1,32,16,128]{3,2,1,0:T(8,128)(2,1)S(1)}, u32[]{:S(2)}, u32[]{:S(2)}) collective-permute-start(bf16[1,32,16,128]{3,2,1,0:T(8,128)(2,1)S(1)} %get-tuple-element.16), channel_id=1, source_target_pairs={{0,1},{1,2},{2,3},{4,5},{5,6},{6,7},{8,9},{9,10},{10,11},{12,13},{... | collective-permute-start | bytes 393224 | tf_op jit(solution)/shard_map/ppermute | solution.py:354
  86.7 9.2 %collective-permute-start.5 = (bf16[16,1,16,128]{3,2,1,0:T(8,128)(2,1)S(1)}, bf16[16,1,16,128]{3,2,1,0:T(8,128)(2,1)S(1)}, u32[]{:S(2)}, u32[]{:S(2)}) collective-permute-start(bf16[16,1,16,128]{3,2,1,0:T(8,128)(2,1)S(1)} %get-tuple-element.17), channel_id=1, source_target_pairs={{0,4},{4,8},{8,12},{12,16},{16,20},{20,24},{24,28},{1,5},{5,9},{9,... | collective-permute-start | bytes 196616 | tf_op jit(solution)/shard_map/ppermute | solution.py:354
  89.2 6.7 %collective-permute-start.6 = (bf16[1,1,16,128]{3,2,1,0:T(8,128)(2,1)S(1)}, bf16[1,1,16,128]{3,2,1,0:T(8,128)(2,1)S(1)}, u32[]{:S(2)}, u32[]{:S(2)}) collective-permute-start(bf16[1,1,16,128]{3,2,1,0:T(8,128)(2,1)S(1)} %get-tuple-element.18), channel_id=1, source_target_pairs={{0,5},{1,6},{2,7},{4,9},{5,10},{6,11},{8,13},{9,14},{10,15},{12,17... | collective-permute-start | bytes 12296 | tf_op jit(solution)/shard_map/ppermute | solution.py:389

commit v3 on v2

--- a/solution.py
+++ b/solution.py
@@ -1,4 +1,5 @@
 import functools
+import math
 import jax
 import jax.numpy as jnp
 from jax import lax
@@ -11,11 +12,13 @@
 EXTRA = 8
 
 
-def pack_kernel(devices, cap, owner_ref, cell_ref, rows_ref, out_ref,
+def pack_kernel(devices, cap, cut, owner_ref, cell_ref, rows_ref, first_ref, second_ref,
                 wide, spread, slot_vmem, slot_smem, sem):
     p_local, _ = rows_ref.shape
     blocks = p_local // LANES
-    stride = cap + EXTRA
+    stride = cut + EXTRA
+    rest = cap - cut
+    break_at = devices * stride
     upper = (lax.broadcasted_iota(jnp.int32, (LANES, LANES), 0)
              <= lax.broadcasted_iota(jnp.int32, (LANES, LANES), 1)).astype(jnp.bfloat16)
     ids = lax.broadcasted_iota(jnp.int32, (devices, LANES), 0)
@@ -30,7 +33,8 @@
         run = jnp.dot(hot.astype(jnp.bfloat16), upper, preferred_element_type=jnp.float32)
         place = jnp.sum(hot * (run + base), axis=0, keepdims=True).astype(jnp.int32) - 1
         base = base + run[:, LANES - 1:LANES]
-        slot_vmem[b:b + 1, :] = own * stride + place
+        slot_vmem[b:b + 1, :] = jnp.where(
+            place < cut, own * stride + place, break_at - cut + own * rest + place)
         high = jnp.where(hit, (cell // LANES + 1).astype(jnp.float32), 0.0)
         low = jnp.where(hit, (cell % LANES).astype(jnp.float32), 0.0)
         left = jnp.concatenate([high, low], axis=0).astype(jnp.bfloat16)
@@ -48,7 +52,7 @@
             if width < LANES:
                 piece = jnp.concatenate(
                     [piece, jnp.zeros((devices, LANES - width), jnp.float32)], axis=1)
-            spread[pl.ds(cap + part * per + j, devices, stride=stride), :] = piece
+            spread[pl.ds(cut + part * per + j, devices, stride=stride), :] = piece
     copy.wait()
 
     def step(b, carry):
@@ -57,19 +61,23 @@
         return carry
 
     lax.fori_loop(0, blocks, step, 0)
-    out_ref[...] = spread[...].astype(jnp.bfloat16)
-
-
-def pack(owner, cell, rows, devices, cap):
+    first_ref[...] = spread[0:break_at, :].astype(jnp.bfloat16)
+    second_ref[...] = spread[break_at:, :].astype(jnp.bfloat16)
+
+
+def pack(owner, cell, rows, devices, cap, cut):
     p_local, channels = rows.shape
     blocks = p_local // LANES
     total = devices * (cap + EXTRA)
     vm = pl.BlockSpec(memory_space=pltpu.VMEM)
     return pl.pallas_call(
-        functools.partial(pack_kernel, devices, cap),
-        out_shape=jax.ShapeDtypeStruct((total, channels), jnp.bfloat16),
+        functools.partial(pack_kernel, devices, cap, cut),
+        out_shape=[
+            jax.ShapeDtypeStruct((devices * (cut + EXTRA), channels), jnp.bfloat16),
+            jax.ShapeDtypeStruct((devices * (cap - cut), channels), jnp.bfloat16),
+        ],
         in_specs=[vm, vm, vm],
-        out_specs=vm,
+        out_specs=[vm, vm],
         scratch_shapes=[
             pltpu.VMEM((p_local, channels), jnp.float32),
             pltpu.VMEM((total, channels), jnp.float32),
@@ -82,58 +90,86 @@
     )(owner.reshape(blocks, LANES), cell.reshape(blocks, LANES), rows)
 
 
-WAYS = 6
-PIECES = 4
-LIMIT = 48 * 2**20
-
-
-def add_kernel(capacity, got_hbm, base_hbm, out_ref, front_ref, side_ref, corner_ref,
-               landed, wide, slot_vmem, slot_smem, sems, *sums):
-    span_x, span_y, span_z, channels = out_ref.shape
-    cells = span_x * span_y * span_z
-    total, _ = landed.shape
-    stride = capacity + EXTRA
-    devices = total // stride
-    per = -(-capacity // LANES)
-    width = min(LANES, capacity)
-    piece = total // PIECES
-    copies = [
-        pltpu.make_async_copy(got_hbm.at[pl.ds(i * piece, piece)],
-                              landed.at[pl.ds(i * piece, piece)], sems.at[i])
-        for i in range(PIECES)
-    ]
-    for copy in copies:
-        copy.start()
-    first = pltpu.make_async_copy(base_hbm, sums[0].at[pl.ds(0, cells)], sems.at[PIECES])
-    first.start()
-    half = len(sums) // 2
-    for s in sums[1:half]:
-        s[...] = jnp.zeros_like(s)
-    for i, copy in enumerate(copies):
-        copy.wait()
-        wide[i * piece:(i + 1) * piece, :] = landed[i * piece:(i + 1) * piece, :].astype(
-            jnp.float32)
-    for j in range(per):
-        high = wide[pl.ds(capacity + j, devices, stride=stride), :].astype(jnp.int32)
-        low = wide[pl.ds(capacity + per + j, devices, stride=stride), :].astype(jnp.int32)
-        slot_vmem[j * devices:(j + 1) * devices, :] = jnp.where(
-            high > 0, (high - 1) * LANES + low, cells)
-    copy = pltpu.make_async_copy(slot_vmem, slot_smem, sems.at[PIECES + 1])
-    copy.start()
-    for s in sums[max(half, 1):]:
-        s[...] = jnp.zeros_like(s)
-    copy.wait()
-    first.wait()
-    for j in range(per):
+WAYS = 4
+
+
+def add_loop(slots, wide, sums, devices, stride, begin, end):
+    for j in range(begin // LANES, -(-end // LANES)):
+        low, high = max(begin, j * LANES), min(end, (j + 1) * LANES)
+
         def step(o, carry):
-            start = pl.multiple_of(o * stride + j * LANES, 8)
-            for u in range(width):
-                at = slot_smem[j * devices + o, u]
+            start = pl.multiple_of(o * stride + (low - begin), 8)
+            for u in range(high - low):
+                at = slots[j * devices + o, low - j * LANES + u]
                 s = sums[u % len(sums)]
                 s[pl.ds(at, 1), :] += wide[pl.ds(start + u, 1), :]
             return carry
 
         lax.fori_loop(0, devices, step, 0)
+
+
+def early_kernel(cap, cut, got_ref, out_ref, slot_ref, wide, slot_smem, sem, *sums):
+    cells, _ = out_ref.shape
+    total, _ = got_ref.shape
+    stride = cut + EXTRA
+    devices = total // stride
+    per = -(-cap // LANES)
+    wide[...] = got_ref[...].astype(jnp.float32)
+    for j in range(per):
+        high = wide[pl.ds(cut + j, devices, stride=stride), :].astype(jnp.int32)
+        low = wide[pl.ds(cut + per + j, devices, stride=stride), :].astype(jnp.int32)
+        slot_ref[j * devices:(j + 1) * devices, :] = jnp.where(
+            high > 0, (high - 1) * LANES + low, cells)
+    copy = pltpu.make_async_copy(slot_ref, slot_smem, sem)
+    copy.start()
+    for s in sums:
+        s[...] = jnp.zeros_like(s)
+    copy.wait()
+    add_loop(slot_smem, wide, sums, devices, stride, 0, cut)
+    total = sums[0][pl.ds(0, cells), :]
+    for s in sums[1:]:
+        total = total + s[pl.ds(0, cells), :]
+    out_ref[...] = total
+
+
+def add_early(got, cells, cap, cut):
+    total, channels = got.shape
+    devices = total // (cut + EXTRA)
+    per = -(-cap // LANES)
+    vm = pl.BlockSpec(memory_space=pltpu.VMEM)
+    return pl.pallas_call(
+        functools.partial(early_kernel, cap, cut),
+        out_shape=[
+            jax.ShapeDtypeStruct((cells, channels), jnp.float32),
+            jax.ShapeDtypeStruct((devices * per, LANES), jnp.int32),
+        ],
+        in_specs=[vm],
+        out_specs=[vm, vm],
+        scratch_shapes=[
+            pltpu.VMEM((total, channels), jnp.float32),
+            pltpu.SMEM((devices * per, LANES), jnp.int32),
+            pltpu.SemaphoreType.DMA,
+        ] + [pltpu.VMEM((cells + 8, channels), jnp.float32)] * WAYS,
+        compiler_params=pltpu.CompilerParams(vmem_limit_bytes=36 * 2**20),
+        name="add_early",
+        cost_estimate=pl.CostEstimate(flops=10**8, bytes_accessed=8 * 10**6, transcendentals=0),
+    )(got)
+
+
+def late_kernel(cap, cut, slots, got_ref, base_hbm, out_ref, front_ref, side_ref, corner_ref,
+                wide, sem, *sums):
+    span_x, span_y, span_z, channels = out_ref.shape
+    cells = span_x * span_y * span_z
+    total, _ = got_ref.shape
+    rest = cap - cut
+    devices = total // rest
+    first = pltpu.make_async_copy(base_hbm, sums[0].at[pl.ds(0, cells)], sem)
+    first.start()
+    for s in sums[1:]:
+        s[...] = jnp.zeros_like(s)
+    wide[...] = got_ref[...].astype(jnp.float32)
+    first.wait()
+    add_loop(slots, wide, sums, devices, rest, cut, cap)
 
     def finish(x, carry):
         at = pl.ds(pl.multiple_of(x * (span_y * span_z), 8), span_y * span_z)
@@ -150,38 +186,36 @@
     corner_ref[...] = out_ref[span_x - 1:, span_y - 1:]
 
 
-def add_rows(got, base, shape, capacity):
+def add_late(slots, got, base, shape, cap, cut):
     span_x, span_y, span_z, channels = shape
     cells = span_x * span_y * span_z
     total = got.shape[0]
-    devices = total // (capacity + EXTRA)
-    per = -(-capacity // LANES)
     vm = pl.BlockSpec(memory_space=pltpu.VMEM)
-    hbm = pl.BlockSpec(memory_space=pl.ANY)
     return pl.pallas_call(
-        functools.partial(add_kernel, capacity),
+        functools.partial(late_kernel, cap, cut),
         out_shape=[
             jax.ShapeDtypeStruct(shape, jnp.bfloat16),
             jax.ShapeDtypeStruct((1, span_y, span_z, channels), jnp.bfloat16),
             jax.ShapeDtypeStruct((span_x, 1, span_z, channels), jnp.bfloat16),
             jax.ShapeDtypeStruct((1, 1, span_z, channels), jnp.bfloat16),
         ],
-        in_specs=[hbm, hbm],
+        in_specs=[pl.BlockSpec(memory_space=pltpu.SMEM), vm, pl.BlockSpec(memory_space=pl.ANY)],
         out_specs=[vm] * 4,
         scratch_shapes=[
-            pltpu.VMEM((total, channels), jnp.bfloat16),
             pltpu.VMEM((total, channels), jnp.float32),
-            pltpu.VMEM((devices * per, LANES), jnp.int32),
-            pltpu.SMEM((devices * per, LANES), jnp.int32),
-            pltpu.SemaphoreType.DMA((PIECES + 2,)),
+            pltpu.SemaphoreType.DMA,
         ] + [pltpu.VMEM((cells + 8, channels), jnp.float32)] * WAYS,
         compiler_params=pltpu.CompilerParams(vmem_limit_bytes=LIMIT),
-        name="add_rows",
+        name="add_late",
         cost_estimate=pl.CostEstimate(flops=10**8, bytes_accessed=8 * 10**6, transcendentals=0),
-    )(got, base)
-
-
-def residual_kernel(group, level_ref, ylow_ref, yhigh_ref, xlow_ref, xhigh_ref, w_ref, out_ref,
+    )(slots, got, base)
+
+
+LIMIT = 48 * 2**20
+
+
+def residual_kernel(group, level_ref, ylow_ref, yhigh_ref, xlow_ref, xhigh_ref,
+                    ll_ref, lh_ref, hl_ref, hh_ref, partial_ref, w_ref, out_ref,
                     plane, taps, wide, result):
     span_x, span_y, span_z, channels = level_ref.shape
     half = (span_y + 2) // 2
@@ -215,17 +249,19 @@
                      par * three + c * channels:par * three + (c + 1) * channels] = (
                     value[:, par].reshape(lines, channels))
 
-    for x, ref in ((0, xlow_ref), (span_x + 1, xhigh_ref)):
-        plane[8:8 + count, :] = ref[...].reshape(count, channels).astype(jnp.float32)
+    def stage(x, low, middle, high):
+        plane[8:8 + span_z, :] = low.reshape(span_z, channels).astype(jnp.float32)
+        plane[8 + span_z:8 + count - span_z, :] = middle.reshape(
+            span_y * span_z, channels).astype(jnp.float32)
+        plane[8 + count - span_z:8 + count, :] = high.reshape(
+            span_z, channels).astype(jnp.float32)
         spread(x)
 
+    stage(0, ll_ref[...], xlow_ref[...], lh_ref[...])
+    stage(span_x + 1, hl_ref[...], xhigh_ref[...], hh_ref[...])
+
     def fill(x, carry):
-        plane[8:8 + span_z, :] = ylow_ref[x].reshape(span_z, channels).astype(jnp.float32)
-        plane[8 + span_z:8 + count - span_z, :] = level_ref[x].reshape(
-            span_y * span_z, channels).astype(jnp.float32)
-        plane[8 + count - span_z:8 + count, :] = yhigh_ref[x].reshape(
-            span_z, channels).astype(jnp.float32)
-        spread(x + 1)
+        stage(x + 1, ylow_ref[x], level_ref[x], yhigh_ref[x])
         return carry
 
     lax.fori_loop(0, span_x, fill, 0)
@@ -248,13 +284,13 @@
                                s * channels:(s + 1) * channels]
                 value = jnp.maximum(value, 0.0).reshape(span_y // 2, span_z, channels)
                 here = level_ref[x].reshape(span_y // 2, 2, span_z, channels)[:, s]
-                out_ref[x, :, s] = value + here.astype(jnp.float32)
+                out_ref[x, :, s] = value + here.astype(jnp.float32) + partial_ref[x, :, s]
         return carry
 
     lax.fori_loop(0, span_x // group, multiply, 0)
 
 
-def residual_base(level, ylow, yhigh, xlow, xhigh, w_res, group=4):
+def residual_base(level, faces, partial, w_res, group=4):
     span_x, span_y, span_z, channels = level.shape
     lines = (span_y + 2) // 2 * span_z
     vm = pl.BlockSpec(memory_space=pltpu.VMEM)
@@ -262,7 +298,7 @@
     out = pl.pallas_call(
         functools.partial(residual_kernel, group),
         out_shape=jax.ShapeDtypeStruct((span_x, span_y // 2, 2, span_z, channels), jnp.float32),
-        in_specs=[vm] * 6,
+        in_specs=[vm] * 11,
         out_specs=vm,
         scratch_shapes=[
             pltpu.VMEM(((span_y + 2) * span_z + 16, channels), jnp.float32),
@@ -273,7 +309,7 @@
         compiler_params=pltpu.CompilerParams(vmem_limit_bytes=36 * 2**20),
         name="residual",
         cost_estimate=pl.CostEstimate(flops=flops, bytes_accessed=8 * 10**6, transcendentals=0),
-    )(level, ylow, yhigh, xlow, xhigh, w_res)
+    )(level, *faces, partial.reshape(span_x, span_y // 2, 2, span_z, channels), w_res)
     return out.reshape(span_x * span_y * span_z, channels)
 
 
@@ -345,48 +381,57 @@
     )(joined, front, side, corner, w_down.reshape(-1, wide))
 
 
-def pairs_of(axis, by):
-    count = lax.axis_size(axis)
-    return [(i, i + by) for i in range(count) if 0 <= i + by < count]
-
-
-def passed_along(array, axis, by):
-    return lax.ppermute(array, axis, pairs_of(axis, by))
-
-
-def body(points, dest_owner, dest_cell, level_input, w_res, w_down):
+def shifted(array, by_pts, by_nbr):
     count_pts = lax.axis_size("pts")
     count_nbr = lax.axis_size("nbr")
-    devices = count_pts * count_nbr
-    channels = points.shape[-1]
-    rows = points.reshape(-1, channels)
-    capacity = 2 * rows.shape[0] // devices
-    level = level_input
-    low_y = passed_along(level[:, -1:], "pts", 1)
-    high_y = passed_along(level[:, :1], "pts", -1)
-    outgoing = pack(dest_owner.reshape(-1), dest_cell.reshape(-1), rows, devices, capacity)
-    last = jnp.concatenate([low_y[-1:], level[-1:], high_y[-1:]], axis=1)
-    first = jnp.concatenate([low_y[:1], level[:1], high_y[:1]], axis=1)
-    outgoing, last, first = lax.optimization_barrier((outgoing, last, first))
-    low_x = passed_along(last, "nbr", 1)
-    high_x = passed_along(first, "nbr", -1)
+    pairs = [
+        (i * count_nbr + j, (i + by_pts) * count_nbr + j + by_nbr)
+        for i in range(count_pts)
+        for j in range(count_nbr)
+        if 0 <= i + by_pts < count_pts and 0 <= j + by_nbr < count_nbr
+    ]
+    return lax.ppermute(array, ("pts", "nbr"), pairs)
+
+
+def exchanged(array, devices):
     got = lax.all_to_all(
-        outgoing.reshape(devices, capacity + EXTRA, channels),
+        array.reshape(devices, -1, array.shape[-1]),
         ("pts", "nbr"),
         split_axis=0,
         concat_axis=0,
         tiled=True,
-    ).reshape(outgoing.shape)
-    base = residual_base(level, low_y, high_y, low_x, high_x, w_res)
-    joined, front, side, corner = add_rows(got, base, level.shape, capacity)
-    diagonal = [
-        (i * count_nbr + j, (i + 1) * count_nbr + j + 1)
-        for i in range(count_pts - 1)
-        for j in range(count_nbr - 1)
+    )
+    return got.reshape(array.shape)
+
+
+def body(points, dest_owner, dest_cell, level_input, w_res, w_down):
+    devices = lax.axis_size("pts") * lax.axis_size("nbr")
+    channels = points.shape[-1]
+    rows = points.reshape(-1, channels)
+    capacity = 2 * rows.shape[0] // devices
+    cut = capacity // 2
+    cells = math.prod(level_input.shape[:3])
+    early, late = pack(
+        dest_owner.reshape(-1), dest_cell.reshape(-1), rows, devices, capacity, cut)
+    early, late, level = lax.optimization_barrier((early, late, level_input))
+    early = exchanged(early, devices)
+    faces = [
+        shifted(level[:, -1:], 1, 0),
+        shifted(level[:, :1], -1, 0),
+        shifted(level[-1:], 0, 1),
+        shifted(level[:1], 0, -1),
+        shifted(level[-1:, -1:], 1, 1),
+        shifted(level[-1:, :1], -1, 1),
+        shifted(level[:1, -1:], 1, -1),
+        shifted(level[:1, :1], -1, -1),
     ]
-    front = passed_along(front, "nbr", 1)
-    side = passed_along(side, "pts", 1)
-    corner = lax.ppermute(corner, ("pts", "nbr"), diagonal)
+    late = exchanged(late, devices)
+    partial, slots = add_early(early, cells, capacity, cut)
+    base = residual_base(level, faces, partial, w_res)
+    joined, front, side, corner = add_late(slots, late, base, level.shape, capacity, cut)
+    front = shifted(front, 0, 1)
+    side = shifted(side, 1, 0)
+    corner = shifted(corner, 1, 1)
     return lower(joined, front, side, corner, w_down)
 
 

time: 103 us -> 143 us (1.39)
  blocking collectives: 0 us -> 33.2 us
  waiting for transfers between devices: 30.4 us -> 12.4 us
  starting transfers between devices: 24.7 us -> 40.7 us
  Pallas kernels: 40.5 us -> 48 us
    all_to_all x0 -> x1, blocking collectives: none -> 33.2 us  [exchanged(): lax.all_to_all(array.reshape(devices, -1, array.shape[-1]), ('pts', 'nbr'...]
    all_to_all x1, waiting for transfers between devices: 17 us -> 0.01 us  [exchanged(): lax.all_to_all(array.reshape(devices, -1, array.shape[-1]), ('pts', 'nbr'...]
    ppermute x7 -> x11, starting transfers between devices: 19.6 us -> 35.8 us  [shifted(): return lax.ppermute(array, ('pts', 'nbr'), pairs)]
    pallas_call x2 -> x3, Pallas kernels: 22.2 us -> 29.7 us  [the longest x1 11.9 us: add_late(): pl.pallas_call(functools.partial(late_kernel, cap, cut), out_shape=[jax.S...]
    ppermute x7 -> x11, waiting for transfers between devices: 13.4 us -> 12.4 us  [shifted(): return lax.ppermute(array, ('pts', 'nbr'), pairs)]
  transfers between devices with their start and end apart: 8 -> 12, of which waited for: 3 -> 4; matrix products, arithmetic and copies ran while one was open for 1% -> 2% of each run, Pallas kernels for 22% -> 15%
where the time goes in v3:
time: 143 us; the launch traced here: 141 us
  Pallas kernels  48 us (34%)
  starting transfers between devices  40.7 us (28%)
  blocking collectives  33.2 us (23%)
  waiting for transfers between devices  12.4 us (9%)
  local copies, waits for them, and re-layouts  6.15 us (4%)
    ppermute x11, starting transfers between devices, shifted(): return lax.ppermute(array, ('pts', 'nbr'), pairs)  35.8 us
    all_to_all x1, blocking collectives, exchanged(): lax.all_to_all(array.reshape(devices, -1, array.shape[-1]), ('pts', 'nbr'...  33.2 us
    pallas_call x1, Pallas kernels, residual_base(): pl.pallas_call(functools.partial(residual_kernel, group), out_shape=jax.S...  13 us
    ppermute x11, waiting for transfers between devices, shifted(): return lax.ppermute(array, ('pts', 'nbr'), pairs)  12.4 us
    pallas_call x1, Pallas kernels, add_late(): pl.pallas_call(functools.partial(late_kernel, cap, cut), out_shape=[jax.S...  11.9 us
    pallas_call x1, Pallas kernels, pack(): pl.pallas_call(functools.partial(pack_kernel, devices, cap, cut), out_sha...  9.02 us
    pallas_call x1, Pallas kernels, add_early(): pl.pallas_call(functools.partial(early_kernel, cap, cut), out_shape=[jax....  8.75 us
    pallas_call x1, Pallas kernels, lower(): pl.pallas_call(lower_kernel, out_shape=jax.ShapeDtypeStruct((span_x // 2,...  5.29 us
  transfers between devices with their start and end apart: 12, of which 4 were waited for; matrix products, arithmetic and copies ran while one was open for 2% of the time, Pallas kernels for 15%

profile of v3, /device:TPU:12, one launch (start us, length us, event | category | flops | bytes accessed | tf_op | source)
XLA Modules:
  0.0 140.6 jit_solution(2575522518593400342)
XLA Ops:
  0.0 9.0 %pack.1 = (bf16[4352,128]{1,0:T(8,128)(2,1)}, bf16[4096,128]{1,0:T(8,128)(2,1)}) custom-call(s32[32,128]{1,0:T(8,128)} %bitcast.18, s32[32,128]{1,0:T(8,128)} %bitcast.19, bf16[4096,128]{1,0:T(8,128)(2,1)} %bitcast.16), custom_call_target="tpu_custom_call" | custom-call | flops 100000000 | bytes 4000000 | tf_op jit(solution)/shard_map/pack/pallas_call | solution.py:73
  9.0 33.2 %all_to_all.10 = bf16[32,136,128]{2,1,0:T(8,128)(2,1)S(1)} all-to-all(bf16[32,136,128]{2,1,0:T(8,128)(2,1)} %bitcast.15), channel_id=1, replica_groups=mesh['pts'=8,'nbr'=4] {'pts','nbr'}, dimensions={0} | all-to-all | bytes 2228224 | tf_op jit(solution)/shard_map/all_to_all | solution.py:397
  42.2 4.9 %all-to-all-start.1 = ((bf16[32,128,128]{2,1,0:T(8,128)(2,1)}), bf16[32,128,128]{2,1,0:T(8,128)(2,1)S(1)}, u32[]{:S(2)}, u32[]{:S(2)}) async-start(bf16[32,128,128]{2,1,0:T(8,128)(2,1)} %bitcast.17), calls=%async_computation.1 | async-start | bytes 2097152 | tf_op jit(solution)/shard_map/all_to_all | solution.py:397
  47.1 0.9 fusion.2
  48.0 3.3 %collective-permute-start.1 = (bf16[16,1,16,128]{3,2,1,0:T(8,128)(2,1)S(1)}, bf16[16,1,16,128]{3,2,1,0:T(8,128)(2,1)S(1)}, u32[]{:S(2)}, u32[]{:S(2)}) collective-permute-start(bf16[16,1,16,128]{3,2,1,0:T(8,128)(2,1)S(1)} %get-tuple-element.33), channel_id=1, source_target_pairs={{4,0},{5,1},{6,2},{7,3},{8,4},{9,5},{10,6},{11,7},{12,8},{13,9},{1... | collective-permute-start | bytes 196616 | tf_op jit(solution)/shard_map/ppermute | solution.py:393
  51.3 2.5 %collective-permute-start = (bf16[16,1,16,128]{3,2,1,0:T(8,128)(2,1)S(1)}, bf16[16,1,16,128]{3,2,1,0:T(8,128)(2,1)S(1)}, u32[]{:S(2)}, u32[]{:S(2)}) collective-permute-start(bf16[16,1,16,128]{3,2,1,0:T(8,128)(2,1)S(1)} %get-tuple-element.34), channel_id=1, source_target_pairs={{0,4},{1,5},{2,6},{3,7},{4,8},{5,9},{6,10},{7,11},{8,12},{9,13},{1... | collective-permute-start | bytes 196616 | tf_op jit(solution)/shard_map/ppermute | solution.py:393
  53.9 1.0 fusion.1
  54.9 1.9 %collective-permute-start.3 = (bf16[1,32,16,128]{3,2,1,0:T(8,128)(2,1)S(1)}, bf16[1,32,16,128]{3,2,1,0:T(8,128)(2,1)S(1)}, u32[]{:S(2)}, u32[]{:S(2)}) collective-permute-start(bf16[1,32,16,128]{3,2,1,0:T(8,128)(2,1)S(1)} %get-tuple-element.31), channel_id=1, source_target_pairs={{1,0},{2,1},{3,2},{5,4},{6,5},{7,6},{9,8},{10,9},{11,10},{13,12},{... | collective-permute-start | bytes 393224 | tf_op jit(solution)/shard_map/ppermute | solution.py:393
  56.8 2.4 %collective-permute-start.2 = (bf16[1,32,16,128]{3,2,1,0:T(8,128)(2,1)S(1)}, bf16[1,32,16,128]{3,2,1,0:T(8,128)(2,1)S(1)}, u32[]{:S(2)}, u32[]{:S(2)}) collective-permute-start(bf16[1,32,16,128]{3,2,1,0:T(8,128)(2,1)S(1)} %get-tuple-element.32), channel_id=1, source_target_pairs={{0,1},{1,2},{2,3},{4,5},{5,6},{6,7},{8,9},{9,10},{10,11},{12,13},{... | collective-permute-start | bytes 393224 | tf_op jit(solution)/shard_map/ppermute | solution.py:393
  59.2 0.7 fusion
  59.9 4.9 %collective-permute-start.7 = (bf16[1,1,16,128]{3,2,1,0:T(8,128)(2,1)S(1)}, bf16[1,1,16,128]{3,2,1,0:T(8,128)(2,1)S(1)}, u32[]{:S(2)}, u32[]{:S(2)}) collective-permute-start(bf16[1,1,16,128]{3,2,1,0:T(8,128)(2,1)S(1)} %get-tuple-element.27), channel_id=1, source_target_pairs={{5,0},{6,1},{7,2},{9,4},{10,5},{11,6},{13,8},{14,9},{15,10},{17,12... | collective-permute-start | bytes 12296 | tf_op jit(solution)/shard_map/ppermute | solution.py:393
  64.8 1.3 collective-permute-done.7.hh_ref
  66.1 11.2 %collective-permute-start.6 = (bf16[1,1,16,128]{3,2,1,0:T(8,128)(2,1)S(1)}, bf16[1,1,16,128]{3,2,1,0:T(8,128)(2,1)S(1)}, u32[]{:S(2)}, u32[]{:S(2)}) collective-permute-start(bf16[1,1,16,128]{3,2,1,0:T(8,128)(2,1)S(1)} %get-tuple-element.28), channel_id=1, source_target_pairs={{1,4},{2,5},{3,6},{5,8},{6,9},{7,10},{9,12},{10,13},{11,14},{13,16... | collective-permute-start | bytes 12296 | tf_op jit(solution)/shard_map/ppermute | solution.py:393
  77.4 1.3 collective-permute-done.6.hl_ref
  78.7 1.9 %collective-permute-start.5 = (bf16[1,1,16,128]{3,2,1,0:T(8,128)(2,1)S(1)}, bf16[1,1,16,128]{3,2,1,0:T(8,128)(2,1)S(1)}, u32[]{:S(2)}, u32[]{:S(2)}) collective-permute-start(bf16[1,1,16,128]{3,2,1,0:T(8,128)(2,1)S(1)} %get-tuple-element.29), channel_id=1, source_target_pairs={{4,1},{5,2},{6,3},{8,5},{9,6},{10,7},{12,9},{13,10},{14,11},{16,13... | collective-permute-start | bytes 12296 | tf_op jit(solution)/shard_map/ppermute | solution.py:393
  80.6 3.9 %collective-permute-done.5.lh_ref = bf16[1,1,16,128]{3,2,1,0:T(8,128)(2,1)S(1)} collective-permute-done((bf16[1,1,16,128]{3,2,1,0:T(8,128)(2,1)S(1)}, bf16[1,1,16,128]{3,2,1,0:T(8,128)(2,1)S(1)}, u32[]{:S(2)}, u32[]{:S(2)}) %collective-permute-start.5) | collective-permute-done | bytes 4128 | tf_op jit(solution)/shard_map/ppermute | solution.py:393
  84.5 1.9 %collective-permute-start.4 = (bf16[1,1,16,128]{3,2,1,0:T(8,128)(2,1)S(1)}, bf16[1,1,16,128]{3,2,1,0:T(8,128)(2,1)S(1)}, u32[]{:S(2)}, u32[]{:S(2)}) collective-permute-start(bf16[1,1,16,128]{3,2,1,0:T(8,128)(2,1)S(1)} %get-tuple-element.30), channel_id=1, source_target_pairs={{0,5},{1,6},{2,7},{4,9},{5,10},{6,11},{8,13},{9,14},{10,15},{12,17... | collective-permute-start | bytes 12296 | tf_op jit(solution)/shard_map/ppermute | solution.py:393
  86.4 8.7 %add_early.1 = (f32[8192,128]{1,0:T(8,128)S(1)}, s32[64,128]{1,0:T(8,128)S(1)}) custom-call(bf16[4352,128]{1,0:T(8,128)(2,1)S(1)} %bitcast.10), custom_call_target="tpu_custom_call" | custom-call | flops 100000000 | bytes 8000000 | tf_op jit(solution)/shard_map/add_early/pallas_call | solution.py:140
  95.2 0.0 collective-permute-done.4.ll_ref
  95.2 0.0 collective-permute-done.1.yhigh_ref
  95.2 0.0 collective-permute-done.3.xhigh_ref
  95.2 0.0 collective-permute-done.2.xlow_ref
  95.2 0.0 copy-start.1
  95.2 1.6 %copy-done.1 = bf16[16,32,16,128]{3,2,1,0:T(8,128)(2,1)S(1)} copy-done((bf16[16,32,16,128]{3,2,1,0:T(8,128)(2,1)S(1)}, bf16[16,32,16,128]{3,2,1,0:T(8,128)(2,1)}, u32[]{:S(2)}) %copy-start.1) | copy-done | bytes 2097176
  96.8 13.0 %residual.1 = f32[16,16,2,16,128]{4,3,2,1,0:T(8,128)S(1)} custom-call(bf16[16,32,16,128]{3,2,1,0:T(8,128)(2,1)S(1)} %copy-done.1, bf16[16,1,16,128]{3,2,1,0:T(8,128)(2,1)S(1)} %collective-permute-done.ylow_ref, bf16[16,1,16,128]{3,2,1,0:T(8,128)(2,1)S(1)} %collective-permute-done.1.yhigh_ref, bf16[1,32,16,128]{3,2,1,0:T(8,128)(2,1)S(1)} %collective-permute-done.2.xlow_ref, ...), custom_call_target="tpu_custom_call" | custom-call | flops 7247757312 | bytes 8000000 | tf_op jit(solution)/shard_map/residual/pallas_call | solution.py:298
  109.8 1.9 %copy-done = f32[16,16,2,16,128]{4,3,2,1,0:T(8,128)} copy-done((f32[16,16,2,16,128]{4,3,2,1,0:T(8,128)}, f32[16,16,2,16,128]{4,3,2,1,0:T(8,128)S(1)}, u32[]{:S(2)}) %copy-start) | copy-done | bytes 4194328
  111.8 11.9 %add_late.1 = (bf16[16,32,16,128]{3,2,1,0:T(8,128)(2,1)S(1)}, bf16[1,32,16,128]{3,2,1,0:T(8,128)(2,1)S(1)}, bf16[16,1,16,128]{3,2,1,0:T(8,128)(2,1)S(1)}, bf16[1,1,16,128]{3,2,1,0:T(8,128)(2,1)S(1)}) custom-call(s32[64,128]{1,0:T(8,128)S(1)} %get-tuple-element.19.slots, bf16[4096,128]{1,0:T(8,128)(2,1)S(1)} %bitcast.12, f32[8192,128]{1,0:T(8,128)} %bitcast.11), custom_call_target="tpu_custom_call" | custom-call | flops 100000000 | bytes 8000000 | tf_op jit(solution)/shard_map/add_late/pallas_call | solution.py:194
  123.7 1.9 %collective-permute-start.8 = (bf16[1,32,16,128]{3,2,1,0:T(8,128)(2,1)S(1)}, bf16[1,32,16,128]{3,2,1,0:T(8,128)(2,1)S(1)}, u32[]{:S(2)}, u32[]{:S(2)}) collective-permute-start(bf16[1,32,16,128]{3,2,1,0:T(8,128)(2,1)S(1)} %get-tuple-element.24), channel_id=1, source_target_pairs={{0,1},{1,2},{2,3},{4,5},{5,6},{6,7},{8,9},{9,10},{10,11},{12,13},{... | collective-permute-start | bytes 393224 | tf_op jit(solution)/shard_map/ppermute | solution.py:393
  125.6 1.9 %collective-permute-start.9 = (bf16[16,1,16,128]{3,2,1,0:T(8,128)(2,1)S(1)}, bf16[16,1,16,128]{3,2,1,0:T(8,128)(2,1)S(1)}, u32[]{:S(2)}, u32[]{:S(2)}) collective-permute-start(bf16[16,1,16,128]{3,2,1,0:T(8,128)(2,1)S(1)} %get-tuple-element.25), channel_id=1, source_target_pairs={{0,4},{1,5},{2,6},{3,7},{4,8},{5,9},{6,10},{7,11},{8,12},{9,13},{1... | collective-permute-start | bytes 196616 | tf_op jit(solution)/shard_map/ppermute | solution.py:393
  127.5 1.9 %collective-permute-start.10 = (bf16[1,1,16,128]{3,2,1,0:T(8,128)(2,1)S(1)}, bf16[1,1,16,128]{3,2,1,0:T(8,128)(2,1)S(1)}, u32[]{:S(2)}, u32[]{:S(2)}) collective-permute-start(bf16[1,1,16,128]{3,2,1,0:T(8,128)(2,1)S(1)} %get-tuple-element.26), channel_id=1, source_target_pairs={{0,5},{1,6},{2,7},{4,9},{5,10},{6,11},{8,13},{9,14},{10,15},{12,17... | collective-permute-start | bytes 12296 | tf_op jit(solution)/shard_map/ppermute | solution.py:393
  129.4 5.9 %collective-permute-done.10.corner_ref = bf16[1,1,16,128]{3,2,1,0:T(8,128)(2,1)S(1)} collective-permute-done((bf16[1,1,16,128]{3,2,1,0:T(8,128)(2,1)S(1)}, bf16[1,1,16,128]{3,2,1,0:T(8,128)(2,1)S(1)}, u32[]{:S(2)}, u32[]{:S(2)}) %collective-permute-start.10) | collective-permute-done | bytes 4128 | tf_op jit(solution)/shard_map/ppermute | solution.py:393
  135.3 5.3 %lower.1 = bf16[8,16,8,256]{3,2,1,0:T(8,128)(2,1)} custom-call(bf16[16,32,16,128]{3,2,1,0:T(8,128)(2,1)S(1)} %get-tuple-element.23.joined_ref, bf16[1,32,16,128]{3,2,1,0:T(8,128)(2,1)S(1)} %collective-permute-done.8.front_ref, bf16[16,1,16,128]{3,2,1,0:T(8,128)(2,1)S(1)} %collective-permute-done.9.side_ref, ...), custom_call_target="tpu_custom_call" | custom-call | flops 1811939328 | bytes 5000000 | tf_op jit(solution)/shard_map/lower/pallas_call | solution.py:368
  (9 shorter events, 0.0 us)
Async XLA Ops:
  42.2 53.0 %copy-start.3 = (bf16[27,128,128]{2,1,0:T(8,128)(2,1)S(1)}, bf16[27,128,128]{2,1,0:T(8,128)(2,1)}, u32[]{:S(2)}) copy-start(bf16[27,128,128]{2,1,0:T(8,128)(2,1)} %w_ref.1) | copy-start | bytes 2654212
  42.2 69.5 %all-to-all-start.1 = ((bf16[32,128,128]{2,1,0:T(8,128)(2,1)}), bf16[32,128,128]{2,1,0:T(8,128)(2,1)S(1)}, u32[]{:S(2)}, u32[]{:S(2)}) async-start(bf16[32,128,128]{2,1,0:T(8,128)(2,1)} %bitcast.17), calls=%async_computation.1 | async-start | bytes 2097152 | tf_op jit(solution)/shard_map/all_to_all | solution.py:397
  48.0 47.2 %collective-permute-start.1 = (bf16[16,1,16,128]{3,2,1,0:T(8,128)(2,1)S(1)}, bf16[16,1,16,128]{3,2,1,0:T(8,128)(2,1)S(1)}, u32[]{:S(2)}, u32[]{:S(2)}) collective-permute-start(bf16[16,1,16,128]{3,2,1,0:T(8,128)(2,1)S(1)} %get-tuple-element.33), channel_id=1, source_target_pairs={{4,0},{5,1},{6,2},{7,3},{8,4},{9,5},{10,6},{11,7},{12,8},{13,9},{1... | collective-permute-start | bytes 196616 | tf_op jit(solution)/shard_map/ppermute | solution.py:393
  51.3 43.8 %collective-permute-start = (bf16[16,1,16,128]{3,2,1,0:T(8,128)(2,1)S(1)}, bf16[16,1,16,128]{3,2,1,0:T(8,128)(2,1)S(1)}, u32[]{:S(2)}, u32[]{:S(2)}) collective-permute-start(bf16[16,1,16,128]{3,2,1,0:T(8,128)(2,1)S(1)} %get-tuple-element.34), channel_id=1, source_target_pairs={{0,4},{1,5},{2,6},{3,7},{4,8},{5,9},{6,10},{7,11},{8,12},{9,13},{1... | collective-permute-start | bytes 196616 | tf_op jit(solution)/shard_map/ppermute | solution.py:393
  54.9 40.3 %collective-permute-start.3 = (bf16[1,32,16,128]{3,2,1,0:T(8,128)(2,1)S(1)}, bf16[1,32,16,128]{3,2,1,0:T(8,128)(2,1)S(1)}, u32[]{:S(2)}, u32[]{:S(2)}) collective-permute-start(bf16[1,32,16,128]{3,2,1,0:T(8,128)(2,1)S(1)} %get-tuple-element.31), channel_id=1, source_target_pairs={{1,0},{2,1},{3,2},{5,4},{6,5},{7,6},{9,8},{10,9},{11,10},{13,12},{... | collective-permute-start | bytes 393224 | tf_op jit(solution)/shard_map/ppermute | solution.py:393
  56.8 38.4 %collective-permute-start.2 = (bf16[1,32,16,128]{3,2,1,0:T(8,128)(2,1)S(1)}, bf16[1,32,16,128]{3,2,1,0:T(8,128)(2,1)S(1)}, u32[]{:S(2)}, u32[]{:S(2)}) collective-permute-start(bf16[1,32,16,128]{3,2,1,0:T(8,128)(2,1)S(1)} %get-tuple-element.32), channel_id=1, source_target_pairs={{0,1},{1,2},{2,3},{4,5},{5,6},{6,7},{8,9},{9,10},{10,11},{12,13},{... | collective-permute-start | bytes 393224 | tf_op jit(solution)/shard_map/ppermute | solution.py:393
  59.9 6.2 %collective-permute-start.7 = (bf16[1,1,16,128]{3,2,1,0:T(8,128)(2,1)S(1)}, bf16[1,1,16,128]{3,2,1,0:T(8,128)(2,1)S(1)}, u32[]{:S(2)}, u32[]{:S(2)}) collective-permute-start(bf16[1,1,16,128]{3,2,1,0:T(8,128)(2,1)S(1)} %get-tuple-element.27), channel_id=1, source_target_pairs={{5,0},{6,1},{7,2},{9,4},{10,5},{11,6},{13,8},{14,9},{15,10},{17,12... | collective-permute-start | bytes 12296 | tf_op jit(solution)/shard_map/ppermute | solution.py:393
  66.1 12.5 %collective-permute-start.6 = (bf16[1,1,16,128]{3,2,1,0:T(8,128)(2,1)S(1)}, bf16[1,1,16,128]{3,2,1,0:T(8,128)(2,1)S(1)}, u32[]{:S(2)}, u32[]{:S(2)}) collective-permute-start(bf16[1,1,16,128]{3,2,1,0:T(8,128)(2,1)S(1)} %get-tuple-element.28), channel_id=1, source_target_pairs={{1,4},{2,5},{3,6},{5,8},{6,9},{7,10},{9,12},{10,13},{11,14},{13,16... | collective-permute-start | bytes 12296 | tf_op jit(solution)/shard_map/ppermute | solution.py:393
  78.7 5.8 %collective-permute-start.5 = (bf16[1,1,16,128]{3,2,1,0:T(8,128)(2,1)S(1)}, bf16[1,1,16,128]{3,2,1,0:T(8,128)(2,1)S(1)}, u32[]{:S(2)}, u32[]{:S(2)}) collective-permute-start(bf16[1,1,16,128]{3,2,1,0:T(8,128)(2,1)S(1)} %get-tuple-element.29), channel_id=1, source_target_pairs={{4,1},{5,2},{6,3},{8,5},{9,6},{10,7},{12,9},{13,10},{14,11},{16,13... | collective-permute-start | bytes 12296 | tf_op jit(solution)/shard_map/ppermute | solution.py:393
  84.5 10.7 %collective-permute-start.4 = (bf16[1,1,16,128]{3,2,1,0:T(8,128)(2,1)S(1)}, bf16[1,1,16,128]{3,2,1,0:T(8,128)(2,1)S(1)}, u32[]{:S(2)}, u32[]{:S(2)}) collective-permute-start(bf16[1,1,16,128]{3,2,1,0:T(8,128)(2,1)S(1)} %get-tuple-element.30), channel_id=1, source_target_pairs={{0,5},{1,6},{2,7},{4,9},{5,10},{6,11},{8,13},{9,14},{10,15},{12,17... | collective-permute-start | bytes 12296 | tf_op jit(solution)/shard_map/ppermute | solution.py:393
  95.2 1.6 %copy-start.1 = (bf16[16,32,16,128]{3,2,1,0:T(8,128)(2,1)S(1)}, bf16[16,32,16,128]{3,2,1,0:T(8,128)(2,1)}, u32[]{:S(2)}) copy-start(bf16[16,32,16,128]{3,2,1,0:T(8,128)(2,1)} %level_ref) | copy-start | bytes 6291460
  109.8 1.9 %copy-start = (f32[16,16,2,16,128]{4,3,2,1,0:T(8,128)}, f32[16,16,2,16,128]{4,3,2,1,0:T(8,128)S(1)}, u32[]{:S(2)}) copy-start(f32[16,16,2,16,128]{4,3,2,1,0:T(8,128)S(1)} %residual.1) | copy-start | bytes 12582916
  111.8 23.6 %copy-start.2 = (bf16[27,128,256]{2,1,0:T(8,128)(2,1)S(1)}, bf16[27,128,256]{2,1,0:T(8,128)(2,1)}, u32[]{:S(2)}) copy-start(bf16[27,128,256]{2,1,0:T(8,128)(2,1)} %param.11) | copy-start | bytes 5308420
  123.7 11.7 %collective-permute-start.8 = (bf16[1,32,16,128]{3,2,1,0:T(8,128)(2,1)S(1)}, bf16[1,32,16,128]{3,2,1,0:T(8,128)(2,1)S(1)}, u32[]{:S(2)}, u32[]{:S(2)}) collective-permute-start(bf16[1,32,16,128]{3,2,1,0:T(8,128)(2,1)S(1)} %get-tuple-element.24), channel_id=1, source_target_pairs={{0,1},{1,2},{2,3},{4,5},{5,6},{6,7},{8,9},{9,10},{10,11},{12,13},{... | collective-permute-start | bytes 393224 | tf_op jit(solution)/shard_map/ppermute | solution.py:393
  125.6 9.7 %collective-permute-start.9 = (bf16[16,1,16,128]{3,2,1,0:T(8,128)(2,1)S(1)}, bf16[16,1,16,128]{3,2,1,0:T(8,128)(2,1)S(1)}, u32[]{:S(2)}, u32[]{:S(2)}) collective-permute-start(bf16[16,1,16,128]{3,2,1,0:T(8,128)(2,1)S(1)} %get-tuple-element.25), channel_id=1, source_target_pairs={{0,4},{1,5},{2,6},{3,7},{4,8},{5,9},{6,10},{7,11},{8,12},{9,13},{1... | collective-permute-start | bytes 196616 | tf_op jit(solution)/shard_map/ppermute | solution.py:393
  127.5 7.8 %collective-permute-start.10 = (bf16[1,1,16,128]{3,2,1,0:T(8,128)(2,1)S(1)}, bf16[1,1,16,128]{3,2,1,0:T(8,128)(2,1)S(1)}, u32[]{:S(2)}, u32[]{:S(2)}) collective-permute-start(bf16[1,1,16,128]{3,2,1,0:T(8,128)(2,1)S(1)} %get-tuple-element.26), channel_id=1, source_target_pairs={{0,5},{1,6},{2,7},{4,9},{5,10},{6,11},{8,13},{9,14},{10,15},{12,17... | collective-permute-start | bytes 12296 | tf_op jit(solution)/shard_map/ppermute | solution.py:393

commit v4 on v2

--- a/solution.py
+++ b/solution.py
@@ -87,7 +87,7 @@
 LIMIT = 48 * 2**20
 
 
-def add_kernel(capacity, got_hbm, base_hbm, out_ref, front_ref, side_ref, corner_ref,
+def add_kernel(capacity, got_hbm, base_hbm, ends_ref, edges_ref, out_ref, front_ref, side_ref, corner_ref,
                landed, wide, slot_vmem, slot_smem, sems, *sums):
     span_x, span_y, span_z, channels = out_ref.shape
     cells = span_x * span_y * span_z
@@ -124,6 +124,14 @@
         s[...] = jnp.zeros_like(s)
     copy.wait()
     first.wait()
+    for i in range(span_x):
+        for k, y in ((0, 0), (1, span_y - 1)):
+            start = (i * span_y + y) * span_z
+            sums[0][start:start + span_z, :] = edges_ref[k, i]
+    for k, x in ((0, 0), (1, span_x - 1)):
+        start = x * span_y * span_z
+        sums[0][start:start + span_y * span_z, :] = ends_ref[k].reshape(
+            span_y * span_z, channels)
     for j in range(per):
         def step(o, carry):
             start = pl.multiple_of(o * stride + j * LANES, 8)
@@ -150,7 +158,7 @@
     corner_ref[...] = out_ref[span_x - 1:, span_y - 1:]
 
 
-def add_rows(got, base, shape, capacity):
+def add_rows(got, base, ends, edges, shape, capacity):
     span_x, span_y, span_z, channels = shape
     cells = span_x * span_y * span_z
     total = got.shape[0]
@@ -166,7 +174,7 @@
             jax.ShapeDtypeStruct((span_x, 1, span_z, channels), jnp.bfloat16),
             jax.ShapeDtypeStruct((1, 1, span_z, channels), jnp.bfloat16),
         ],
-        in_specs=[hbm, hbm],
+        in_specs=[hbm, hbm, vm, vm],
         out_specs=[vm] * 4,
         scratch_shapes=[
             pltpu.VMEM((total, channels), jnp.bfloat16),
@@ -178,20 +186,16 @@
         compiler_params=pltpu.CompilerParams(vmem_limit_bytes=LIMIT),
         name="add_rows",
         cost_estimate=pl.CostEstimate(flops=10**8, bytes_accessed=8 * 10**6, transcendentals=0),
-    )(got, base)
-
-
-def residual_kernel(group, level_ref, ylow_ref, yhigh_ref, xlow_ref, xhigh_ref, w_ref, out_ref,
-                    plane, taps, wide, result):
-    span_x, span_y, span_z, channels = level_ref.shape
-    half = (span_y + 2) // 2
-    lines = half * span_z
-    three = 3 * channels
-    for a in range(3):
+    )(got, base, ends, edges)
+
+
+def join_taps(w_ref, wide, rows):
+    channels = w_ref.shape[-1]
+    for r, a in enumerate(rows):
         for d in range(2):
             for par in range(2):
                 for c in range(3):
-                    at = ((a * 2 + d) * 2 + par) * three + c * channels
+                    at = (((r * 2 + d) * 2 + par) * 3 + c) * channels
                     for s in range(2):
                         b = 2 * d + par - s
                         if 0 <= b <= 2:
@@ -199,33 +203,43 @@
                         else:
                             tile = jnp.zeros((channels, channels), jnp.bfloat16)
                         wide[at:at + channels, s * channels:(s + 1) * channels] = tile
-    spot = lax.broadcasted_iota(jnp.int32, ((span_y + 2) * span_z, channels), 0) % span_z
+
+
+def shifts(plane, count, span_z):
+    spot = lax.broadcasted_iota(jnp.int32, (count, plane.shape[-1]), 0) % span_z
+    middle = plane[8:8 + count, :]
+    low = jnp.where(spot == 0, 0.0, plane[7:7 + count, :])
+    high = jnp.where(spot == span_z - 1, 0.0, plane[9:9 + count, :])
+    return [value.astype(jnp.bfloat16) for value in (low, middle, high)]
+
+
+def spread_plane(plane, taps, start, half, span_z):
+    channels = plane.shape[-1]
+    lines = half * span_z
+    for c, value in enumerate(shifts(plane, 2 * lines, span_z)):
+        value = value.reshape(half, 2, span_z, channels)
+        for par in range(2):
+            at = (par * 3 + c) * channels
+            taps[pl.ds(start, lines), at:at + channels] = value[:, par].reshape(lines, channels)
+
+
+def residual_kernel(group, level_ref, w_ref, out_ref, ends_ref, edges_ref,
+                    plane, taps, wide, result):
+    span_x, span_y, span_z, channels = level_ref.shape
+    half = (span_y + 2) // 2
+    lines = half * span_z
+    depth = 6 * channels
     count = (span_y + 2) * span_z
-    plane[0:8, :] = jnp.zeros((8, channels), jnp.float32)
-    plane[8 + count:16 + count, :] = jnp.zeros((8, channels), jnp.float32)
-
-    def spread(x):
-        middle = plane[8:8 + count, :]
-        low = jnp.where(spot == 0, 0.0, plane[7:7 + count, :])
-        high = jnp.where(spot == span_z - 1, 0.0, plane[9:9 + count, :])
-        for c, value in enumerate((low, middle, high)):
-            value = value.astype(jnp.bfloat16).reshape(half, 2, span_z, channels)
-            for par in range(2):
-                taps[pl.ds(pl.multiple_of(x * lines, 16), lines),
-                     par * three + c * channels:par * three + (c + 1) * channels] = (
-                    value[:, par].reshape(lines, channels))
-
-    for x, ref in ((0, xlow_ref), (span_x + 1, xhigh_ref)):
-        plane[8:8 + count, :] = ref[...].reshape(count, channels).astype(jnp.float32)
-        spread(x)
+    join_taps(w_ref, wide, (0, 1, 2))
+    plane[0:8 + span_z, :] = jnp.zeros((8 + span_z, channels), jnp.float32)
+    plane[8 + count - span_z:16 + count, :] = jnp.zeros((8 + span_z, channels), jnp.float32)
+    for x in (0, span_x + 1):
+        taps[x * lines:(x + 1) * lines, :] = jnp.zeros((lines, depth), jnp.bfloat16)
 
     def fill(x, carry):
-        plane[8:8 + span_z, :] = ylow_ref[x].reshape(span_z, channels).astype(jnp.float32)
         plane[8 + span_z:8 + count - span_z, :] = level_ref[x].reshape(
             span_y * span_z, channels).astype(jnp.float32)
-        plane[8 + count - span_z:8 + count, :] = yhigh_ref[x].reshape(
-            span_z, channels).astype(jnp.float32)
-        spread(x + 1)
+        spread_plane(plane, taps, pl.multiple_of((x + 1) * lines, 16), half, span_z)
         return carry
 
     lax.fori_loop(0, span_x, fill, 0)
@@ -236,8 +250,8 @@
         for a in range(3):
             for d in range(2):
                 start = pl.multiple_of((g * group + a) * lines + d * span_z, 16)
-                at = (a * 2 + d) * 2 * three
-                part = jnp.dot(taps[pl.ds(start, height), :], wide[at:at + 2 * three, :],
+                at = (a * 2 + d) * depth
+                part = jnp.dot(taps[pl.ds(start, height), :], wide[at:at + depth, :],
                                preferred_element_type=jnp.float32)
                 total = part if total is None else total + part
         result[0:height, :] = total
@@ -246,24 +260,40 @@
             for s in range(2):
                 value = result[i * lines:i * lines + span_y // 2 * span_z,
                                s * channels:(s + 1) * channels]
-                value = jnp.maximum(value, 0.0).reshape(span_y // 2, span_z, channels)
+                value = value.reshape(span_y // 2, span_z, channels)
+                edges_ref[s, x] = value[s * (span_y // 2 - 1)]
+                if i == 0:
+                    @pl.when(g == 0)
+                    def _():
+                        ends_ref[0, :, s] = value
+
+                if i == group - 1:
+                    @pl.when(x == span_x - 1)
+                    def _():
+                        ends_ref[1, :, s] = value
+
                 here = level_ref[x].reshape(span_y // 2, 2, span_z, channels)[:, s]
-                out_ref[x, :, s] = value + here.astype(jnp.float32)
+                out_ref[x, :, s] = jnp.maximum(value, 0.0) + here.astype(jnp.float32)
         return carry
 
     lax.fori_loop(0, span_x // group, multiply, 0)
 
 
-def residual_base(level, ylow, yhigh, xlow, xhigh, w_res, group=4):
+def residual_base(level, w_res, group=4):
     span_x, span_y, span_z, channels = level.shape
     lines = (span_y + 2) // 2 * span_z
     vm = pl.BlockSpec(memory_space=pltpu.VMEM)
     flops = 2 * span_x * span_y * span_z * 27 * channels * channels
-    out = pl.pallas_call(
+    pairs = (span_y // 2, 2, span_z, channels)
+    return pl.pallas_call(
         functools.partial(residual_kernel, group),
-        out_shape=jax.ShapeDtypeStruct((span_x, span_y // 2, 2, span_z, channels), jnp.float32),
-        in_specs=[vm] * 6,
-        out_specs=vm,
+        out_shape=[
+            jax.ShapeDtypeStruct((span_x,) + pairs, jnp.float32),
+            jax.ShapeDtypeStruct((2,) + pairs, jnp.float32),
+            jax.ShapeDtypeStruct((2, span_x, span_z, channels), jnp.float32),
+        ],
+        in_specs=[vm] * 2,
+        out_specs=[vm] * 3,
         scratch_shapes=[
             pltpu.VMEM(((span_y + 2) * span_z + 16, channels), jnp.float32),
             pltpu.VMEM(((span_x + 2) * lines, 6 * channels), jnp.bfloat16),
@@ -273,8 +303,83 @@
         compiler_params=pltpu.CompilerParams(vmem_limit_bytes=36 * 2**20),
         name="residual",
         cost_estimate=pl.CostEstimate(flops=flops, bytes_accessed=8 * 10**6, transcendentals=0),
-    )(level, ylow, yhigh, xlow, xhigh, w_res)
-    return out.reshape(span_x * span_y * span_z, channels)
+    )(level, w_res)
+
+
+def border_kernel(ends_ref, edges_ref, xfirst_ref, xlast_ref, yfirst_ref, ylast_ref,
+                  xlow_ref, xhigh_ref, ylow_ref, yhigh_ref, ll_ref, lh_ref, hl_ref, hh_ref,
+                  w_ref, new_ends_ref, new_edges_ref, plane, taps, wide):
+    _, half_y, _, span_z, channels = ends_ref.shape
+    span_x = edges_ref.shape[1]
+    span_y = 2 * half_y
+    count = (span_y + 2) * span_z
+    depth = 6 * channels
+    join_taps(w_ref, wide, (0, 2))
+    plane[0:8, :] = jnp.zeros((8, channels), jnp.float32)
+    plane[8 + count:16 + count, :] = jnp.zeros((8, channels), jnp.float32)
+    for k, (low, middle, high) in enumerate(
+            ((ll_ref, xlow_ref, lh_ref), (hl_ref, xhigh_ref, hh_ref))):
+        plane[8:8 + span_z, :] = low[...].reshape(span_z, channels).astype(jnp.float32)
+        plane[8 + span_z:8 + count - span_z, :] = middle[...].reshape(
+            span_y * span_z, channels).astype(jnp.float32)
+        plane[8 + count - span_z:8 + count, :] = high[...].reshape(
+            span_z, channels).astype(jnp.float32)
+        spread_plane(plane, taps, 0, half_y + 1, span_z)
+        change = None
+        for d in range(2):
+            at = (k * 2 + d) * depth
+            part = jnp.dot(taps[d * span_z:(d + half_y) * span_z, :], wide[at:at + depth, :],
+                           preferred_element_type=jnp.float32)
+            change = part if change is None else change + part
+        for s in range(2):
+            value = change[:, s * channels:(s + 1) * channels].reshape(
+                half_y, span_z, channels)
+            new_ends_ref[k, :, s] = ends_ref[k, :, s] + value
+    rows = (span_x + 2) * span_z
+    for k, (source, here) in enumerate(((ylow_ref, yfirst_ref), (yhigh_ref, ylast_ref))):
+        plane[8:8 + span_z, :] = jnp.zeros((span_z, channels), jnp.float32)
+        plane[8 + span_z:8 + rows - span_z, :] = source[...].reshape(
+            span_x * span_z, channels).astype(jnp.float32)
+        plane[8 + rows - span_z:16 + rows, :] = jnp.zeros((span_z + 8, channels), jnp.float32)
+        for c, value in enumerate(shifts(plane, rows, span_z)):
+            taps[0:rows, c * channels:(c + 1) * channels] = value
+        change = None
+        for a in range(3):
+            first = 9 * a + 3 * (2 * k)
+            part = jnp.dot(taps[a * span_z:(a + span_x) * span_z, 0:3 * channels],
+                           w_ref[first:first + 3].reshape(3 * channels, channels),
+                           preferred_element_type=jnp.float32)
+            change = part if change is None else change + part
+        change = change.reshape(span_x, span_z, channels)
+        new_edges_ref[k] = jnp.maximum(edges_ref[k] + change, 0.0) + here[...].reshape(
+            span_x, span_z, channels).astype(jnp.float32)
+        for e, x in ((0, 0), (1, span_x - 1)):
+            new_ends_ref[e, k * (half_y - 1), k] = new_ends_ref[e, k * (half_y - 1), k] + change[x]
+    for e, here in enumerate((xfirst_ref, xlast_ref)):
+        new_ends_ref[e] = jnp.maximum(new_ends_ref[e], 0.0) + here[...].reshape(
+            half_y, 2, span_z, channels).astype(jnp.float32)
+
+
+def border(ends, edges, own, faces, w_res):
+    _, half_y, _, span_z, channels = ends.shape
+    span_x = edges.shape[1]
+    rows = max((half_y + 1), (span_x + 2)) * span_z
+    vm = pl.BlockSpec(memory_space=pltpu.VMEM)
+    return pl.pallas_call(
+        border_kernel,
+        out_shape=[jax.ShapeDtypeStruct(ends.shape, jnp.float32),
+                   jax.ShapeDtypeStruct(edges.shape, jnp.float32)],
+        in_specs=[vm] * 15,
+        out_specs=[vm] * 2,
+        scratch_shapes=[
+            pltpu.VMEM((2 * rows + 16, channels), jnp.float32),
+            pltpu.VMEM((rows, 6 * channels), jnp.bfloat16),
+            pltpu.VMEM((24 * channels, 2 * channels), jnp.bfloat16),
+        ],
+        compiler_params=pltpu.CompilerParams(vmem_limit_bytes=24 * 2**20),
+        name="border",
+        cost_estimate=pl.CostEstimate(flops=10**9, bytes_accessed=3 * 10**6, transcendentals=0),
+    )(ends, edges, *own, *faces, w_res)
 
 
 def lower_kernel(joined_ref, front_ref, side_ref, corner_ref, w_ref, out_ref, plane, taps):
@@ -345,48 +450,56 @@
     )(joined, front, side, corner, w_down.reshape(-1, wide))
 
 
-def pairs_of(axis, by):
-    count = lax.axis_size(axis)
-    return [(i, i + by) for i in range(count) if 0 <= i + by < count]
-
-
-def passed_along(array, axis, by):
-    return lax.ppermute(array, axis, pairs_of(axis, by))
-
-
-def body(points, dest_owner, dest_cell, level_input, w_res, w_down):
+def shifted(array, by_pts, by_nbr):
     count_pts = lax.axis_size("pts")
     count_nbr = lax.axis_size("nbr")
-    devices = count_pts * count_nbr
-    channels = points.shape[-1]
-    rows = points.reshape(-1, channels)
-    capacity = 2 * rows.shape[0] // devices
-    level = level_input
-    low_y = passed_along(level[:, -1:], "pts", 1)
-    high_y = passed_along(level[:, :1], "pts", -1)
-    outgoing = pack(dest_owner.reshape(-1), dest_cell.reshape(-1), rows, devices, capacity)
-    last = jnp.concatenate([low_y[-1:], level[-1:], high_y[-1:]], axis=1)
-    first = jnp.concatenate([low_y[:1], level[:1], high_y[:1]], axis=1)
-    outgoing, last, first = lax.optimization_barrier((outgoing, last, first))
-    low_x = passed_along(last, "nbr", 1)
-    high_x = passed_along(first, "nbr", -1)
+    pairs = [
+        (i * count_nbr + j, (i + by_pts) * count_nbr + j + by_nbr)
+        for i in range(count_pts)
+        for j in range(count_nbr)
+        if 0 <= i + by_pts < count_pts and 0 <= j + by_nbr < count_nbr
+    ]
+    return lax.ppermute(array, ("pts", "nbr"), pairs)
+
+
+def exchanged(array, devices):
     got = lax.all_to_all(
-        outgoing.reshape(devices, capacity + EXTRA, channels),
+        array.reshape(devices, -1, array.shape[-1]),
         ("pts", "nbr"),
         split_axis=0,
         concat_axis=0,
         tiled=True,
-    ).reshape(outgoing.shape)
-    base = residual_base(level, low_y, high_y, low_x, high_x, w_res)
-    joined, front, side, corner = add_rows(got, base, level.shape, capacity)
-    diagonal = [
-        (i * count_nbr + j, (i + 1) * count_nbr + j + 1)
-        for i in range(count_pts - 1)
-        for j in range(count_nbr - 1)
+    )
+    return got.reshape(array.shape)
+
+
+def body(points, dest_owner, dest_cell, level_input, w_res, w_down):
+    devices = lax.axis_size("pts") * lax.axis_size("nbr")
+    channels = points.shape[-1]
+    rows = points.reshape(-1, channels)
+    capacity = 2 * rows.shape[0] // devices
+    outgoing = pack(dest_owner.reshape(-1), dest_cell.reshape(-1), rows, devices, capacity)
+    outgoing, level = lax.optimization_barrier((outgoing, level_input))
+    got = exchanged(outgoing, devices)
+    x_first, x_last = level[:1], level[-1:]
+    y_first, y_last = level[:, :1], level[:, -1:]
+    faces = [
+        shifted(x_last, 0, 1),
+        shifted(x_first, 0, -1),
+        shifted(y_last, 1, 0),
+        shifted(y_first, -1, 0),
+        shifted(level[-1:, -1:], 1, 1),
+        shifted(level[-1:, :1], -1, 1),
+        shifted(level[:1, -1:], 1, -1),
+        shifted(level[:1, :1], -1, -1),
     ]
-    front = passed_along(front, "nbr", 1)
-    side = passed_along(side, "pts", 1)
-    corner = lax.ppermute(corner, ("pts", "nbr"), diagonal)
+    base, ends, edges = residual_base(level, w_res)
+    ends, edges = border(ends, edges, (x_first, x_last, y_first, y_last), faces, w_res)
+    joined, front, side, corner = add_rows(
+        got, base.reshape(-1, channels), ends, edges, level.shape, capacity)
+    front = shifted(front, 0, 1)
+    side = shifted(side, 1, 0)
+    corner = shifted(corner, 1, 1)
     return lower(joined, front, side, corner, w_down)
 
 

time: 103 us -> 121 us (1.17)
  starting transfers between devices: 24.7 us -> 49.5 us
  waiting for transfers between devices: 30.4 us -> 20.7 us
  Pallas kernels: 40.5 us -> 42.4 us
    ppermute x7 -> x11, starting transfers between devices: 19.6 us -> 43.5 us  [shifted(): return lax.ppermute(array, ('pts', 'nbr'), pairs)]
    all_to_all x1, waiting for transfers between devices: 17 us -> 0.01 us  [exchanged(): lax.all_to_all(array.reshape(devices, -1, array.shape[-1]), ('pts', 'nbr'...]
    ppermute x7 -> x11, waiting for transfers between devices: 13.4 us -> 20.7 us  [shifted(): return lax.ppermute(array, ('pts', 'nbr'), pairs)]
    pallas_call x1 -> x2, Pallas kernels: 13 us -> 14.9 us  [the longest x1 13.6 us: residual_base(): pl.pallas_call(functools.partial(residual_kernel, group), out_shape=[jax....]
    slice x4 -> x3, local copies, waits for them, and re-layouts: 1.88 us -> 2.63 us  [the longest x1 0.99 us: body(): x_first, x_last = (level[:1], level[-1:])]
    unnamed x8 -> x10, local copies, waits for them, and re-layouts: 3.55 us -> 3.53 us
  transfers between devices with their start and end apart: 8 -> 12, of which waited for: 3 -> 3; matrix products, arithmetic and copies ran while one was open for 1% -> 2% of each run, Pallas kernels for 22% -> 13%
where the time goes in v4:
time: 121 us; the launch traced here: 119 us
  starting transfers between devices  49.5 us (41%)
  Pallas kernels  42.4 us (35%)
  waiting for transfers between devices  20.7 us (17%)
  local copies, waits for them, and re-layouts  6.15 us (5%)
    ppermute x11, starting transfers between devices, shifted(): return lax.ppermute(array, ('pts', 'nbr'), pairs)  43.5 us
    ppermute x11, waiting for transfers between devices, shifted(): return lax.ppermute(array, ('pts', 'nbr'), pairs)  20.7 us
    pallas_call x1, Pallas kernels, residual_base(): pl.pallas_call(functools.partial(residual_kernel, group), out_shape=[jax....  13.6 us
    pallas_call x1, Pallas kernels, add_rows(): pl.pallas_call(functools.partial(add_kernel, capacity), out_shape=[jax.Sh...  13.1 us
    pallas_call x1, Pallas kernels, pack(): pl.pallas_call(functools.partial(pack_kernel, devices, cap), out_shape=ja...  9.17 us
    all_to_all x1, starting transfers between devices, exchanged(): lax.all_to_all(array.reshape(devices, -1, array.shape[-1]), ('pts', 'nbr'...  6 us
    pallas_call x1, Pallas kernels, lower(): pl.pallas_call(lower_kernel, out_shape=jax.ShapeDtypeStruct((span_x // 2,...  5.29 us
    unnamed x10, local copies, waits for them, and re-layouts  3.53 us
  transfers between devices with their start and end apart: 12, of which 3 were waited for; matrix products, arithmetic and copies ran while one was open for 2% of the time, Pallas kernels for 13%

profile of v4, /device:TPU:12, one launch (start us, length us, event | category | flops | bytes accessed | tf_op | source)
XLA Modules:
  0.0 119.1 jit_solution(7722950178275200179)
XLA Ops:
  0.0 9.2 %pack.1 = bf16[8448,128]{1,0:T(8,128)(2,1)} custom-call(s32[32,128]{1,0:T(8,128)} %bitcast.12, s32[32,128]{1,0:T(8,128)} %bitcast.13, bf16[4096,128]{1,0:T(8,128)(2,1)} %bitcast.11), custom_call_target="tpu_custom_call" | custom-call | flops 100000000 | bytes 4000000 | tf_op jit(solution)/shard_map/pack/pallas_call | solution.py:68
  9.2 0.0 copy-start.3
  9.2 6.0 %all-to-all-start = ((bf16[32,264,128]{2,1,0:T(8,128)(2,1)}), bf16[32,264,128]{2,1,0:T(8,128)(2,1)S(1)}, u32[]{:S(2)}, u32[]{:S(2)}) async-start(bf16[32,264,128]{2,1,0:T(8,128)(2,1)} %bitcast.10), calls=%async_computation | async-start | bytes 4325376 | tf_op jit(solution)/shard_map/all_to_all | solution.py:466
  15.2 0.7 fusion
  15.9 3.1 %collective-permute-start.7 = (bf16[1,1,16,128]{3,2,1,0:T(8,128)(2,1)S(1)}, bf16[1,1,16,128]{3,2,1,0:T(8,128)(2,1)S(1)}, u32[]{:S(2)}, u32[]{:S(2)}) collective-permute-start(bf16[1,1,16,128]{3,2,1,0:T(8,128)(2,1)S(1)} %get-tuple-element.27), channel_id=1, source_target_pairs={{5,0},{6,1},{7,2},{9,4},{10,5},{11,6},{13,8},{14,9},{15,10},{17,12... | collective-permute-start | bytes 12296 | tf_op jit(solution)/shard_map/ppermute | solution.py:462
  19.0 2.5 %collective-permute-start.6 = (bf16[1,1,16,128]{3,2,1,0:T(8,128)(2,1)S(1)}, bf16[1,1,16,128]{3,2,1,0:T(8,128)(2,1)S(1)}, u32[]{:S(2)}, u32[]{:S(2)}) collective-permute-start(bf16[1,1,16,128]{3,2,1,0:T(8,128)(2,1)S(1)} %get-tuple-element.28), channel_id=1, source_target_pairs={{1,4},{2,5},{3,6},{5,8},{6,9},{7,10},{9,12},{10,13},{11,14},{13,16... | collective-permute-start | bytes 12296 | tf_op jit(solution)/shard_map/ppermute | solution.py:462
  21.5 4.0 %collective-permute-start.5 = (bf16[1,1,16,128]{3,2,1,0:T(8,128)(2,1)S(1)}, bf16[1,1,16,128]{3,2,1,0:T(8,128)(2,1)S(1)}, u32[]{:S(2)}, u32[]{:S(2)}) collective-permute-start(bf16[1,1,16,128]{3,2,1,0:T(8,128)(2,1)S(1)} %get-tuple-element.29), channel_id=1, source_target_pairs={{4,1},{5,2},{6,3},{8,5},{9,6},{10,7},{12,9},{13,10},{14,11},{16,13... | collective-permute-start | bytes 12296 | tf_op jit(solution)/shard_map/ppermute | solution.py:462
  25.5 1.9 %collective-permute-start.4 = (bf16[1,1,16,128]{3,2,1,0:T(8,128)(2,1)S(1)}, bf16[1,1,16,128]{3,2,1,0:T(8,128)(2,1)S(1)}, u32[]{:S(2)}, u32[]{:S(2)}) collective-permute-start(bf16[1,1,16,128]{3,2,1,0:T(8,128)(2,1)S(1)} %get-tuple-element.30), channel_id=1, source_target_pairs={{0,5},{1,6},{2,7},{4,9},{5,10},{6,11},{8,13},{9,14},{10,15},{12,17... | collective-permute-start | bytes 12296 | tf_op jit(solution)/shard_map/ppermute | solution.py:462
  27.4 0.9 fusion.1
  28.3 2.2 %collective-permute-start.2 = (bf16[16,1,16,128]{3,2,1,0:T(8,128)(2,1)S(1)}, bf16[16,1,16,128]{3,2,1,0:T(8,128)(2,1)S(1)}, u32[]{:S(2)}, u32[]{:S(2)}) collective-permute-start(bf16[16,1,16,128]{3,2,1,0:T(8,128)(2,1)S(1)} %get-tuple-element.31.ylast_ref), channel_id=1, source_target_pairs={{0,4},{1,5},{2,6},{3,7},{4,8},{5,9},{6,10},{7,11},{8,12},{9,13},{1... | collective-permute-start | bytes 196616 | tf_op jit(solution)/shard_map/ppermute | solution.py:462
  30.5 1.0 fusion.2
  31.5 7.3 %collective-permute-done.7.hh_ref = bf16[1,1,16,128]{3,2,1,0:T(8,128)(2,1)S(1)} collective-permute-done((bf16[1,1,16,128]{3,2,1,0:T(8,128)(2,1)S(1)}, bf16[1,1,16,128]{3,2,1,0:T(8,128)(2,1)S(1)}, u32[]{:S(2)}, u32[]{:S(2)}) %collective-permute-start.7) | collective-permute-done | bytes 4128 | tf_op jit(solution)/shard_map/ppermute | solution.py:462
  38.8 4.5 %collective-permute-start.3 = (bf16[16,1,16,128]{3,2,1,0:T(8,128)(2,1)S(1)}, bf16[16,1,16,128]{3,2,1,0:T(8,128)(2,1)S(1)}, u32[]{:S(2)}, u32[]{:S(2)}) collective-permute-start(bf16[16,1,16,128]{3,2,1,0:T(8,128)(2,1)S(1)} %get-tuple-element.32.yfirst_ref), channel_id=1, source_target_pairs={{4,0},{5,1},{6,2},{7,3},{8,4},{9,5},{10,6},{11,7},{12,8},{13,9},{1... | collective-permute-start | bytes 196616 | tf_op jit(solution)/shard_map/ppermute | solution.py:462
  43.3 8.8 %collective-permute-done.6.hl_ref = bf16[1,1,16,128]{3,2,1,0:T(8,128)(2,1)S(1)} collective-permute-done((bf16[1,1,16,128]{3,2,1,0:T(8,128)(2,1)S(1)}, bf16[1,1,16,128]{3,2,1,0:T(8,128)(2,1)S(1)}, u32[]{:S(2)}, u32[]{:S(2)}) %collective-permute-start.6) | collective-permute-done | bytes 4128 | tf_op jit(solution)/shard_map/ppermute | solution.py:462
  52.1 1.9 %collective-permute-start = (bf16[1,32,16,128]{3,2,1,0:T(8,128)(2,1)S(1)}, bf16[1,32,16,128]{3,2,1,0:T(8,128)(2,1)S(1)}, u32[]{:S(2)}, u32[]{:S(2)}) collective-permute-start(bf16[1,32,16,128]{3,2,1,0:T(8,128)(2,1)S(1)} %get-tuple-element.33.xlast_ref), channel_id=1, source_target_pairs={{0,1},{1,2},{2,3},{4,5},{5,6},{6,7},{8,9},{9,10},{10,11},{12,13},{... | collective-permute-start | bytes 393224 | tf_op jit(solution)/shard_map/ppermute | solution.py:462
  54.0 0.0 collective-permute-done.5.lh_ref
  54.1 3.9 %collective-permute-start.1 = (bf16[1,32,16,128]{3,2,1,0:T(8,128)(2,1)S(1)}, bf16[1,32,16,128]{3,2,1,0:T(8,128)(2,1)S(1)}, u32[]{:S(2)}, u32[]{:S(2)}) collective-permute-start(bf16[1,32,16,128]{3,2,1,0:T(8,128)(2,1)S(1)} %get-tuple-element.34.xfirst_ref), channel_id=1, source_target_pairs={{1,0},{2,1},{3,2},{5,4},{6,5},{7,6},{9,8},{10,9},{11,10},{13,12},{... | collective-permute-start | bytes 393224 | tf_op jit(solution)/shard_map/ppermute | solution.py:462
  58.0 0.0 copy-start.1
  58.0 1.6 %copy-done.1 = bf16[16,32,16,128]{3,2,1,0:T(8,128)(2,1)S(1)} copy-done((bf16[16,32,16,128]{3,2,1,0:T(8,128)(2,1)S(1)}, bf16[16,32,16,128]{3,2,1,0:T(8,128)(2,1)}, u32[]{:S(2)}) %copy-start.1) | copy-done | bytes 2097176
  59.6 13.6 %residual.1 = (f32[16,16,2,16,128]{4,3,2,1,0:T(8,128)S(1)}, f32[2,16,2,16,128]{4,3,2,1,0:T(8,128)S(1)}, f32[2,16,16,128]{3,2,1,0:T(8,128)S(1)}) custom-call(bf16[16,32,16,128]{3,2,1,0:T(8,128)(2,1)S(1)} %copy-done.1, bf16[27,128,128]{2,1,0:T(8,128)(2,1)S(1)} %copy-done.3), custom_call_target="tpu_custom_call" | custom-call | flops 7247757312 | bytes 8000000 | tf_op jit(solution)/shard_map/residual/pallas_call | solution.py:288
  73.2 1.9 %copy-done = f32[16,16,2,16,128]{4,3,2,1,0:T(8,128)} copy-done((f32[16,16,2,16,128]{4,3,2,1,0:T(8,128)}, f32[16,16,2,16,128]{4,3,2,1,0:T(8,128)S(1)}, u32[]{:S(2)}) %copy-start) | copy-done | bytes 4194328
  75.2 0.0 collective-permute-done.4.ll_ref
  75.2 0.0 collective-permute-done.2.ylow_ref
  75.2 0.0 collective-permute-done.3.yhigh_ref
  75.2 1.3 %border.1 = (f32[2,16,2,16,128]{4,3,2,1,0:T(8,128)S(1)}, f32[2,16,16,128]{3,2,1,0:T(8,128)S(1)}) custom-call(f32[2,16,2,16,128]{4,3,2,1,0:T(8,128)S(1)} %get-tuple-element.19.ends_ref, f32[2,16,16,128]{3,2,1,0:T(8,128)S(1)} %get-tuple-element.20.edges_ref, bf16[1,32,16,128]{3,2,1,0:T(8,128)(2,1)S(1)} %get-tuple-element.34.xfirst_ref, ...), custom_call_target="tpu_custom_call" | custom-call | flops 1000000000 | bytes 3000000 | tf_op jit(solution)/shard_map/border/pallas_call | solution.py:368
  76.5 0.0 copy-start.2
  76.5 13.1 %add_rows.1 = (bf16[16,32,16,128]{3,2,1,0:T(8,128)(2,1)S(1)}, bf16[1,32,16,128]{3,2,1,0:T(8,128)(2,1)S(1)}, bf16[16,1,16,128]{3,2,1,0:T(8,128)(2,1)S(1)}, bf16[1,1,16,128]{3,2,1,0:T(8,128)(2,1)S(1)}) custom-call(bf16[8448,128]{1,0:T(8,128)(2,1)S(1)} %bitcast.7, f32[8192,128]{1,0:T(8,128)} %bitcast.8, f32[2,16,2,16,128]{4,3,2,1,0:T(8,128)S(1)} %get-tuple-element.21.ends_ref, ...), custom_call_target="tpu_custom_call" | custom-call | flops 100000000 | bytes 8000000 | tf_op jit(solution)/shard_map/add_rows/pallas_call | solution.py:169
  89.6 1.9 %collective-permute-start.8 = (bf16[1,32,16,128]{3,2,1,0:T(8,128)(2,1)S(1)}, bf16[1,32,16,128]{3,2,1,0:T(8,128)(2,1)S(1)}, u32[]{:S(2)}, u32[]{:S(2)}) collective-permute-start(bf16[1,32,16,128]{3,2,1,0:T(8,128)(2,1)S(1)} %get-tuple-element.24), channel_id=1, source_target_pairs={{0,1},{1,2},{2,3},{4,5},{5,6},{6,7},{8,9},{9,10},{10,11},{12,13},{... | collective-permute-start | bytes 393224 | tf_op jit(solution)/shard_map/ppermute | solution.py:462
  91.5 15.5 %collective-permute-start.9 = (bf16[16,1,16,128]{3,2,1,0:T(8,128)(2,1)S(1)}, bf16[16,1,16,128]{3,2,1,0:T(8,128)(2,1)S(1)}, u32[]{:S(2)}, u32[]{:S(2)}) collective-permute-start(bf16[16,1,16,128]{3,2,1,0:T(8,128)(2,1)S(1)} %get-tuple-element.25), channel_id=1, source_target_pairs={{0,4},{1,5},{2,6},{3,7},{4,8},{5,9},{6,10},{7,11},{8,12},{9,13},{1... | collective-permute-start | bytes 196616 | tf_op jit(solution)/shard_map/ppermute | solution.py:462
  107.1 2.1 %collective-permute-start.10 = (bf16[1,1,16,128]{3,2,1,0:T(8,128)(2,1)S(1)}, bf16[1,1,16,128]{3,2,1,0:T(8,128)(2,1)S(1)}, u32[]{:S(2)}, u32[]{:S(2)}) collective-permute-start(bf16[1,1,16,128]{3,2,1,0:T(8,128)(2,1)S(1)} %get-tuple-element.26), channel_id=1, source_target_pairs={{0,5},{1,6},{2,7},{4,9},{5,10},{6,11},{8,13},{9,14},{10,15},{12,17... | collective-permute-start | bytes 12296 | tf_op jit(solution)/shard_map/ppermute | solution.py:462
  109.2 4.6 %collective-permute-done.10.corner_ref = bf16[1,1,16,128]{3,2,1,0:T(8,128)(2,1)S(1)} collective-permute-done((bf16[1,1,16,128]{3,2,1,0:T(8,128)(2,1)S(1)}, bf16[1,1,16,128]{3,2,1,0:T(8,128)(2,1)S(1)}, u32[]{:S(2)}, u32[]{:S(2)}) %collective-permute-start.10) | collective-permute-done | bytes 4128 | tf_op jit(solution)/shard_map/ppermute | solution.py:462
  113.8 5.3 %lower.1 = bf16[8,16,8,256]{3,2,1,0:T(8,128)(2,1)} custom-call(bf16[16,32,16,128]{3,2,1,0:T(8,128)(2,1)S(1)} %get-tuple-element.23.joined_ref, bf16[1,32,16,128]{3,2,1,0:T(8,128)(2,1)S(1)} %collective-permute-done.8.front_ref, bf16[16,1,16,128]{3,2,1,0:T(8,128)(2,1)S(1)} %collective-permute-done.9.side_ref, ...), custom_call_target="tpu_custom_call" | custom-call | flops 1811939328 | bytes 5000000 | tf_op jit(solution)/shard_map/lower/pallas_call | solution.py:437
  (10 shorter events, 0.0 us)
Async XLA Ops:
  9.2 48.8 %copy-start.3 = (bf16[27,128,128]{2,1,0:T(8,128)(2,1)S(1)}, bf16[27,128,128]{2,1,0:T(8,128)(2,1)}, u32[]{:S(2)}) copy-start(bf16[27,128,128]{2,1,0:T(8,128)(2,1)} %w_ref.3) | copy-start | bytes 2654212
  9.2 67.3 %all-to-all-start = ((bf16[32,264,128]{2,1,0:T(8,128)(2,1)}), bf16[32,264,128]{2,1,0:T(8,128)(2,1)S(1)}, u32[]{:S(2)}, u32[]{:S(2)}) async-start(bf16[32,264,128]{2,1,0:T(8,128)(2,1)} %bitcast.10), calls=%async_computation | async-start | bytes 4325376 | tf_op jit(solution)/shard_map/all_to_all | solution.py:466
  15.9 22.9 %collective-permute-start.7 = (bf16[1,1,16,128]{3,2,1,0:T(8,128)(2,1)S(1)}, bf16[1,1,16,128]{3,2,1,0:T(8,128)(2,1)S(1)}, u32[]{:S(2)}, u32[]{:S(2)}) collective-permute-start(bf16[1,1,16,128]{3,2,1,0:T(8,128)(2,1)S(1)} %get-tuple-element.27), channel_id=1, source_target_pairs={{5,0},{6,1},{7,2},{9,4},{10,5},{11,6},{13,8},{14,9},{15,10},{17,12... | collective-permute-start | bytes 12296 | tf_op jit(solution)/shard_map/ppermute | solution.py:462
  19.0 33.1 %collective-permute-start.6 = (bf16[1,1,16,128]{3,2,1,0:T(8,128)(2,1)S(1)}, bf16[1,1,16,128]{3,2,1,0:T(8,128)(2,1)S(1)}, u32[]{:S(2)}, u32[]{:S(2)}) collective-permute-start(bf16[1,1,16,128]{3,2,1,0:T(8,128)(2,1)S(1)} %get-tuple-element.28), channel_id=1, source_target_pairs={{1,4},{2,5},{3,6},{5,8},{6,9},{7,10},{9,12},{10,13},{11,14},{13,16... | collective-permute-start | bytes 12296 | tf_op jit(solution)/shard_map/ppermute | solution.py:462
  21.5 32.5 %collective-permute-start.5 = (bf16[1,1,16,128]{3,2,1,0:T(8,128)(2,1)S(1)}, bf16[1,1,16,128]{3,2,1,0:T(8,128)(2,1)S(1)}, u32[]{:S(2)}, u32[]{:S(2)}) collective-permute-start(bf16[1,1,16,128]{3,2,1,0:T(8,128)(2,1)S(1)} %get-tuple-element.29), channel_id=1, source_target_pairs={{4,1},{5,2},{6,3},{8,5},{9,6},{10,7},{12,9},{13,10},{14,11},{16,13... | collective-permute-start | bytes 12296 | tf_op jit(solution)/shard_map/ppermute | solution.py:462
  25.5 49.7 %collective-permute-start.4 = (bf16[1,1,16,128]{3,2,1,0:T(8,128)(2,1)S(1)}, bf16[1,1,16,128]{3,2,1,0:T(8,128)(2,1)S(1)}, u32[]{:S(2)}, u32[]{:S(2)}) collective-permute-start(bf16[1,1,16,128]{3,2,1,0:T(8,128)(2,1)S(1)} %get-tuple-element.30), channel_id=1, source_target_pairs={{0,5},{1,6},{2,7},{4,9},{5,10},{6,11},{8,13},{9,14},{10,15},{12,17... | collective-permute-start | bytes 12296 | tf_op jit(solution)/shard_map/ppermute | solution.py:462
  28.3 46.9 %collective-permute-start.2 = (bf16[16,1,16,128]{3,2,1,0:T(8,128)(2,1)S(1)}, bf16[16,1,16,128]{3,2,1,0:T(8,128)(2,1)S(1)}, u32[]{:S(2)}, u32[]{:S(2)}) collective-permute-start(bf16[16,1,16,128]{3,2,1,0:T(8,128)(2,1)S(1)} %get-tuple-element.31.ylast_ref), channel_id=1, source_target_pairs={{0,4},{1,5},{2,6},{3,7},{4,8},{5,9},{6,10},{7,11},{8,12},{9,13},{1... | collective-permute-start | bytes 196616 | tf_op jit(solution)/shard_map/ppermute | solution.py:462
  38.8 36.4 %collective-permute-start.3 = (bf16[16,1,16,128]{3,2,1,0:T(8,128)(2,1)S(1)}, bf16[16,1,16,128]{3,2,1,0:T(8,128)(2,1)S(1)}, u32[]{:S(2)}, u32[]{:S(2)}) collective-permute-start(bf16[16,1,16,128]{3,2,1,0:T(8,128)(2,1)S(1)} %get-tuple-element.32.yfirst_ref), channel_id=1, source_target_pairs={{4,0},{5,1},{6,2},{7,3},{8,4},{9,5},{10,6},{11,7},{12,8},{13,9},{1... | collective-permute-start | bytes 196616 | tf_op jit(solution)/shard_map/ppermute | solution.py:462
  52.1 23.1 %collective-permute-start = (bf16[1,32,16,128]{3,2,1,0:T(8,128)(2,1)S(1)}, bf16[1,32,16,128]{3,2,1,0:T(8,128)(2,1)S(1)}, u32[]{:S(2)}, u32[]{:S(2)}) collective-permute-start(bf16[1,32,16,128]{3,2,1,0:T(8,128)(2,1)S(1)} %get-tuple-element.33.xlast_ref), channel_id=1, source_target_pairs={{0,1},{1,2},{2,3},{4,5},{5,6},{6,7},{8,9},{9,10},{10,11},{12,13},{... | collective-permute-start | bytes 393224 | tf_op jit(solution)/shard_map/ppermute | solution.py:462
  54.1 21.1 %collective-permute-start.1 = (bf16[1,32,16,128]{3,2,1,0:T(8,128)(2,1)S(1)}, bf16[1,32,16,128]{3,2,1,0:T(8,128)(2,1)S(1)}, u32[]{:S(2)}, u32[]{:S(2)}) collective-permute-start(bf16[1,32,16,128]{3,2,1,0:T(8,128)(2,1)S(1)} %get-tuple-element.34.xfirst_ref), channel_id=1, source_target_pairs={{1,0},{2,1},{3,2},{5,4},{6,5},{7,6},{9,8},{10,9},{11,10},{13,12},{... | collective-permute-start | bytes 393224 | tf_op jit(solution)/shard_map/ppermute | solution.py:462
  58.0 1.6 %copy-start.1 = (bf16[16,32,16,128]{3,2,1,0:T(8,128)(2,1)S(1)}, bf16[16,32,16,128]{3,2,1,0:T(8,128)(2,1)}, u32[]{:S(2)}) copy-start(bf16[16,32,16,128]{3,2,1,0:T(8,128)(2,1)} %level_ref) | copy-start | bytes 6291460
  59.6 15.6 %copy-start.4 = (bf16[27,128,128]{2,1,0:T(8,128)(2,1)S(1)}, bf16[27,128,128]{2,1,0:T(8,128)(2,1)}, u32[]{:S(2)}) copy-start(bf16[27,128,128]{2,1,0:T(8,128)(2,1)} %w_ref.3) | copy-start | bytes 2654212
  73.2 1.9 %copy-start = (f32[16,16,2,16,128]{4,3,2,1,0:T(8,128)}, f32[16,16,2,16,128]{4,3,2,1,0:T(8,128)S(1)}, u32[]{:S(2)}) copy-start(f32[16,16,2,16,128]{4,3,2,1,0:T(8,128)S(1)} %get-tuple-element.18) | copy-start | bytes 12582916
  76.5 37.3 %copy-start.2 = (bf16[27,128,256]{2,1,0:T(8,128)(2,1)S(1)}, bf16[27,128,256]{2,1,0:T(8,128)(2,1)}, u32[]{:S(2)}) copy-start(bf16[27,128,256]{2,1,0:T(8,128)(2,1)} %param.11) | copy-start | bytes 5308420
  89.6 24.2 %collective-permute-start.8 = (bf16[1,32,16,128]{3,2,1,0:T(8,128)(2,1)S(1)}, bf16[1,32,16,128]{3,2,1,0:T(8,128)(2,1)S(1)}, u32[]{:S(2)}, u32[]{:S(2)}) collective-permute-start(bf16[1,32,16,128]{3,2,1,0:T(8,128)(2,1)S(1)} %get-tuple-element.24), channel_id=1, source_target_pairs={{0,1},{1,2},{2,3},{4,5},{5,6},{6,7},{8,9},{9,10},{10,11},{12,13},{... | collective-permute-start | bytes 393224 | tf_op jit(solution)/shard_map/ppermute | solution.py:462
  91.5 22.2 %collective-permute-start.9 = (bf16[16,1,16,128]{3,2,1,0:T(8,128)(2,1)S(1)}, bf16[16,1,16,128]{3,2,1,0:T(8,128)(2,1)S(1)}, u32[]{:S(2)}, u32[]{:S(2)}) collective-permute-start(bf16[16,1,16,128]{3,2,1,0:T(8,128)(2,1)S(1)} %get-tuple-element.25), channel_id=1, source_target_pairs={{0,4},{1,5},{2,6},{3,7},{4,8},{5,9},{6,10},{7,11},{8,12},{9,13},{1... | collective-permute-start | bytes 196616 | tf_op jit(solution)/shard_map/ppermute | solution.py:462
  107.1 6.7 %collective-permute-start.10 = (bf16[1,1,16,128]{3,2,1,0:T(8,128)(2,1)S(1)}, bf16[1,1,16,128]{3,2,1,0:T(8,128)(2,1)S(1)}, u32[]{:S(2)}, u32[]{:S(2)}) collective-permute-start(bf16[1,1,16,128]{3,2,1,0:T(8,128)(2,1)S(1)} %get-tuple-element.26), channel_id=1, source_target_pairs={{0,5},{1,6},{2,7},{4,9},{5,10},{6,11},{8,13},{9,14},{10,15},{12,17... | collective-permute-start | bytes 12296 | tf_op jit(solution)/shard_map/ppermute | solution.py:462

commit v5 on v4

--- a/solution.py
+++ b/solution.py
@@ -9,11 +9,14 @@
 
 LANES = 128
 EXTRA = 8
-
-
-def pack_kernel(devices, cap, owner_ref, cell_ref, rows_ref, out_ref,
-                wide, spread, slot_vmem, slot_smem, sem):
+PIECES = 4
+
+
+def pack_kernel(devices, cap, owner_ref, cell_ref, rows_hbm, out_hbm,
+                rows_ref, wide, spread, staged, slot_vmem, slot_smem, sems):
     p_local, _ = rows_ref.shape
+    fetch = pltpu.make_async_copy(rows_hbm, rows_ref, sems.at[PIECES + 1])
+    fetch.start()
     blocks = p_local // LANES
     stride = cap + EXTRA
     upper = (lax.broadcasted_iota(jnp.int32, (LANES, LANES), 0)
@@ -37,8 +40,9 @@
         right = (spots == place).astype(jnp.float32).astype(jnp.bfloat16)
         table = table + lax.dot_general(left, right, (((1,), (1,)), ((), ())),
                                         preferred_element_type=jnp.float32)
-    copy = pltpu.make_async_copy(slot_vmem, slot_smem, sem)
+    copy = pltpu.make_async_copy(slot_vmem, slot_smem, sems.at[PIECES])
     copy.start()
+    fetch.wait()
     wide[...] = rows_ref[...].astype(jnp.float32)
     per = -(-cap // LANES)
     for part in range(2):
@@ -57,7 +61,15 @@
         return carry
 
     lax.fori_loop(0, blocks, step, 0)
-    out_ref[...] = spread[...].astype(jnp.bfloat16)
+    piece = staged.shape[0] // PIECES
+    sends = []
+    for i in range(PIECES):
+        part = pl.ds(i * piece, piece)
+        staged[part, :] = spread[part, :].astype(jnp.bfloat16)
+        sends.append(pltpu.make_async_copy(staged.at[part], out_hbm.at[part], sems.at[i]))
+        sends[-1].start()
+    for send in sends:
+        send.wait()
 
 
 def pack(owner, cell, rows, devices, cap):
@@ -65,17 +77,20 @@
     blocks = p_local // LANES
     total = devices * (cap + EXTRA)
     vm = pl.BlockSpec(memory_space=pltpu.VMEM)
+    hbm = pl.BlockSpec(memory_space=pl.ANY)
     return pl.pallas_call(
         functools.partial(pack_kernel, devices, cap),
         out_shape=jax.ShapeDtypeStruct((total, channels), jnp.bfloat16),
-        in_specs=[vm, vm, vm],
-        out_specs=vm,
+        in_specs=[vm, vm, hbm],
+        out_specs=hbm,
         scratch_shapes=[
+            pltpu.VMEM((p_local, channels), jnp.bfloat16),
             pltpu.VMEM((p_local, channels), jnp.float32),
             pltpu.VMEM((total, channels), jnp.float32),
+            pltpu.VMEM((total, channels), jnp.bfloat16),
             pltpu.VMEM((blocks, LANES), jnp.int32),
             pltpu.SMEM((blocks, LANES), jnp.int32),
-            pltpu.SemaphoreType.DMA,
+            pltpu.SemaphoreType.DMA((PIECES + 2,)),
         ],
         name="pack",
         cost_estimate=pl.CostEstimate(flops=10**8, bytes_accessed=4 * 10**6, transcendentals=0),
@@ -83,55 +98,37 @@
 
 
 WAYS = 6
-PIECES = 4
-LIMIT = 48 * 2**20
-
-
-def add_kernel(capacity, got_hbm, base_hbm, ends_ref, edges_ref, out_ref, front_ref, side_ref, corner_ref,
-               landed, wide, slot_vmem, slot_smem, sems, *sums):
+
+
+def add_kernel(capacity, got_ref, base_hbm, ends_ref, edges_ref, out_ref, front_ref, side_ref,
+               corner_ref, wide, slot_vmem, slot_smem, sems, *sums):
     span_x, span_y, span_z, channels = out_ref.shape
     cells = span_x * span_y * span_z
-    total, _ = landed.shape
+    total, _ = got_ref.shape
     stride = capacity + EXTRA
     devices = total // stride
     per = -(-capacity // LANES)
     width = min(LANES, capacity)
-    piece = total // PIECES
-    copies = [
-        pltpu.make_async_copy(got_hbm.at[pl.ds(i * piece, piece)],
-                              landed.at[pl.ds(i * piece, piece)], sems.at[i])
-        for i in range(PIECES)
-    ]
-    for copy in copies:
-        copy.start()
-    first = pltpu.make_async_copy(base_hbm, sums[0].at[pl.ds(0, cells)], sems.at[PIECES])
+    area = span_y * span_z
+    first = pltpu.make_async_copy(base_hbm, sums[0].at[pl.ds(0, cells)], sems.at[0])
     first.start()
-    half = len(sums) // 2
-    for s in sums[1:half]:
-        s[...] = jnp.zeros_like(s)
-    for i, copy in enumerate(copies):
-        copy.wait()
-        wide[i * piece:(i + 1) * piece, :] = landed[i * piece:(i + 1) * piece, :].astype(
-            jnp.float32)
+    wide[...] = got_ref[...].astype(jnp.float32)
     for j in range(per):
         high = wide[pl.ds(capacity + j, devices, stride=stride), :].astype(jnp.int32)
         low = wide[pl.ds(capacity + per + j, devices, stride=stride), :].astype(jnp.int32)
         slot_vmem[j * devices:(j + 1) * devices, :] = jnp.where(
             high > 0, (high - 1) * LANES + low, cells)
-    copy = pltpu.make_async_copy(slot_vmem, slot_smem, sems.at[PIECES + 1])
+    copy = pltpu.make_async_copy(slot_vmem, slot_smem, sems.at[1])
     copy.start()
-    for s in sums[max(half, 1):]:
+    for s in sums[1:]:
         s[...] = jnp.zeros_like(s)
+    first.wait()
+    for x in range(span_x):
+        sums[0][x * area:x * area + span_z, :] = edges_ref[0, x]
+        sums[0][(x + 1) * area - span_z:(x + 1) * area, :] = edges_ref[1, x]
+    for k, x in ((0, 0), (1, span_x - 1)):
+        sums[0][x * area:(x + 1) * area, :] = ends_ref[k].reshape(area, channels)
     copy.wait()
-    first.wait()
-    for i in range(span_x):
-        for k, y in ((0, 0), (1, span_y - 1)):
-            start = (i * span_y + y) * span_z
-            sums[0][start:start + span_z, :] = edges_ref[k, i]
-    for k, x in ((0, 0), (1, span_x - 1)):
-        start = x * span_y * span_z
-        sums[0][start:start + span_y * span_z, :] = ends_ref[k].reshape(
-            span_y * span_z, channels)
     for j in range(per):
         def step(o, carry):
             start = pl.multiple_of(o * stride + j * LANES, 8)
@@ -144,7 +141,7 @@
         lax.fori_loop(0, devices, step, 0)
 
     def finish(x, carry):
-        at = pl.ds(pl.multiple_of(x * (span_y * span_z), 8), span_y * span_z)
+        at = pl.ds(pl.multiple_of(x * area, 8), area)
         value = sums[0][at, :]
         for s in sums[1:]:
             value = value + s[at, :]
@@ -165,7 +162,6 @@
     devices = total // (capacity + EXTRA)
     per = -(-capacity // LANES)
     vm = pl.BlockSpec(memory_space=pltpu.VMEM)
-    hbm = pl.BlockSpec(memory_space=pl.ANY)
     return pl.pallas_call(
         functools.partial(add_kernel, capacity),
         out_shape=[
@@ -174,19 +170,21 @@
             jax.ShapeDtypeStruct((span_x, 1, span_z, channels), jnp.bfloat16),
             jax.ShapeDtypeStruct((1, 1, span_z, channels), jnp.bfloat16),
         ],
-        in_specs=[hbm, hbm, vm, vm],
+        in_specs=[vm, pl.BlockSpec(memory_space=pl.ANY), vm, vm],
         out_specs=[vm] * 4,
         scratch_shapes=[
-            pltpu.VMEM((total, channels), jnp.bfloat16),
             pltpu.VMEM((total, channels), jnp.float32),
             pltpu.VMEM((devices * per, LANES), jnp.int32),
             pltpu.SMEM((devices * per, LANES), jnp.int32),
-            pltpu.SemaphoreType.DMA((PIECES + 2,)),
+            pltpu.SemaphoreType.DMA((2,)),
         ] + [pltpu.VMEM((cells + 8, channels), jnp.float32)] * WAYS,
         compiler_params=pltpu.CompilerParams(vmem_limit_bytes=LIMIT),
         name="add_rows",
         cost_estimate=pl.CostEstimate(flops=10**8, bytes_accessed=8 * 10**6, transcendentals=0),
     )(got, base, ends, edges)
+
+
+LIMIT = 48 * 2**20
 
 
 def join_taps(w_ref, wide, rows):
@@ -300,7 +298,7 @@
             pltpu.VMEM((36 * channels, 2 * channels), jnp.bfloat16),
             pltpu.VMEM((group * lines, 2 * channels), jnp.float32),
         ],
-        compiler_params=pltpu.CompilerParams(vmem_limit_bytes=36 * 2**20),
+        compiler_params=pltpu.CompilerParams(vmem_limit_bytes=26 * 2**20),
         name="residual",
         cost_estimate=pl.CostEstimate(flops=flops, bytes_accessed=8 * 10**6, transcendentals=0),
     )(level, w_res)
@@ -376,22 +374,28 @@
             pltpu.VMEM((rows, 6 * channels), jnp.bfloat16),
             pltpu.VMEM((24 * channels, 2 * channels), jnp.bfloat16),
         ],
-        compiler_params=pltpu.CompilerParams(vmem_limit_bytes=24 * 2**20),
+        compiler_params=pltpu.CompilerParams(vmem_limit_bytes=8 * 2**20),
         name="border",
         cost_estimate=pl.CostEstimate(flops=10**9, bytes_accessed=3 * 10**6, transcendentals=0),
     )(ends, edges, *own, *faces, w_res)
 
 
-def lower_kernel(joined_ref, front_ref, side_ref, corner_ref, w_ref, out_ref, plane, taps):
+def lower_kernel(joined_ref, front_ref, side_ref, corner_ref, w_ref, out_ref, planes, taps):
     span_x, span_y, span_z, channels = joined_ref.shape
     half_y, half_z = span_y // 2, span_z // 2
     lines = half_y * half_z
     count = (span_y + 1) * span_z
-    zero = lax.broadcasted_iota(jnp.int32, ((span_y + 1) * half_z, channels), 0) % half_z == 0
-    plane[0:8, :] = jnp.zeros((8, channels), jnp.float32)
-
-    def spread(x):
-        rows = (span_y + 1) * half_z
+    rows = (span_y + 1) * half_z
+    depth = 9 * channels
+    zero = lax.broadcasted_iota(jnp.int32, (rows, channels), 0) % half_z == 0
+    for k in range(2):
+        planes[k, 0:8, :] = jnp.zeros((8, channels), jnp.float32)
+
+    def fill(x, first, rest):
+        plane = planes.at[x % 2]
+        plane[8:8 + span_z, :] = first.reshape(span_z, channels).astype(jnp.float32)
+        plane[8 + span_z:8 + count, :] = rest.reshape(
+            span_y * span_z, channels).astype(jnp.float32)
         low = jnp.where(zero, 0.0, plane[pl.ds(7, rows, stride=2), :])
         for c, value in enumerate((low, plane[pl.ds(8, rows, stride=2), :],
                                    plane[pl.ds(9, rows, stride=2), :])):
@@ -402,31 +406,19 @@
                 at = (b * 3 + c) * channels
                 taps[x, :, at:at + channels] = piece.reshape(lines, channels).astype(jnp.bfloat16)
 
-    plane[8:8 + span_z, :] = corner_ref[...].reshape(span_z, channels).astype(jnp.float32)
-    plane[8 + span_z:8 + count, :] = front_ref[...].reshape(
-        span_y * span_z, channels).astype(jnp.float32)
-    spread(0)
-
-    def fill(x, carry):
-        plane[8:8 + span_z, :] = side_ref[x].reshape(span_z, channels).astype(jnp.float32)
-        plane[8 + span_z:8 + count, :] = joined_ref[x].reshape(
-            span_y * span_z, channels).astype(jnp.float32)
-        spread(x + 1)
-        return carry
-
-    lax.fori_loop(0, span_x, fill, 0)
-    depth = 9 * channels
-
-    def multiply(i, carry):
+    def multiply(i):
         total = None
         for a in range(3):
             part = jnp.dot(taps[2 * i + a], w_ref[a * depth:(a + 1) * depth, :],
                            preferred_element_type=jnp.float32)
             total = part if total is None else total + part
         out_ref[i] = total.reshape(half_y, half_z, w_ref.shape[-1]).astype(jnp.bfloat16)
-        return carry
-
-    lax.fori_loop(0, span_x // 2, multiply, 0)
+
+    fill(0, corner_ref[...], front_ref[...])
+    for x in range(1, span_x + 1):
+        fill(x, side_ref[x - 1], joined_ref[x - 1])
+        if x % 2 == 0:
+            multiply(x // 2 - 1)
 
 
 def lower(joined, front, side, corner, w_down):
@@ -441,7 +433,7 @@
         in_specs=[vm] * 5,
         out_specs=vm,
         scratch_shapes=[
-            pltpu.VMEM(((span_y + 1) * span_z + 16, channels), jnp.float32),
+            pltpu.VMEM((2, (span_y + 1) * span_z + 16, channels), jnp.float32),
             pltpu.VMEM((span_x + 1, span_y * span_z // 4, 9 * channels), jnp.bfloat16),
         ],
         compiler_params=pltpu.CompilerParams(vmem_limit_bytes=28 * 2**20),

time: 121 us -> 118 us (0.975)
  Pallas kernels: 42.4 us -> 39.4 us
    pallas_call x1, Pallas kernels: 5.29 us -> 3.39 us  [lower(): pl.pallas_call(lower_kernel, out_shape=jax.ShapeDtypeStruct((span_x // 2,...]
where the time goes in v5:
time: 118 us; the launch traced here: 116 us
  starting transfers between devices  49.5 us (42%)
  Pallas kernels  39.4 us (33%)
  waiting for transfers between devices  20.8 us (18%)
  local copies, waits for them, and re-layouts  6.15 us (5%)
    ppermute x11, starting transfers between devices, shifted(): return lax.ppermute(array, ('pts', 'nbr'), pairs)  43.5 us
    ppermute x11, waiting for transfers between devices, shifted(): return lax.ppermute(array, ('pts', 'nbr'), pairs)  20.8 us
    pallas_call x1, Pallas kernels, residual_base(): pl.pallas_call(functools.partial(residual_kernel, group), out_shape=[jax....  13.6 us
    pallas_call x1, Pallas kernels, add_rows(): pl.pallas_call(functools.partial(add_kernel, capacity), out_shape=[jax.Sh...  12.7 us
    pallas_call x1, Pallas kernels, pack(): pl.pallas_call(functools.partial(pack_kernel, devices, cap), out_shape=ja...  8.41 us
    all_to_all x1, starting transfers between devices, exchanged(): lax.all_to_all(array.reshape(devices, -1, array.shape[-1]), ('pts', 'nbr'...  6 us
    unnamed x10, local copies, waits for them, and re-layouts  3.53 us
    pallas_call x1, Pallas kernels, lower(): pl.pallas_call(lower_kernel, out_shape=jax.ShapeDtypeStruct((span_x // 2,...  3.39 us
  transfers between devices with their start and end apart: 12, of which 3 were waited for; matrix products, arithmetic and copies ran while one was open for 2% of the time, Pallas kernels for 13%

profile of v5, /device:TPU:12, one launch (start us, length us, event | category | flops | bytes accessed | tf_op | source)
XLA Modules:
  0.0 116.1 jit_solution(2780955797182782788)
XLA Ops:
  0.0 8.4 %pack.1 = bf16[8448,128]{1,0:T(8,128)(2,1)} custom-call(s32[32,128]{1,0:T(8,128)} %bitcast.12, s32[32,128]{1,0:T(8,128)} %bitcast.13, bf16[4096,128]{1,0:T(8,128)(2,1)} %bitcast.11), custom_call_target="tpu_custom_call" | custom-call | flops 100000000 | bytes 4000000 | tf_op jit(solution)/shard_map/pack/pallas_call | solution.py:81
  8.4 0.0 copy-start.3
  8.4 6.0 %all-to-all-start = ((bf16[32,264,128]{2,1,0:T(8,128)(2,1)}), bf16[32,264,128]{2,1,0:T(8,128)(2,1)S(1)}, u32[]{:S(2)}, u32[]{:S(2)}) async-start(bf16[32,264,128]{2,1,0:T(8,128)(2,1)} %bitcast.10), calls=%async_computation | async-start | bytes 4325376 | tf_op jit(solution)/shard_map/all_to_all | solution.py:458
  14.4 0.7 fusion
  15.2 3.1 %collective-permute-start.7 = (bf16[1,1,16,128]{3,2,1,0:T(8,128)(2,1)S(1)}, bf16[1,1,16,128]{3,2,1,0:T(8,128)(2,1)S(1)}, u32[]{:S(2)}, u32[]{:S(2)}) collective-permute-start(bf16[1,1,16,128]{3,2,1,0:T(8,128)(2,1)S(1)} %get-tuple-element.27), channel_id=1, source_target_pairs={{5,0},{6,1},{7,2},{9,4},{10,5},{11,6},{13,8},{14,9},{15,10},{17,12... | collective-permute-start | bytes 12296 | tf_op jit(solution)/shard_map/ppermute | solution.py:454
  18.3 2.5 %collective-permute-start.6 = (bf16[1,1,16,128]{3,2,1,0:T(8,128)(2,1)S(1)}, bf16[1,1,16,128]{3,2,1,0:T(8,128)(2,1)S(1)}, u32[]{:S(2)}, u32[]{:S(2)}) collective-permute-start(bf16[1,1,16,128]{3,2,1,0:T(8,128)(2,1)S(1)} %get-tuple-element.28), channel_id=1, source_target_pairs={{1,4},{2,5},{3,6},{5,8},{6,9},{7,10},{9,12},{10,13},{11,14},{13,16... | collective-permute-start | bytes 12296 | tf_op jit(solution)/shard_map/ppermute | solution.py:454
  20.7 4.0 %collective-permute-start.5 = (bf16[1,1,16,128]{3,2,1,0:T(8,128)(2,1)S(1)}, bf16[1,1,16,128]{3,2,1,0:T(8,128)(2,1)S(1)}, u32[]{:S(2)}, u32[]{:S(2)}) collective-permute-start(bf16[1,1,16,128]{3,2,1,0:T(8,128)(2,1)S(1)} %get-tuple-element.29), channel_id=1, source_target_pairs={{4,1},{5,2},{6,3},{8,5},{9,6},{10,7},{12,9},{13,10},{14,11},{16,13... | collective-permute-start | bytes 12296 | tf_op jit(solution)/shard_map/ppermute | solution.py:454
  24.7 1.9 %collective-permute-start.4 = (bf16[1,1,16,128]{3,2,1,0:T(8,128)(2,1)S(1)}, bf16[1,1,16,128]{3,2,1,0:T(8,128)(2,1)S(1)}, u32[]{:S(2)}, u32[]{:S(2)}) collective-permute-start(bf16[1,1,16,128]{3,2,1,0:T(8,128)(2,1)S(1)} %get-tuple-element.30), channel_id=1, source_target_pairs={{0,5},{1,6},{2,7},{4,9},{5,10},{6,11},{8,13},{9,14},{10,15},{12,17... | collective-permute-start | bytes 12296 | tf_op jit(solution)/shard_map/ppermute | solution.py:454
  26.7 0.9 fusion.1
  27.6 2.2 %collective-permute-start.2 = (bf16[16,1,16,128]{3,2,1,0:T(8,128)(2,1)S(1)}, bf16[16,1,16,128]{3,2,1,0:T(8,128)(2,1)S(1)}, u32[]{:S(2)}, u32[]{:S(2)}) collective-permute-start(bf16[16,1,16,128]{3,2,1,0:T(8,128)(2,1)S(1)} %get-tuple-element.31.ylast_ref), channel_id=1, source_target_pairs={{0,4},{1,5},{2,6},{3,7},{4,8},{5,9},{6,10},{7,11},{8,12},{9,13},{1... | collective-permute-start | bytes 196616 | tf_op jit(solution)/shard_map/ppermute | solution.py:454
  29.8 1.0 fusion.2
  30.8 7.3 %collective-permute-done.7.hh_ref = bf16[1,1,16,128]{3,2,1,0:T(8,128)(2,1)S(1)} collective-permute-done((bf16[1,1,16,128]{3,2,1,0:T(8,128)(2,1)S(1)}, bf16[1,1,16,128]{3,2,1,0:T(8,128)(2,1)S(1)}, u32[]{:S(2)}, u32[]{:S(2)}) %collective-permute-start.7) | collective-permute-done | bytes 4128 | tf_op jit(solution)/shard_map/ppermute | solution.py:454
  38.1 4.5 %collective-permute-start.3 = (bf16[16,1,16,128]{3,2,1,0:T(8,128)(2,1)S(1)}, bf16[16,1,16,128]{3,2,1,0:T(8,128)(2,1)S(1)}, u32[]{:S(2)}, u32[]{:S(2)}) collective-permute-start(bf16[16,1,16,128]{3,2,1,0:T(8,128)(2,1)S(1)} %get-tuple-element.32.yfirst_ref), channel_id=1, source_target_pairs={{4,0},{5,1},{6,2},{7,3},{8,4},{9,5},{10,6},{11,7},{12,8},{13,9},{1... | collective-permute-start | bytes 196616 | tf_op jit(solution)/shard_map/ppermute | solution.py:454
  42.6 8.8 %collective-permute-done.6.hl_ref = bf16[1,1,16,128]{3,2,1,0:T(8,128)(2,1)S(1)} collective-permute-done((bf16[1,1,16,128]{3,2,1,0:T(8,128)(2,1)S(1)}, bf16[1,1,16,128]{3,2,1,0:T(8,128)(2,1)S(1)}, u32[]{:S(2)}, u32[]{:S(2)}) %collective-permute-start.6) | collective-permute-done | bytes 4128 | tf_op jit(solution)/shard_map/ppermute | solution.py:454
  51.4 1.9 %collective-permute-start = (bf16[1,32,16,128]{3,2,1,0:T(8,128)(2,1)S(1)}, bf16[1,32,16,128]{3,2,1,0:T(8,128)(2,1)S(1)}, u32[]{:S(2)}, u32[]{:S(2)}) collective-permute-start(bf16[1,32,16,128]{3,2,1,0:T(8,128)(2,1)S(1)} %get-tuple-element.33.xlast_ref), channel_id=1, source_target_pairs={{0,1},{1,2},{2,3},{4,5},{5,6},{6,7},{8,9},{9,10},{10,11},{12,13},{... | collective-permute-start | bytes 393224 | tf_op jit(solution)/shard_map/ppermute | solution.py:454
  53.3 0.0 collective-permute-done.5.lh_ref
  53.3 3.9 %collective-permute-start.1 = (bf16[1,32,16,128]{3,2,1,0:T(8,128)(2,1)S(1)}, bf16[1,32,16,128]{3,2,1,0:T(8,128)(2,1)S(1)}, u32[]{:S(2)}, u32[]{:S(2)}) collective-permute-start(bf16[1,32,16,128]{3,2,1,0:T(8,128)(2,1)S(1)} %get-tuple-element.34.xfirst_ref), channel_id=1, source_target_pairs={{1,0},{2,1},{3,2},{5,4},{6,5},{7,6},{9,8},{10,9},{11,10},{13,12},{... | collective-permute-start | bytes 393224 | tf_op jit(solution)/shard_map/ppermute | solution.py:454
  57.3 0.0 copy-start.1
  57.3 1.6 %copy-done.1 = bf16[16,32,16,128]{3,2,1,0:T(8,128)(2,1)S(1)} copy-done((bf16[16,32,16,128]{3,2,1,0:T(8,128)(2,1)S(1)}, bf16[16,32,16,128]{3,2,1,0:T(8,128)(2,1)}, u32[]{:S(2)}) %copy-start.1) | copy-done | bytes 2097176
  58.8 13.6 %residual.1 = (f32[16,16,2,16,128]{4,3,2,1,0:T(8,128)S(1)}, f32[2,16,2,16,128]{4,3,2,1,0:T(8,128)S(1)}, f32[2,16,16,128]{3,2,1,0:T(8,128)S(1)}) custom-call(bf16[16,32,16,128]{3,2,1,0:T(8,128)(2,1)S(1)} %copy-done.1, bf16[27,128,128]{2,1,0:T(8,128)(2,1)S(1)} %copy-done.3), custom_call_target="tpu_custom_call" | custom-call | flops 7247757312 | bytes 8000000 | tf_op jit(solution)/shard_map/residual/pallas_call | solution.py:286
  72.5 1.9 %copy-done = f32[16,16,2,16,128]{4,3,2,1,0:T(8,128)} copy-done((f32[16,16,2,16,128]{4,3,2,1,0:T(8,128)}, f32[16,16,2,16,128]{4,3,2,1,0:T(8,128)S(1)}, u32[]{:S(2)}) %copy-start) | copy-done | bytes 4194328
  74.4 0.0 collective-permute-done.2.ylow_ref
  74.4 0.0 collective-permute-done.3.yhigh_ref
  74.4 0.0 collective-permute-done.1.xhigh_ref
  74.4 1.3 %border.1 = (f32[2,16,2,16,128]{4,3,2,1,0:T(8,128)S(1)}, f32[2,16,16,128]{3,2,1,0:T(8,128)S(1)}) custom-call(f32[2,16,2,16,128]{4,3,2,1,0:T(8,128)S(1)} %get-tuple-element.19.ends_ref, f32[2,16,16,128]{3,2,1,0:T(8,128)S(1)} %get-tuple-element.20.edges_ref, bf16[1,32,16,128]{3,2,1,0:T(8,128)(2,1)S(1)} %get-tuple-element.34.xfirst_ref, ...), custom_call_target="tpu_custom_call" | custom-call | flops 1000000000 | bytes 3000000 | tf_op jit(solution)/shard_map/border/pallas_call | solution.py:366
  75.8 0.0 copy-start.2
  75.8 12.7 %add_rows.1 = (bf16[16,32,16,128]{3,2,1,0:T(8,128)(2,1)S(1)}, bf16[1,32,16,128]{3,2,1,0:T(8,128)(2,1)S(1)}, bf16[16,1,16,128]{3,2,1,0:T(8,128)(2,1)S(1)}, bf16[1,1,16,128]{3,2,1,0:T(8,128)(2,1)S(1)}) custom-call(bf16[8448,128]{1,0:T(8,128)(2,1)S(1)} %bitcast.7, f32[8192,128]{1,0:T(8,128)} %bitcast.8, f32[2,16,2,16,128]{4,3,2,1,0:T(8,128)S(1)} %get-tuple-element.21.ends_ref, ...), custom_call_target="tpu_custom_call" | custom-call | flops 100000000 | bytes 8000000 | tf_op jit(solution)/shard_map/add_rows/pallas_call | solution.py:165
  88.5 1.9 %collective-permute-start.8 = (bf16[1,32,16,128]{3,2,1,0:T(8,128)(2,1)S(1)}, bf16[1,32,16,128]{3,2,1,0:T(8,128)(2,1)S(1)}, u32[]{:S(2)}, u32[]{:S(2)}) collective-permute-start(bf16[1,32,16,128]{3,2,1,0:T(8,128)(2,1)S(1)} %get-tuple-element.24), channel_id=1, source_target_pairs={{0,1},{1,2},{2,3},{4,5},{5,6},{6,7},{8,9},{9,10},{10,11},{12,13},{... | collective-permute-start | bytes 393224 | tf_op jit(solution)/shard_map/ppermute | solution.py:454
  90.4 15.5 %collective-permute-start.9 = (bf16[16,1,16,128]{3,2,1,0:T(8,128)(2,1)S(1)}, bf16[16,1,16,128]{3,2,1,0:T(8,128)(2,1)S(1)}, u32[]{:S(2)}, u32[]{:S(2)}) collective-permute-start(bf16[16,1,16,128]{3,2,1,0:T(8,128)(2,1)S(1)} %get-tuple-element.25), channel_id=1, source_target_pairs={{0,4},{1,5},{2,6},{3,7},{4,8},{5,9},{6,10},{7,11},{8,12},{9,13},{1... | collective-permute-start | bytes 196616 | tf_op jit(solution)/shard_map/ppermute | solution.py:454
  106.0 2.1 %collective-permute-start.10 = (bf16[1,1,16,128]{3,2,1,0:T(8,128)(2,1)S(1)}, bf16[1,1,16,128]{3,2,1,0:T(8,128)(2,1)S(1)}, u32[]{:S(2)}, u32[]{:S(2)}) collective-permute-start(bf16[1,1,16,128]{3,2,1,0:T(8,128)(2,1)S(1)} %get-tuple-element.26), channel_id=1, source_target_pairs={{0,5},{1,6},{2,7},{4,9},{5,10},{6,11},{8,13},{9,14},{10,15},{12,17... | collective-permute-start | bytes 12296 | tf_op jit(solution)/shard_map/ppermute | solution.py:454
  108.1 4.6 %collective-permute-done.10.corner_ref = bf16[1,1,16,128]{3,2,1,0:T(8,128)(2,1)S(1)} collective-permute-done((bf16[1,1,16,128]{3,2,1,0:T(8,128)(2,1)S(1)}, bf16[1,1,16,128]{3,2,1,0:T(8,128)(2,1)S(1)}, u32[]{:S(2)}, u32[]{:S(2)}) %collective-permute-start.10) | collective-permute-done | bytes 4128 | tf_op jit(solution)/shard_map/ppermute | solution.py:454
  112.7 3.4 %lower.1 = bf16[8,16,8,256]{3,2,1,0:T(8,128)(2,1)} custom-call(bf16[16,32,16,128]{3,2,1,0:T(8,128)(2,1)S(1)} %get-tuple-element.23.joined_ref, bf16[1,32,16,128]{3,2,1,0:T(8,128)(2,1)S(1)} %collective-permute-done.8.front_ref, bf16[16,1,16,128]{3,2,1,0:T(8,128)(2,1)S(1)} %collective-permute-done.9.side_ref, ...), custom_call_target="tpu_custom_call" | custom-call | flops 1811939328 | bytes 5000000 | tf_op jit(solution)/shard_map/lower/pallas_call | solution.py:429
  (10 shorter events, 0.0 us)
Async XLA Ops:
  8.4 48.8 %copy-start.3 = (bf16[27,128,128]{2,1,0:T(8,128)(2,1)S(1)}, bf16[27,128,128]{2,1,0:T(8,128)(2,1)}, u32[]{:S(2)}) copy-start(bf16[27,128,128]{2,1,0:T(8,128)(2,1)} %w_ref.3) | copy-start | bytes 2654212
  8.4 67.3 %all-to-all-start = ((bf16[32,264,128]{2,1,0:T(8,128)(2,1)}), bf16[32,264,128]{2,1,0:T(8,128)(2,1)S(1)}, u32[]{:S(2)}, u32[]{:S(2)}) async-start(bf16[32,264,128]{2,1,0:T(8,128)(2,1)} %bitcast.10), calls=%async_computation | async-start | bytes 4325376 | tf_op jit(solution)/shard_map/all_to_all | solution.py:458
  15.2 22.9 %collective-permute-start.7 = (bf16[1,1,16,128]{3,2,1,0:T(8,128)(2,1)S(1)}, bf16[1,1,16,128]{3,2,1,0:T(8,128)(2,1)S(1)}, u32[]{:S(2)}, u32[]{:S(2)}) collective-permute-start(bf16[1,1,16,128]{3,2,1,0:T(8,128)(2,1)S(1)} %get-tuple-element.27), channel_id=1, source_target_pairs={{5,0},{6,1},{7,2},{9,4},{10,5},{11,6},{13,8},{14,9},{15,10},{17,12... | collective-permute-start | bytes 12296 | tf_op jit(solution)/shard_map/ppermute | solution.py:454
  18.3 33.1 %collective-permute-start.6 = (bf16[1,1,16,128]{3,2,1,0:T(8,128)(2,1)S(1)}, bf16[1,1,16,128]{3,2,1,0:T(8,128)(2,1)S(1)}, u32[]{:S(2)}, u32[]{:S(2)}) collective-permute-start(bf16[1,1,16,128]{3,2,1,0:T(8,128)(2,1)S(1)} %get-tuple-element.28), channel_id=1, source_target_pairs={{1,4},{2,5},{3,6},{5,8},{6,9},{7,10},{9,12},{10,13},{11,14},{13,16... | collective-permute-start | bytes 12296 | tf_op jit(solution)/shard_map/ppermute | solution.py:454
  20.7 32.5 %collective-permute-start.5 = (bf16[1,1,16,128]{3,2,1,0:T(8,128)(2,1)S(1)}, bf16[1,1,16,128]{3,2,1,0:T(8,128)(2,1)S(1)}, u32[]{:S(2)}, u32[]{:S(2)}) collective-permute-start(bf16[1,1,16,128]{3,2,1,0:T(8,128)(2,1)S(1)} %get-tuple-element.29), channel_id=1, source_target_pairs={{4,1},{5,2},{6,3},{8,5},{9,6},{10,7},{12,9},{13,10},{14,11},{16,13... | collective-permute-start | bytes 12296 | tf_op jit(solution)/shard_map/ppermute | solution.py:454
  24.7 49.7 %collective-permute-start.4 = (bf16[1,1,16,128]{3,2,1,0:T(8,128)(2,1)S(1)}, bf16[1,1,16,128]{3,2,1,0:T(8,128)(2,1)S(1)}, u32[]{:S(2)}, u32[]{:S(2)}) collective-permute-start(bf16[1,1,16,128]{3,2,1,0:T(8,128)(2,1)S(1)} %get-tuple-element.30), channel_id=1, source_target_pairs={{0,5},{1,6},{2,7},{4,9},{5,10},{6,11},{8,13},{9,14},{10,15},{12,17... | collective-permute-start | bytes 12296 | tf_op jit(solution)/shard_map/ppermute | solution.py:454
  27.6 46.9 %collective-permute-start.2 = (bf16[16,1,16,128]{3,2,1,0:T(8,128)(2,1)S(1)}, bf16[16,1,16,128]{3,2,1,0:T(8,128)(2,1)S(1)}, u32[]{:S(2)}, u32[]{:S(2)}) collective-permute-start(bf16[16,1,16,128]{3,2,1,0:T(8,128)(2,1)S(1)} %get-tuple-element.31.ylast_ref), channel_id=1, source_target_pairs={{0,4},{1,5},{2,6},{3,7},{4,8},{5,9},{6,10},{7,11},{8,12},{9,13},{1... | collective-permute-start | bytes 196616 | tf_op jit(solution)/shard_map/ppermute | solution.py:454
  38.1 36.4 %collective-permute-start.3 = (bf16[16,1,16,128]{3,2,1,0:T(8,128)(2,1)S(1)}, bf16[16,1,16,128]{3,2,1,0:T(8,128)(2,1)S(1)}, u32[]{:S(2)}, u32[]{:S(2)}) collective-permute-start(bf16[16,1,16,128]{3,2,1,0:T(8,128)(2,1)S(1)} %get-tuple-element.32.yfirst_ref), channel_id=1, source_target_pairs={{4,0},{5,1},{6,2},{7,3},{8,4},{9,5},{10,6},{11,7},{12,8},{13,9},{1... | collective-permute-start | bytes 196616 | tf_op jit(solution)/shard_map/ppermute | solution.py:454
  51.4 23.0 %collective-permute-start = (bf16[1,32,16,128]{3,2,1,0:T(8,128)(2,1)S(1)}, bf16[1,32,16,128]{3,2,1,0:T(8,128)(2,1)S(1)}, u32[]{:S(2)}, u32[]{:S(2)}) collective-permute-start(bf16[1,32,16,128]{3,2,1,0:T(8,128)(2,1)S(1)} %get-tuple-element.33.xlast_ref), channel_id=1, source_target_pairs={{0,1},{1,2},{2,3},{4,5},{5,6},{6,7},{8,9},{9,10},{10,11},{12,13},{... | collective-permute-start | bytes 393224 | tf_op jit(solution)/shard_map/ppermute | solution.py:454
  53.3 21.1 %collective-permute-start.1 = (bf16[1,32,16,128]{3,2,1,0:T(8,128)(2,1)S(1)}, bf16[1,32,16,128]{3,2,1,0:T(8,128)(2,1)S(1)}, u32[]{:S(2)}, u32[]{:S(2)}) collective-permute-start(bf16[1,32,16,128]{3,2,1,0:T(8,128)(2,1)S(1)} %get-tuple-element.34.xfirst_ref), channel_id=1, source_target_pairs={{1,0},{2,1},{3,2},{5,4},{6,5},{7,6},{9,8},{10,9},{11,10},{13,12},{... | collective-permute-start | bytes 393224 | tf_op jit(solution)/shard_map/ppermute | solution.py:454
  57.3 1.6 %copy-start.1 = (bf16[16,32,16,128]{3,2,1,0:T(8,128)(2,1)S(1)}, bf16[16,32,16,128]{3,2,1,0:T(8,128)(2,1)}, u32[]{:S(2)}) copy-start(bf16[16,32,16,128]{3,2,1,0:T(8,128)(2,1)} %level_ref) | copy-start | bytes 6291460
  58.8 15.6 %copy-start.4 = (bf16[27,128,128]{2,1,0:T(8,128)(2,1)S(1)}, bf16[27,128,128]{2,1,0:T(8,128)(2,1)}, u32[]{:S(2)}) copy-start(bf16[27,128,128]{2,1,0:T(8,128)(2,1)} %w_ref.3) | copy-start | bytes 2654212
  72.5 1.9 %copy-start = (f32[16,16,2,16,128]{4,3,2,1,0:T(8,128)}, f32[16,16,2,16,128]{4,3,2,1,0:T(8,128)S(1)}, u32[]{:S(2)}) copy-start(f32[16,16,2,16,128]{4,3,2,1,0:T(8,128)S(1)} %get-tuple-element.18) | copy-start | bytes 12582916
  75.8 36.9 %copy-start.2 = (bf16[27,128,256]{2,1,0:T(8,128)(2,1)S(1)}, bf16[27,128,256]{2,1,0:T(8,128)(2,1)}, u32[]{:S(2)}) copy-start(bf16[27,128,256]{2,1,0:T(8,128)(2,1)} %param.11) | copy-start | bytes 5308420
  88.5 24.2 %collective-permute-start.8 = (bf16[1,32,16,128]{3,2,1,0:T(8,128)(2,1)S(1)}, bf16[1,32,16,128]{3,2,1,0:T(8,128)(2,1)S(1)}, u32[]{:S(2)}, u32[]{:S(2)}) collective-permute-start(bf16[1,32,16,128]{3,2,1,0:T(8,128)(2,1)S(1)} %get-tuple-element.24), channel_id=1, source_target_pairs={{0,1},{1,2},{2,3},{4,5},{5,6},{6,7},{8,9},{9,10},{10,11},{12,13},{... | collective-permute-start | bytes 393224 | tf_op jit(solution)/shard_map/ppermute | solution.py:454
  90.4 22.2 %collective-permute-start.9 = (bf16[16,1,16,128]{3,2,1,0:T(8,128)(2,1)S(1)}, bf16[16,1,16,128]{3,2,1,0:T(8,128)(2,1)S(1)}, u32[]{:S(2)}, u32[]{:S(2)}) collective-permute-start(bf16[16,1,16,128]{3,2,1,0:T(8,128)(2,1)S(1)} %get-tuple-element.25), channel_id=1, source_target_pairs={{0,4},{1,5},{2,6},{3,7},{4,8},{5,9},{6,10},{7,11},{8,12},{9,13},{1... | collective-permute-start | bytes 196616 | tf_op jit(solution)/shard_map/ppermute | solution.py:454
  106.0 6.7 %collective-permute-start.10 = (bf16[1,1,16,128]{3,2,1,0:T(8,128)(2,1)S(1)}, bf16[1,1,16,128]{3,2,1,0:T(8,128)(2,1)S(1)}, u32[]{:S(2)}, u32[]{:S(2)}) collective-permute-start(bf16[1,1,16,128]{3,2,1,0:T(8,128)(2,1)S(1)} %get-tuple-element.26), channel_id=1, source_target_pairs={{0,5},{1,6},{2,7},{4,9},{5,10},{6,11},{8,13},{9,14},{10,15},{12,17... | collective-permute-start | bytes 12296 | tf_op jit(solution)/shard_map/ppermute | solution.py:454

commit v6 on v5

--- a/solution.py
+++ b/solution.py
@@ -10,6 +10,7 @@
 LANES = 128
 EXTRA = 8
 PIECES = 4
+LINES = 4
 
 
 def pack_kernel(devices, cap, owner_ref, cell_ref, rows_hbm, out_hbm,
@@ -56,11 +57,14 @@
     copy.wait()
 
     def step(b, carry):
+        lines = [slot_smem.at[b * LINES + i] for i in range(LINES)]
         for u in range(LANES):
-            spread[pl.ds(slot_smem[b, u], 1), :] = wide[pl.ds(b * LANES + u, 1), :]
+            for i in range(LINES):
+                spread[pl.ds(lines[i][u], 1), :] = wide[
+                    pl.ds((b * LINES + i) * LANES + u, 1), :]
         return carry
 
-    lax.fori_loop(0, blocks, step, 0)
+    lax.fori_loop(0, blocks // LINES, step, 0)
     piece = staged.shape[0] // PIECES
     sends = []
     for i in range(PIECES):
@@ -132,10 +136,10 @@
     for j in range(per):
         def step(o, carry):
             start = pl.multiple_of(o * stride + j * LANES, 8)
+            line = slot_smem.at[j * devices + o]
             for u in range(width):
-                at = slot_smem[j * devices + o, u]
                 s = sums[u % len(sums)]
-                s[pl.ds(at, 1), :] += wide[pl.ds(start + u, 1), :]
+                s[pl.ds(line[u], 1), :] += wide[pl.ds(start + u, 1), :]
             return carry
 
         lax.fori_loop(0, devices, step, 0)

time: 118 us -> 117 us (level)
  no operation moved by 1% of the time
where the time goes in v6:
time: 117 us; the launch traced here: 115 us
  starting transfers between devices  49.5 us (42%)
  Pallas kernels  38.5 us (33%)
  waiting for transfers between devices  20.7 us (18%)
  local copies, waits for them, and re-layouts  6.15 us (5%)
    ppermute x11, starting transfers between devices, shifted(): return lax.ppermute(array, ('pts', 'nbr'), pairs)  43.5 us
    ppermute x11, waiting for transfers between devices, shifted(): return lax.ppermute(array, ('pts', 'nbr'), pairs)  20.7 us
    pallas_call x1, Pallas kernels, residual_base(): pl.pallas_call(functools.partial(residual_kernel, group), out_shape=[jax....  13.6 us
    pallas_call x1, Pallas kernels, add_rows(): pl.pallas_call(functools.partial(add_kernel, capacity), out_shape=[jax.Sh...  12.7 us
    pallas_call x1, Pallas kernels, pack(): pl.pallas_call(functools.partial(pack_kernel, devices, cap), out_shape=ja...  7.5 us
    all_to_all x1, starting transfers between devices, exchanged(): lax.all_to_all(array.reshape(devices, -1, array.shape[-1]), ('pts', 'nbr'...  6 us
    unnamed x10, local copies, waits for them, and re-layouts  3.53 us
    pallas_call x1, Pallas kernels, lower(): pl.pallas_call(lower_kernel, out_shape=jax.ShapeDtypeStruct((span_x // 2,...  3.39 us
  transfers between devices with their start and end apart: 12, of which 3 were waited for; matrix products, arithmetic and copies ran while one was open for 2% of the time, Pallas kernels for 13%

profile of v6, /device:TPU:12, one launch (start us, length us, event | category | flops | bytes accessed | tf_op | source)
XLA Modules:
  0.0 115.2 jit_solution(16621652036050207478)
XLA Ops:
  0.0 7.5 %pack.1 = bf16[8448,128]{1,0:T(8,128)(2,1)} custom-call(s32[32,128]{1,0:T(8,128)} %bitcast.12, s32[32,128]{1,0:T(8,128)} %bitcast.13, bf16[4096,128]{1,0:T(8,128)(2,1)} %bitcast.11), custom_call_target="tpu_custom_call" | custom-call | flops 100000000 | bytes 4000000 | tf_op jit(solution)/shard_map/pack/pallas_call | solution.py:85
  7.5 0.0 copy-start.3
  7.5 6.0 %all-to-all-start = ((bf16[32,264,128]{2,1,0:T(8,128)(2,1)}), bf16[32,264,128]{2,1,0:T(8,128)(2,1)S(1)}, u32[]{:S(2)}, u32[]{:S(2)}) async-start(bf16[32,264,128]{2,1,0:T(8,128)(2,1)} %bitcast.10), calls=%async_computation | async-start | bytes 4325376 | tf_op jit(solution)/shard_map/all_to_all | solution.py:462
  13.5 0.7 fusion
  14.3 3.1 %collective-permute-start.7 = (bf16[1,1,16,128]{3,2,1,0:T(8,128)(2,1)S(1)}, bf16[1,1,16,128]{3,2,1,0:T(8,128)(2,1)S(1)}, u32[]{:S(2)}, u32[]{:S(2)}) collective-permute-start(bf16[1,1,16,128]{3,2,1,0:T(8,128)(2,1)S(1)} %get-tuple-element.27), channel_id=1, source_target_pairs={{5,0},{6,1},{7,2},{9,4},{10,5},{11,6},{13,8},{14,9},{15,10},{17,12... | collective-permute-start | bytes 12296 | tf_op jit(solution)/shard_map/ppermute | solution.py:458
  17.3 2.5 %collective-permute-start.6 = (bf16[1,1,16,128]{3,2,1,0:T(8,128)(2,1)S(1)}, bf16[1,1,16,128]{3,2,1,0:T(8,128)(2,1)S(1)}, u32[]{:S(2)}, u32[]{:S(2)}) collective-permute-start(bf16[1,1,16,128]{3,2,1,0:T(8,128)(2,1)S(1)} %get-tuple-element.28), channel_id=1, source_target_pairs={{1,4},{2,5},{3,6},{5,8},{6,9},{7,10},{9,12},{10,13},{11,14},{13,16... | collective-permute-start | bytes 12296 | tf_op jit(solution)/shard_map/ppermute | solution.py:458
  19.8 4.0 %collective-permute-start.5 = (bf16[1,1,16,128]{3,2,1,0:T(8,128)(2,1)S(1)}, bf16[1,1,16,128]{3,2,1,0:T(8,128)(2,1)S(1)}, u32[]{:S(2)}, u32[]{:S(2)}) collective-permute-start(bf16[1,1,16,128]{3,2,1,0:T(8,128)(2,1)S(1)} %get-tuple-element.29), channel_id=1, source_target_pairs={{4,1},{5,2},{6,3},{8,5},{9,6},{10,7},{12,9},{13,10},{14,11},{16,13... | collective-permute-start | bytes 12296 | tf_op jit(solution)/shard_map/ppermute | solution.py:458
  23.8 1.9 %collective-permute-start.4 = (bf16[1,1,16,128]{3,2,1,0:T(8,128)(2,1)S(1)}, bf16[1,1,16,128]{3,2,1,0:T(8,128)(2,1)S(1)}, u32[]{:S(2)}, u32[]{:S(2)}) collective-permute-start(bf16[1,1,16,128]{3,2,1,0:T(8,128)(2,1)S(1)} %get-tuple-element.30), channel_id=1, source_target_pairs={{0,5},{1,6},{2,7},{4,9},{5,10},{6,11},{8,13},{9,14},{10,15},{12,17... | collective-permute-start | bytes 12296 | tf_op jit(solution)/shard_map/ppermute | solution.py:458
  25.7 0.9 fusion.1
  26.6 2.2 %collective-permute-start.2 = (bf16[16,1,16,128]{3,2,1,0:T(8,128)(2,1)S(1)}, bf16[16,1,16,128]{3,2,1,0:T(8,128)(2,1)S(1)}, u32[]{:S(2)}, u32[]{:S(2)}) collective-permute-start(bf16[16,1,16,128]{3,2,1,0:T(8,128)(2,1)S(1)} %get-tuple-element.31.ylast_ref), channel_id=1, source_target_pairs={{0,4},{1,5},{2,6},{3,7},{4,8},{5,9},{6,10},{7,11},{8,12},{9,13},{1... | collective-permute-start | bytes 196616 | tf_op jit(solution)/shard_map/ppermute | solution.py:458
  28.9 1.0 fusion.2
  29.9 7.3 %collective-permute-done.7.hh_ref = bf16[1,1,16,128]{3,2,1,0:T(8,128)(2,1)S(1)} collective-permute-done((bf16[1,1,16,128]{3,2,1,0:T(8,128)(2,1)S(1)}, bf16[1,1,16,128]{3,2,1,0:T(8,128)(2,1)S(1)}, u32[]{:S(2)}, u32[]{:S(2)}) %collective-permute-start.7) | collective-permute-done | bytes 4128 | tf_op jit(solution)/shard_map/ppermute | solution.py:458
  37.1 4.5 %collective-permute-start.3 = (bf16[16,1,16,128]{3,2,1,0:T(8,128)(2,1)S(1)}, bf16[16,1,16,128]{3,2,1,0:T(8,128)(2,1)S(1)}, u32[]{:S(2)}, u32[]{:S(2)}) collective-permute-start(bf16[16,1,16,128]{3,2,1,0:T(8,128)(2,1)S(1)} %get-tuple-element.32.yfirst_ref), channel_id=1, source_target_pairs={{4,0},{5,1},{6,2},{7,3},{8,4},{9,5},{10,6},{11,7},{12,8},{13,9},{1... | collective-permute-start | bytes 196616 | tf_op jit(solution)/shard_map/ppermute | solution.py:458
  41.6 8.8 %collective-permute-done.6.hl_ref = bf16[1,1,16,128]{3,2,1,0:T(8,128)(2,1)S(1)} collective-permute-done((bf16[1,1,16,128]{3,2,1,0:T(8,128)(2,1)S(1)}, bf16[1,1,16,128]{3,2,1,0:T(8,128)(2,1)S(1)}, u32[]{:S(2)}, u32[]{:S(2)}) %collective-permute-start.6) | collective-permute-done | bytes 4128 | tf_op jit(solution)/shard_map/ppermute | solution.py:458
  50.5 1.9 %collective-permute-start = (bf16[1,32,16,128]{3,2,1,0:T(8,128)(2,1)S(1)}, bf16[1,32,16,128]{3,2,1,0:T(8,128)(2,1)S(1)}, u32[]{:S(2)}, u32[]{:S(2)}) collective-permute-start(bf16[1,32,16,128]{3,2,1,0:T(8,128)(2,1)S(1)} %get-tuple-element.33.xlast_ref), channel_id=1, source_target_pairs={{0,1},{1,2},{2,3},{4,5},{5,6},{6,7},{8,9},{9,10},{10,11},{12,13},{... | collective-permute-start | bytes 393224 | tf_op jit(solution)/shard_map/ppermute | solution.py:458
  52.4 3.9 %collective-permute-start.1 = (bf16[1,32,16,128]{3,2,1,0:T(8,128)(2,1)S(1)}, bf16[1,32,16,128]{3,2,1,0:T(8,128)(2,1)S(1)}, u32[]{:S(2)}, u32[]{:S(2)}) collective-permute-start(bf16[1,32,16,128]{3,2,1,0:T(8,128)(2,1)S(1)} %get-tuple-element.34.xfirst_ref), channel_id=1, source_target_pairs={{1,0},{2,1},{3,2},{5,4},{6,5},{7,6},{9,8},{10,9},{11,10},{13,12},{... | collective-permute-start | bytes 393224 | tf_op jit(solution)/shard_map/ppermute | solution.py:458
  56.3 0.0 copy-start.1
  56.4 1.6 %copy-done.1 = bf16[16,32,16,128]{3,2,1,0:T(8,128)(2,1)S(1)} copy-done((bf16[16,32,16,128]{3,2,1,0:T(8,128)(2,1)S(1)}, bf16[16,32,16,128]{3,2,1,0:T(8,128)(2,1)}, u32[]{:S(2)}) %copy-start.1) | copy-done | bytes 2097176
  57.9 13.6 %residual.1 = (f32[16,16,2,16,128]{4,3,2,1,0:T(8,128)S(1)}, f32[2,16,2,16,128]{4,3,2,1,0:T(8,128)S(1)}, f32[2,16,16,128]{3,2,1,0:T(8,128)S(1)}) custom-call(bf16[16,32,16,128]{3,2,1,0:T(8,128)(2,1)S(1)} %copy-done.1, bf16[27,128,128]{2,1,0:T(8,128)(2,1)S(1)} %copy-done.3), custom_call_target="tpu_custom_call" | custom-call | flops 7247757312 | bytes 8000000 | tf_op jit(solution)/shard_map/residual/pallas_call | solution.py:290
  71.6 1.9 %copy-done = f32[16,16,2,16,128]{4,3,2,1,0:T(8,128)} copy-done((f32[16,16,2,16,128]{4,3,2,1,0:T(8,128)}, f32[16,16,2,16,128]{4,3,2,1,0:T(8,128)S(1)}, u32[]{:S(2)}) %copy-start) | copy-done | bytes 4194328
  73.5 0.0 collective-permute-done.xlow_ref
  73.5 0.0 collective-permute-done.1.xhigh_ref
  73.5 1.3 %border.1 = (f32[2,16,2,16,128]{4,3,2,1,0:T(8,128)S(1)}, f32[2,16,16,128]{3,2,1,0:T(8,128)S(1)}) custom-call(f32[2,16,2,16,128]{4,3,2,1,0:T(8,128)S(1)} %get-tuple-element.19.ends_ref, f32[2,16,16,128]{3,2,1,0:T(8,128)S(1)} %get-tuple-element.20.edges_ref, bf16[1,32,16,128]{3,2,1,0:T(8,128)(2,1)S(1)} %get-tuple-element.34.xfirst_ref, ...), custom_call_target="tpu_custom_call" | custom-call | flops 1000000000 | bytes 3000000 | tf_op jit(solution)/shard_map/border/pallas_call | solution.py:370
  74.8 0.0 all-to-all-done
  74.9 0.0 copy-start.2
  74.9 12.7 %add_rows.1 = (bf16[16,32,16,128]{3,2,1,0:T(8,128)(2,1)S(1)}, bf16[1,32,16,128]{3,2,1,0:T(8,128)(2,1)S(1)}, bf16[16,1,16,128]{3,2,1,0:T(8,128)(2,1)S(1)}, bf16[1,1,16,128]{3,2,1,0:T(8,128)(2,1)S(1)}) custom-call(bf16[8448,128]{1,0:T(8,128)(2,1)S(1)} %bitcast.7, f32[8192,128]{1,0:T(8,128)} %bitcast.8, f32[2,16,2,16,128]{4,3,2,1,0:T(8,128)S(1)} %get-tuple-element.21.ends_ref, ...), custom_call_target="tpu_custom_call" | custom-call | flops 100000000 | bytes 8000000 | tf_op jit(solution)/shard_map/add_rows/pallas_call | solution.py:169
  87.6 1.9 %collective-permute-start.8 = (bf16[1,32,16,128]{3,2,1,0:T(8,128)(2,1)S(1)}, bf16[1,32,16,128]{3,2,1,0:T(8,128)(2,1)S(1)}, u32[]{:S(2)}, u32[]{:S(2)}) collective-permute-start(bf16[1,32,16,128]{3,2,1,0:T(8,128)(2,1)S(1)} %get-tuple-element.24), channel_id=1, source_target_pairs={{0,1},{1,2},{2,3},{4,5},{5,6},{6,7},{8,9},{9,10},{10,11},{12,13},{... | collective-permute-start | bytes 393224 | tf_op jit(solution)/shard_map/ppermute | solution.py:458
  89.5 15.5 %collective-permute-start.9 = (bf16[16,1,16,128]{3,2,1,0:T(8,128)(2,1)S(1)}, bf16[16,1,16,128]{3,2,1,0:T(8,128)(2,1)S(1)}, u32[]{:S(2)}, u32[]{:S(2)}) collective-permute-start(bf16[16,1,16,128]{3,2,1,0:T(8,128)(2,1)S(1)} %get-tuple-element.25), channel_id=1, source_target_pairs={{0,4},{1,5},{2,6},{3,7},{4,8},{5,9},{6,10},{7,11},{8,12},{9,13},{1... | collective-permute-start | bytes 196616 | tf_op jit(solution)/shard_map/ppermute | solution.py:458
  105.1 2.1 %collective-permute-start.10 = (bf16[1,1,16,128]{3,2,1,0:T(8,128)(2,1)S(1)}, bf16[1,1,16,128]{3,2,1,0:T(8,128)(2,1)S(1)}, u32[]{:S(2)}, u32[]{:S(2)}) collective-permute-start(bf16[1,1,16,128]{3,2,1,0:T(8,128)(2,1)S(1)} %get-tuple-element.26), channel_id=1, source_target_pairs={{0,5},{1,6},{2,7},{4,9},{5,10},{6,11},{8,13},{9,14},{10,15},{12,17... | collective-permute-start | bytes 12296 | tf_op jit(solution)/shard_map/ppermute | solution.py:458
  107.2 4.6 %collective-permute-done.10.corner_ref = bf16[1,1,16,128]{3,2,1,0:T(8,128)(2,1)S(1)} collective-permute-done((bf16[1,1,16,128]{3,2,1,0:T(8,128)(2,1)S(1)}, bf16[1,1,16,128]{3,2,1,0:T(8,128)(2,1)S(1)}, u32[]{:S(2)}, u32[]{:S(2)}) %collective-permute-start.10) | collective-permute-done | bytes 4128 | tf_op jit(solution)/shard_map/ppermute | solution.py:458
  111.8 0.0 collective-permute-done.9.side_ref
  111.8 3.4 %lower.1 = bf16[8,16,8,256]{3,2,1,0:T(8,128)(2,1)} custom-call(bf16[16,32,16,128]{3,2,1,0:T(8,128)(2,1)S(1)} %get-tuple-element.23.joined_ref, bf16[1,32,16,128]{3,2,1,0:T(8,128)(2,1)S(1)} %collective-permute-done.8.front_ref, bf16[16,1,16,128]{3,2,1,0:T(8,128)(2,1)S(1)} %collective-permute-done.9.side_ref, ...), custom_call_target="tpu_custom_call" | custom-call | flops 1811939328 | bytes 5000000 | tf_op jit(solution)/shard_map/lower/pallas_call | solution.py:433
  (10 shorter events, 0.0 us)
Async XLA Ops:
  7.5 48.8 %copy-start.3 = (bf16[27,128,128]{2,1,0:T(8,128)(2,1)S(1)}, bf16[27,128,128]{2,1,0:T(8,128)(2,1)}, u32[]{:S(2)}) copy-start(bf16[27,128,128]{2,1,0:T(8,128)(2,1)} %w_ref.3) | copy-start | bytes 2654212
  7.5 67.3 %all-to-all-start = ((bf16[32,264,128]{2,1,0:T(8,128)(2,1)}), bf16[32,264,128]{2,1,0:T(8,128)(2,1)S(1)}, u32[]{:S(2)}, u32[]{:S(2)}) async-start(bf16[32,264,128]{2,1,0:T(8,128)(2,1)} %bitcast.10), calls=%async_computation | async-start | bytes 4325376 | tf_op jit(solution)/shard_map/all_to_all | solution.py:462
  14.3 22.9 %collective-permute-start.7 = (bf16[1,1,16,128]{3,2,1,0:T(8,128)(2,1)S(1)}, bf16[1,1,16,128]{3,2,1,0:T(8,128)(2,1)S(1)}, u32[]{:S(2)}, u32[]{:S(2)}) collective-permute-start(bf16[1,1,16,128]{3,2,1,0:T(8,128)(2,1)S(1)} %get-tuple-element.27), channel_id=1, source_target_pairs={{5,0},{6,1},{7,2},{9,4},{10,5},{11,6},{13,8},{14,9},{15,10},{17,12... | collective-permute-start | bytes 12296 | tf_op jit(solution)/shard_map/ppermute | solution.py:458
  17.3 33.1 %collective-permute-start.6 = (bf16[1,1,16,128]{3,2,1,0:T(8,128)(2,1)S(1)}, bf16[1,1,16,128]{3,2,1,0:T(8,128)(2,1)S(1)}, u32[]{:S(2)}, u32[]{:S(2)}) collective-permute-start(bf16[1,1,16,128]{3,2,1,0:T(8,128)(2,1)S(1)} %get-tuple-element.28), channel_id=1, source_target_pairs={{1,4},{2,5},{3,6},{5,8},{6,9},{7,10},{9,12},{10,13},{11,14},{13,16... | collective-permute-start | bytes 12296 | tf_op jit(solution)/shard_map/ppermute | solution.py:458
  19.8 32.5 %collective-permute-start.5 = (bf16[1,1,16,128]{3,2,1,0:T(8,128)(2,1)S(1)}, bf16[1,1,16,128]{3,2,1,0:T(8,128)(2,1)S(1)}, u32[]{:S(2)}, u32[]{:S(2)}) collective-permute-start(bf16[1,1,16,128]{3,2,1,0:T(8,128)(2,1)S(1)} %get-tuple-element.29), channel_id=1, source_target_pairs={{4,1},{5,2},{6,3},{8,5},{9,6},{10,7},{12,9},{13,10},{14,11},{16,13... | collective-permute-start | bytes 12296 | tf_op jit(solution)/shard_map/ppermute | solution.py:458
  23.8 49.7 %collective-permute-start.4 = (bf16[1,1,16,128]{3,2,1,0:T(8,128)(2,1)S(1)}, bf16[1,1,16,128]{3,2,1,0:T(8,128)(2,1)S(1)}, u32[]{:S(2)}, u32[]{:S(2)}) collective-permute-start(bf16[1,1,16,128]{3,2,1,0:T(8,128)(2,1)S(1)} %get-tuple-element.30), channel_id=1, source_target_pairs={{0,5},{1,6},{2,7},{4,9},{5,10},{6,11},{8,13},{9,14},{10,15},{12,17... | collective-permute-start | bytes 12296 | tf_op jit(solution)/shard_map/ppermute | solution.py:458
  26.6 46.9 %collective-permute-start.2 = (bf16[16,1,16,128]{3,2,1,0:T(8,128)(2,1)S(1)}, bf16[16,1,16,128]{3,2,1,0:T(8,128)(2,1)S(1)}, u32[]{:S(2)}, u32[]{:S(2)}) collective-permute-start(bf16[16,1,16,128]{3,2,1,0:T(8,128)(2,1)S(1)} %get-tuple-element.31.ylast_ref), channel_id=1, source_target_pairs={{0,4},{1,5},{2,6},{3,7},{4,8},{5,9},{6,10},{7,11},{8,12},{9,13},{1... | collective-permute-start | bytes 196616 | tf_op jit(solution)/shard_map/ppermute | solution.py:458
  37.1 36.4 %collective-permute-start.3 = (bf16[16,1,16,128]{3,2,1,0:T(8,128)(2,1)S(1)}, bf16[16,1,16,128]{3,2,1,0:T(8,128)(2,1)S(1)}, u32[]{:S(2)}, u32[]{:S(2)}) collective-permute-start(bf16[16,1,16,128]{3,2,1,0:T(8,128)(2,1)S(1)} %get-tuple-element.32.yfirst_ref), channel_id=1, source_target_pairs={{4,0},{5,1},{6,2},{7,3},{8,4},{9,5},{10,6},{11,7},{12,8},{13,9},{1... | collective-permute-start | bytes 196616 | tf_op jit(solution)/shard_map/ppermute | solution.py:458
  50.5 23.0 %collective-permute-start = (bf16[1,32,16,128]{3,2,1,0:T(8,128)(2,1)S(1)}, bf16[1,32,16,128]{3,2,1,0:T(8,128)(2,1)S(1)}, u32[]{:S(2)}, u32[]{:S(2)}) collective-permute-start(bf16[1,32,16,128]{3,2,1,0:T(8,128)(2,1)S(1)} %get-tuple-element.33.xlast_ref), channel_id=1, source_target_pairs={{0,1},{1,2},{2,3},{4,5},{5,6},{6,7},{8,9},{9,10},{10,11},{12,13},{... | collective-permute-start | bytes 393224 | tf_op jit(solution)/shard_map/ppermute | solution.py:458
  52.4 21.1 %collective-permute-start.1 = (bf16[1,32,16,128]{3,2,1,0:T(8,128)(2,1)S(1)}, bf16[1,32,16,128]{3,2,1,0:T(8,128)(2,1)S(1)}, u32[]{:S(2)}, u32[]{:S(2)}) collective-permute-start(bf16[1,32,16,128]{3,2,1,0:T(8,128)(2,1)S(1)} %get-tuple-element.34.xfirst_ref), channel_id=1, source_target_pairs={{1,0},{2,1},{3,2},{5,4},{6,5},{7,6},{9,8},{10,9},{11,10},{13,12},{... | collective-permute-start | bytes 393224 | tf_op jit(solution)/shard_map/ppermute | solution.py:458
  56.3 1.6 %copy-start.1 = (bf16[16,32,16,128]{3,2,1,0:T(8,128)(2,1)S(1)}, bf16[16,32,16,128]{3,2,1,0:T(8,128)(2,1)}, u32[]{:S(2)}) copy-start(bf16[16,32,16,128]{3,2,1,0:T(8,128)(2,1)} %level_ref) | copy-start | bytes 6291460
  57.9 15.6 %copy-start.4 = (bf16[27,128,128]{2,1,0:T(8,128)(2,1)S(1)}, bf16[27,128,128]{2,1,0:T(8,128)(2,1)}, u32[]{:S(2)}) copy-start(bf16[27,128,128]{2,1,0:T(8,128)(2,1)} %w_ref.3) | copy-start | bytes 2654212
  71.6 1.9 %copy-start = (f32[16,16,2,16,128]{4,3,2,1,0:T(8,128)}, f32[16,16,2,16,128]{4,3,2,1,0:T(8,128)S(1)}, u32[]{:S(2)}) copy-start(f32[16,16,2,16,128]{4,3,2,1,0:T(8,128)S(1)} %get-tuple-element.18) | copy-start | bytes 12582916
  74.9 36.9 %copy-start.2 = (bf16[27,128,256]{2,1,0:T(8,128)(2,1)S(1)}, bf16[27,128,256]{2,1,0:T(8,128)(2,1)}, u32[]{:S(2)}) copy-start(bf16[27,128,256]{2,1,0:T(8,128)(2,1)} %param.11) | copy-start | bytes 5308420
  87.6 24.2 %collective-permute-start.8 = (bf16[1,32,16,128]{3,2,1,0:T(8,128)(2,1)S(1)}, bf16[1,32,16,128]{3,2,1,0:T(8,128)(2,1)S(1)}, u32[]{:S(2)}, u32[]{:S(2)}) collective-permute-start(bf16[1,32,16,128]{3,2,1,0:T(8,128)(2,1)S(1)} %get-tuple-element.24), channel_id=1, source_target_pairs={{0,1},{1,2},{2,3},{4,5},{5,6},{6,7},{8,9},{9,10},{10,11},{12,13},{... | collective-permute-start | bytes 393224 | tf_op jit(solution)/shard_map/ppermute | solution.py:458
  89.5 22.2 %collective-permute-start.9 = (bf16[16,1,16,128]{3,2,1,0:T(8,128)(2,1)S(1)}, bf16[16,1,16,128]{3,2,1,0:T(8,128)(2,1)S(1)}, u32[]{:S(2)}, u32[]{:S(2)}) collective-permute-start(bf16[16,1,16,128]{3,2,1,0:T(8,128)(2,1)S(1)} %get-tuple-element.25), channel_id=1, source_target_pairs={{0,4},{1,5},{2,6},{3,7},{4,8},{5,9},{6,10},{7,11},{8,12},{9,13},{1... | collective-permute-start | bytes 196616 | tf_op jit(solution)/shard_map/ppermute | solution.py:458
  105.1 6.7 %collective-permute-start.10 = (bf16[1,1,16,128]{3,2,1,0:T(8,128)(2,1)S(1)}, bf16[1,1,16,128]{3,2,1,0:T(8,128)(2,1)S(1)}, u32[]{:S(2)}, u32[]{:S(2)}) collective-permute-start(bf16[1,1,16,128]{3,2,1,0:T(8,128)(2,1)S(1)} %get-tuple-element.26), channel_id=1, source_target_pairs={{0,5},{1,6},{2,7},{4,9},{5,10},{6,11},{8,13},{9,14},{10,15},{12,17... | collective-permute-start | bytes 12296 | tf_op jit(solution)/shard_map/ppermute | solution.py:458

commit v7 on v6

--- a/solution.py
+++ b/solution.py
@@ -44,7 +44,13 @@
     copy = pltpu.make_async_copy(slot_vmem, slot_smem, sems.at[PIECES])
     copy.start()
     fetch.wait()
-    wide[...] = rows_ref[...].astype(jnp.float32)
+
+    def widen(i, carry):
+        at = pl.ds(pl.multiple_of(i * 2 * LANES, 16), 2 * LANES)
+        wide[at, :] = rows_ref[at, :].astype(jnp.float32)
+        return carry
+
+    lax.fori_loop(0, p_local // (2 * LANES), widen, 0)
     per = -(-cap // LANES)
     for part in range(2):
         for j in range(per):
@@ -101,7 +107,7 @@
     )(owner.reshape(blocks, LANES), cell.reshape(blocks, LANES), rows)
 
 
-WAYS = 6
+WAYS = 8
 
 
 def add_kernel(capacity, got_ref, base_hbm, ends_ref, edges_ref, out_ref, front_ref, side_ref,
@@ -124,8 +130,16 @@
             high > 0, (high - 1) * LANES + low, cells)
     copy = pltpu.make_async_copy(slot_vmem, slot_smem, sems.at[1])
     copy.start()
+
+    def clear(x, carry):
+        at = pl.ds(pl.multiple_of(x * area, 8), area)
+        for s in sums[1:]:
+            s[at, :] = jnp.zeros((area, channels), jnp.float32)
+        return carry
+
+    lax.fori_loop(0, span_x, clear, 0)
     for s in sums[1:]:
-        s[...] = jnp.zeros_like(s)
+        s[cells:cells + 8, :] = jnp.zeros((8, channels), jnp.float32)
     first.wait()
     for x in range(span_x):
         sums[0][x * area:x * area + span_z, :] = edges_ref[0, x]
@@ -135,14 +149,16 @@
     copy.wait()
     for j in range(per):
         def step(o, carry):
-            start = pl.multiple_of(o * stride + j * LANES, 8)
-            line = slot_smem.at[j * devices + o]
+            lines = [slot_smem.at[j * devices + o * LINES + i] for i in range(LINES)]
+            starts = [pl.multiple_of((o * LINES + i) * stride + j * LANES, 8)
+                      for i in range(LINES)]
             for u in range(width):
-                s = sums[u % len(sums)]
-                s[pl.ds(line[u], 1), :] += wide[pl.ds(start + u, 1), :]
+                for i in range(LINES):
+                    s = sums[(u * LINES + i) % len(sums)]
+                    s[pl.ds(lines[i][u], 1), :] += wide[pl.ds(starts[i] + u, 1), :]
             return carry
 
-        lax.fori_loop(0, devices, step, 0)
+        lax.fori_loop(0, devices // LINES, step, 0)
 
     def finish(x, carry):
         at = pl.ds(pl.multiple_of(x * area, 8), area)

time: 117 us -> 116 us (level)
  no operation moved by 1% of the time
where the time goes in v7:
time: 116 us; the launch traced here: 114 us
  starting transfers between devices  49.5 us (43%)
  Pallas kernels  37.6 us (32%)
  waiting for transfers between devices  20.7 us (18%)
  local copies, waits for them, and re-layouts  6.15 us (5%)
    ppermute x11, starting transfers between devices, shifted(): return lax.ppermute(array, ('pts', 'nbr'), pairs)  43.5 us
    ppermute x11, waiting for transfers between devices, shifted(): return lax.ppermute(array, ('pts', 'nbr'), pairs)  20.7 us
    pallas_call x1, Pallas kernels, residual_base(): pl.pallas_call(functools.partial(residual_kernel, group), out_shape=[jax....  13.6 us
    pallas_call x1, Pallas kernels, add_rows(): pl.pallas_call(functools.partial(add_kernel, capacity), out_shape=[jax.Sh...  11.8 us
    pallas_call x1, Pallas kernels, pack(): pl.pallas_call(functools.partial(pack_kernel, devices, cap), out_shape=ja...  7.5 us
    all_to_all x1, starting transfers between devices, exchanged(): lax.all_to_all(array.reshape(devices, -1, array.shape[-1]), ('pts', 'nbr'...  6 us
    unnamed x10, local copies, waits for them, and re-layouts  3.53 us
    pallas_call x1, Pallas kernels, lower(): pl.pallas_call(lower_kernel, out_shape=jax.ShapeDtypeStruct((span_x // 2,...  3.39 us
  transfers between devices with their start and end apart: 12, of which 3 were waited for; matrix products, arithmetic and copies ran while one was open for 2% of the time, Pallas kernels for 13%

profile of v7, /device:TPU:12, one launch (start us, length us, event | category | flops | bytes accessed | tf_op | source)
XLA Modules:
  0.0 114.1 jit_solution(16572418350243531454)
XLA Ops:
  0.0 7.5 %pack.1 = bf16[8448,128]{1,0:T(8,128)(2,1)} custom-call(s32[32,128]{1,0:T(8,128)} %bitcast.12, s32[32,128]{1,0:T(8,128)} %bitcast.13, bf16[4096,128]{1,0:T(8,128)(2,1)} %bitcast.11), custom_call_target="tpu_custom_call" | custom-call | flops 100000000 | bytes 4000000 | tf_op jit(solution)/shard_map/pack/pallas_call | solution.py:91
  7.5 0.0 copy-start.3
  7.5 6.0 %all-to-all-start = ((bf16[32,264,128]{2,1,0:T(8,128)(2,1)}), bf16[32,264,128]{2,1,0:T(8,128)(2,1)S(1)}, u32[]{:S(2)}, u32[]{:S(2)}) async-start(bf16[32,264,128]{2,1,0:T(8,128)(2,1)} %bitcast.10), calls=%async_computation | async-start | bytes 4325376 | tf_op jit(solution)/shard_map/all_to_all | solution.py:478
  13.5 0.7 fusion
  14.3 3.1 %collective-permute-start.7 = (bf16[1,1,16,128]{3,2,1,0:T(8,128)(2,1)S(1)}, bf16[1,1,16,128]{3,2,1,0:T(8,128)(2,1)S(1)}, u32[]{:S(2)}, u32[]{:S(2)}) collective-permute-start(bf16[1,1,16,128]{3,2,1,0:T(8,128)(2,1)S(1)} %get-tuple-element.27), channel_id=1, source_target_pairs={{5,0},{6,1},{7,2},{9,4},{10,5},{11,6},{13,8},{14,9},{15,10},{17,12... | collective-permute-start | bytes 12296 | tf_op jit(solution)/shard_map/ppermute | solution.py:474
  17.3 2.5 %collective-permute-start.6 = (bf16[1,1,16,128]{3,2,1,0:T(8,128)(2,1)S(1)}, bf16[1,1,16,128]{3,2,1,0:T(8,128)(2,1)S(1)}, u32[]{:S(2)}, u32[]{:S(2)}) collective-permute-start(bf16[1,1,16,128]{3,2,1,0:T(8,128)(2,1)S(1)} %get-tuple-element.28), channel_id=1, source_target_pairs={{1,4},{2,5},{3,6},{5,8},{6,9},{7,10},{9,12},{10,13},{11,14},{13,16... | collective-permute-start | bytes 12296 | tf_op jit(solution)/shard_map/ppermute | solution.py:474
  19.8 4.0 %collective-permute-start.5 = (bf16[1,1,16,128]{3,2,1,0:T(8,128)(2,1)S(1)}, bf16[1,1,16,128]{3,2,1,0:T(8,128)(2,1)S(1)}, u32[]{:S(2)}, u32[]{:S(2)}) collective-permute-start(bf16[1,1,16,128]{3,2,1,0:T(8,128)(2,1)S(1)} %get-tuple-element.29), channel_id=1, source_target_pairs={{4,1},{5,2},{6,3},{8,5},{9,6},{10,7},{12,9},{13,10},{14,11},{16,13... | collective-permute-start | bytes 12296 | tf_op jit(solution)/shard_map/ppermute | solution.py:474
  23.8 1.9 %collective-permute-start.4 = (bf16[1,1,16,128]{3,2,1,0:T(8,128)(2,1)S(1)}, bf16[1,1,16,128]{3,2,1,0:T(8,128)(2,1)S(1)}, u32[]{:S(2)}, u32[]{:S(2)}) collective-permute-start(bf16[1,1,16,128]{3,2,1,0:T(8,128)(2,1)S(1)} %get-tuple-element.30), channel_id=1, source_target_pairs={{0,5},{1,6},{2,7},{4,9},{5,10},{6,11},{8,13},{9,14},{10,15},{12,17... | collective-permute-start | bytes 12296 | tf_op jit(solution)/shard_map/ppermute | solution.py:474
  25.7 0.9 fusion.1
  26.6 2.2 %collective-permute-start.2 = (bf16[16,1,16,128]{3,2,1,0:T(8,128)(2,1)S(1)}, bf16[16,1,16,128]{3,2,1,0:T(8,128)(2,1)S(1)}, u32[]{:S(2)}, u32[]{:S(2)}) collective-permute-start(bf16[16,1,16,128]{3,2,1,0:T(8,128)(2,1)S(1)} %get-tuple-element.31.ylast_ref), channel_id=1, source_target_pairs={{0,4},{1,5},{2,6},{3,7},{4,8},{5,9},{6,10},{7,11},{8,12},{9,13},{1... | collective-permute-start | bytes 196616 | tf_op jit(solution)/shard_map/ppermute | solution.py:474
  28.9 1.0 fusion.2
  29.9 7.3 %collective-permute-done.7.hh_ref = bf16[1,1,16,128]{3,2,1,0:T(8,128)(2,1)S(1)} collective-permute-done((bf16[1,1,16,128]{3,2,1,0:T(8,128)(2,1)S(1)}, bf16[1,1,16,128]{3,2,1,0:T(8,128)(2,1)S(1)}, u32[]{:S(2)}, u32[]{:S(2)}) %collective-permute-start.7) | collective-permute-done | bytes 4128 | tf_op jit(solution)/shard_map/ppermute | solution.py:474
  37.1 4.5 %collective-permute-start.3 = (bf16[16,1,16,128]{3,2,1,0:T(8,128)(2,1)S(1)}, bf16[16,1,16,128]{3,2,1,0:T(8,128)(2,1)S(1)}, u32[]{:S(2)}, u32[]{:S(2)}) collective-permute-start(bf16[16,1,16,128]{3,2,1,0:T(8,128)(2,1)S(1)} %get-tuple-element.32.yfirst_ref), channel_id=1, source_target_pairs={{4,0},{5,1},{6,2},{7,3},{8,4},{9,5},{10,6},{11,7},{12,8},{13,9},{1... | collective-permute-start | bytes 196616 | tf_op jit(solution)/shard_map/ppermute | solution.py:474
  41.6 8.8 %collective-permute-done.6.hl_ref = bf16[1,1,16,128]{3,2,1,0:T(8,128)(2,1)S(1)} collective-permute-done((bf16[1,1,16,128]{3,2,1,0:T(8,128)(2,1)S(1)}, bf16[1,1,16,128]{3,2,1,0:T(8,128)(2,1)S(1)}, u32[]{:S(2)}, u32[]{:S(2)}) %collective-permute-start.6) | collective-permute-done | bytes 4128 | tf_op jit(solution)/shard_map/ppermute | solution.py:474
  50.5 1.9 %collective-permute-start = (bf16[1,32,16,128]{3,2,1,0:T(8,128)(2,1)S(1)}, bf16[1,32,16,128]{3,2,1,0:T(8,128)(2,1)S(1)}, u32[]{:S(2)}, u32[]{:S(2)}) collective-permute-start(bf16[1,32,16,128]{3,2,1,0:T(8,128)(2,1)S(1)} %get-tuple-element.33.xlast_ref), channel_id=1, source_target_pairs={{0,1},{1,2},{2,3},{4,5},{5,6},{6,7},{8,9},{9,10},{10,11},{12,13},{... | collective-permute-start | bytes 393224 | tf_op jit(solution)/shard_map/ppermute | solution.py:474
  52.4 3.9 %collective-permute-start.1 = (bf16[1,32,16,128]{3,2,1,0:T(8,128)(2,1)S(1)}, bf16[1,32,16,128]{3,2,1,0:T(8,128)(2,1)S(1)}, u32[]{:S(2)}, u32[]{:S(2)}) collective-permute-start(bf16[1,32,16,128]{3,2,1,0:T(8,128)(2,1)S(1)} %get-tuple-element.34.xfirst_ref), channel_id=1, source_target_pairs={{1,0},{2,1},{3,2},{5,4},{6,5},{7,6},{9,8},{10,9},{11,10},{13,12},{... | collective-permute-start | bytes 393224 | tf_op jit(solution)/shard_map/ppermute | solution.py:474
  56.3 0.0 copy-start.1
  56.4 1.6 %copy-done.1 = bf16[16,32,16,128]{3,2,1,0:T(8,128)(2,1)S(1)} copy-done((bf16[16,32,16,128]{3,2,1,0:T(8,128)(2,1)S(1)}, bf16[16,32,16,128]{3,2,1,0:T(8,128)(2,1)}, u32[]{:S(2)}) %copy-start.1) | copy-done | bytes 2097176
  57.9 13.6 %residual.1 = (f32[16,16,2,16,128]{4,3,2,1,0:T(8,128)S(1)}, f32[2,16,2,16,128]{4,3,2,1,0:T(8,128)S(1)}, f32[2,16,16,128]{3,2,1,0:T(8,128)S(1)}) custom-call(bf16[16,32,16,128]{3,2,1,0:T(8,128)(2,1)S(1)} %copy-done.1, bf16[27,128,128]{2,1,0:T(8,128)(2,1)S(1)} %copy-done.3), custom_call_target="tpu_custom_call" | custom-call | flops 7247757312 | bytes 8000000 | tf_op jit(solution)/shard_map/residual/pallas_call | solution.py:306
  71.6 1.9 %copy-done = f32[16,16,2,16,128]{4,3,2,1,0:T(8,128)} copy-done((f32[16,16,2,16,128]{4,3,2,1,0:T(8,128)}, f32[16,16,2,16,128]{4,3,2,1,0:T(8,128)S(1)}, u32[]{:S(2)}) %copy-start) | copy-done | bytes 4194328
  73.5 0.0 collective-permute-done.xlow_ref
  73.5 0.0 collective-permute-done.1.xhigh_ref
  73.5 1.3 %border.1 = (f32[2,16,2,16,128]{4,3,2,1,0:T(8,128)S(1)}, f32[2,16,16,128]{3,2,1,0:T(8,128)S(1)}) custom-call(f32[2,16,2,16,128]{4,3,2,1,0:T(8,128)S(1)} %get-tuple-element.19.ends_ref, f32[2,16,16,128]{3,2,1,0:T(8,128)S(1)} %get-tuple-element.20.edges_ref, bf16[1,32,16,128]{3,2,1,0:T(8,128)(2,1)S(1)} %get-tuple-element.34.xfirst_ref, ...), custom_call_target="tpu_custom_call" | custom-call | flops 1000000000 | bytes 3000000 | tf_op jit(solution)/shard_map/border/pallas_call | solution.py:386
  74.8 0.0 all-to-all-done
  74.9 0.0 copy-start.2
  74.9 11.8 %add_rows.1 = (bf16[16,32,16,128]{3,2,1,0:T(8,128)(2,1)S(1)}, bf16[1,32,16,128]{3,2,1,0:T(8,128)(2,1)S(1)}, bf16[16,1,16,128]{3,2,1,0:T(8,128)(2,1)S(1)}, bf16[1,1,16,128]{3,2,1,0:T(8,128)(2,1)S(1)}) custom-call(bf16[8448,128]{1,0:T(8,128)(2,1)S(1)} %bitcast.7, f32[8192,128]{1,0:T(8,128)} %bitcast.8, f32[2,16,2,16,128]{4,3,2,1,0:T(8,128)S(1)} %get-tuple-element.21.ends_ref, ...), custom_call_target="tpu_custom_call" | custom-call | flops 100000000 | bytes 8000000 | tf_op jit(solution)/shard_map/add_rows/pallas_call | solution.py:185
  86.7 1.9 %collective-permute-start.8 = (bf16[1,32,16,128]{3,2,1,0:T(8,128)(2,1)S(1)}, bf16[1,32,16,128]{3,2,1,0:T(8,128)(2,1)S(1)}, u32[]{:S(2)}, u32[]{:S(2)}) collective-permute-start(bf16[1,32,16,128]{3,2,1,0:T(8,128)(2,1)S(1)} %get-tuple-element.24), channel_id=1, source_target_pairs={{0,1},{1,2},{2,3},{4,5},{5,6},{6,7},{8,9},{9,10},{10,11},{12,13},{... | collective-permute-start | bytes 393224 | tf_op jit(solution)/shard_map/ppermute | solution.py:474
  88.6 15.4 %collective-permute-start.9 = (bf16[16,1,16,128]{3,2,1,0:T(8,128)(2,1)S(1)}, bf16[16,1,16,128]{3,2,1,0:T(8,128)(2,1)S(1)}, u32[]{:S(2)}, u32[]{:S(2)}) collective-permute-start(bf16[16,1,16,128]{3,2,1,0:T(8,128)(2,1)S(1)} %get-tuple-element.25), channel_id=1, source_target_pairs={{0,4},{1,5},{2,6},{3,7},{4,8},{5,9},{6,10},{7,11},{8,12},{9,13},{1... | collective-permute-start | bytes 196616 | tf_op jit(solution)/shard_map/ppermute | solution.py:474
  104.0 2.1 %collective-permute-start.10 = (bf16[1,1,16,128]{3,2,1,0:T(8,128)(2,1)S(1)}, bf16[1,1,16,128]{3,2,1,0:T(8,128)(2,1)S(1)}, u32[]{:S(2)}, u32[]{:S(2)}) collective-permute-start(bf16[1,1,16,128]{3,2,1,0:T(8,128)(2,1)S(1)} %get-tuple-element.26), channel_id=1, source_target_pairs={{0,5},{1,6},{2,7},{4,9},{5,10},{6,11},{8,13},{9,14},{10,15},{12,17... | collective-permute-start | bytes 12296 | tf_op jit(solution)/shard_map/ppermute | solution.py:474
  106.2 4.6 %collective-permute-done.10.corner_ref = bf16[1,1,16,128]{3,2,1,0:T(8,128)(2,1)S(1)} collective-permute-done((bf16[1,1,16,128]{3,2,1,0:T(8,128)(2,1)S(1)}, bf16[1,1,16,128]{3,2,1,0:T(8,128)(2,1)S(1)}, u32[]{:S(2)}, u32[]{:S(2)}) %collective-permute-start.10) | collective-permute-done | bytes 4128 | tf_op jit(solution)/shard_map/ppermute | solution.py:474
  110.7 0.0 collective-permute-done.9.side_ref
  110.7 3.4 %lower.1 = bf16[8,16,8,256]{3,2,1,0:T(8,128)(2,1)} custom-call(bf16[16,32,16,128]{3,2,1,0:T(8,128)(2,1)S(1)} %get-tuple-element.23.joined_ref, bf16[1,32,16,128]{3,2,1,0:T(8,128)(2,1)S(1)} %collective-permute-done.8.front_ref, bf16[16,1,16,128]{3,2,1,0:T(8,128)(2,1)S(1)} %collective-permute-done.9.side_ref, ...), custom_call_target="tpu_custom_call" | custom-call | flops 1811939328 | bytes 5000000 | tf_op jit(solution)/shard_map/lower/pallas_call | solution.py:449
  (10 shorter events, 0.0 us)
Async XLA Ops:
  7.5 48.8 %copy-start.3 = (bf16[27,128,128]{2,1,0:T(8,128)(2,1)S(1)}, bf16[27,128,128]{2,1,0:T(8,128)(2,1)}, u32[]{:S(2)}) copy-start(bf16[27,128,128]{2,1,0:T(8,128)(2,1)} %w_ref.3) | copy-start | bytes 2654212
  7.5 67.3 %all-to-all-start = ((bf16[32,264,128]{2,1,0:T(8,128)(2,1)}), bf16[32,264,128]{2,1,0:T(8,128)(2,1)S(1)}, u32[]{:S(2)}, u32[]{:S(2)}) async-start(bf16[32,264,128]{2,1,0:T(8,128)(2,1)} %bitcast.10), calls=%async_computation | async-start | bytes 4325376 | tf_op jit(solution)/shard_map/all_to_all | solution.py:478
  14.3 22.9 %collective-permute-start.7 = (bf16[1,1,16,128]{3,2,1,0:T(8,128)(2,1)S(1)}, bf16[1,1,16,128]{3,2,1,0:T(8,128)(2,1)S(1)}, u32[]{:S(2)}, u32[]{:S(2)}) collective-permute-start(bf16[1,1,16,128]{3,2,1,0:T(8,128)(2,1)S(1)} %get-tuple-element.27), channel_id=1, source_target_pairs={{5,0},{6,1},{7,2},{9,4},{10,5},{11,6},{13,8},{14,9},{15,10},{17,12... | collective-permute-start | bytes 12296 | tf_op jit(solution)/shard_map/ppermute | solution.py:474
  17.3 33.1 %collective-permute-start.6 = (bf16[1,1,16,128]{3,2,1,0:T(8,128)(2,1)S(1)}, bf16[1,1,16,128]{3,2,1,0:T(8,128)(2,1)S(1)}, u32[]{:S(2)}, u32[]{:S(2)}) collective-permute-start(bf16[1,1,16,128]{3,2,1,0:T(8,128)(2,1)S(1)} %get-tuple-element.28), channel_id=1, source_target_pairs={{1,4},{2,5},{3,6},{5,8},{6,9},{7,10},{9,12},{10,13},{11,14},{13,16... | collective-permute-start | bytes 12296 | tf_op jit(solution)/shard_map/ppermute | solution.py:474
  19.8 32.5 %collective-permute-start.5 = (bf16[1,1,16,128]{3,2,1,0:T(8,128)(2,1)S(1)}, bf16[1,1,16,128]{3,2,1,0:T(8,128)(2,1)S(1)}, u32[]{:S(2)}, u32[]{:S(2)}) collective-permute-start(bf16[1,1,16,128]{3,2,1,0:T(8,128)(2,1)S(1)} %get-tuple-element.29), channel_id=1, source_target_pairs={{4,1},{5,2},{6,3},{8,5},{9,6},{10,7},{12,9},{13,10},{14,11},{16,13... | collective-permute-start | bytes 12296 | tf_op jit(solution)/shard_map/ppermute | solution.py:474
  23.8 49.7 %collective-permute-start.4 = (bf16[1,1,16,128]{3,2,1,0:T(8,128)(2,1)S(1)}, bf16[1,1,16,128]{3,2,1,0:T(8,128)(2,1)S(1)}, u32[]{:S(2)}, u32[]{:S(2)}) collective-permute-start(bf16[1,1,16,128]{3,2,1,0:T(8,128)(2,1)S(1)} %get-tuple-element.30), channel_id=1, source_target_pairs={{0,5},{1,6},{2,7},{4,9},{5,10},{6,11},{8,13},{9,14},{10,15},{12,17... | collective-permute-start | bytes 12296 | tf_op jit(solution)/shard_map/ppermute | solution.py:474
  26.6 46.9 %collective-permute-start.2 = (bf16[16,1,16,128]{3,2,1,0:T(8,128)(2,1)S(1)}, bf16[16,1,16,128]{3,2,1,0:T(8,128)(2,1)S(1)}, u32[]{:S(2)}, u32[]{:S(2)}) collective-permute-start(bf16[16,1,16,128]{3,2,1,0:T(8,128)(2,1)S(1)} %get-tuple-element.31.ylast_ref), channel_id=1, source_target_pairs={{0,4},{1,5},{2,6},{3,7},{4,8},{5,9},{6,10},{7,11},{8,12},{9,13},{1... | collective-permute-start | bytes 196616 | tf_op jit(solution)/shard_map/ppermute | solution.py:474
  37.1 36.4 %collective-permute-start.3 = (bf16[16,1,16,128]{3,2,1,0:T(8,128)(2,1)S(1)}, bf16[16,1,16,128]{3,2,1,0:T(8,128)(2,1)S(1)}, u32[]{:S(2)}, u32[]{:S(2)}) collective-permute-start(bf16[16,1,16,128]{3,2,1,0:T(8,128)(2,1)S(1)} %get-tuple-element.32.yfirst_ref), channel_id=1, source_target_pairs={{4,0},{5,1},{6,2},{7,3},{8,4},{9,5},{10,6},{11,7},{12,8},{13,9},{1... | collective-permute-start | bytes 196616 | tf_op jit(solution)/shard_map/ppermute | solution.py:474
  50.5 23.0 %collective-permute-start = (bf16[1,32,16,128]{3,2,1,0:T(8,128)(2,1)S(1)}, bf16[1,32,16,128]{3,2,1,0:T(8,128)(2,1)S(1)}, u32[]{:S(2)}, u32[]{:S(2)}) collective-permute-start(bf16[1,32,16,128]{3,2,1,0:T(8,128)(2,1)S(1)} %get-tuple-element.33.xlast_ref), channel_id=1, source_target_pairs={{0,1},{1,2},{2,3},{4,5},{5,6},{6,7},{8,9},{9,10},{10,11},{12,13},{... | collective-permute-start | bytes 393224 | tf_op jit(solution)/shard_map/ppermute | solution.py:474
  52.4 21.1 %collective-permute-start.1 = (bf16[1,32,16,128]{3,2,1,0:T(8,128)(2,1)S(1)}, bf16[1,32,16,128]{3,2,1,0:T(8,128)(2,1)S(1)}, u32[]{:S(2)}, u32[]{:S(2)}) collective-permute-start(bf16[1,32,16,128]{3,2,1,0:T(8,128)(2,1)S(1)} %get-tuple-element.34.xfirst_ref), channel_id=1, source_target_pairs={{1,0},{2,1},{3,2},{5,4},{6,5},{7,6},{9,8},{10,9},{11,10},{13,12},{... | collective-permute-start | bytes 393224 | tf_op jit(solution)/shard_map/ppermute | solution.py:474
  56.3 1.6 %copy-start.1 = (bf16[16,32,16,128]{3,2,1,0:T(8,128)(2,1)S(1)}, bf16[16,32,16,128]{3,2,1,0:T(8,128)(2,1)}, u32[]{:S(2)}) copy-start(bf16[16,32,16,128]{3,2,1,0:T(8,128)(2,1)} %level_ref) | copy-start | bytes 6291460
  57.9 15.6 %copy-start.4 = (bf16[27,128,128]{2,1,0:T(8,128)(2,1)S(1)}, bf16[27,128,128]{2,1,0:T(8,128)(2,1)}, u32[]{:S(2)}) copy-start(bf16[27,128,128]{2,1,0:T(8,128)(2,1)} %w_ref.3) | copy-start | bytes 2654212
  71.6 1.9 %copy-start = (f32[16,16,2,16,128]{4,3,2,1,0:T(8,128)}, f32[16,16,2,16,128]{4,3,2,1,0:T(8,128)S(1)}, u32[]{:S(2)}) copy-start(f32[16,16,2,16,128]{4,3,2,1,0:T(8,128)S(1)} %get-tuple-element.18) | copy-start | bytes 12582916
  74.9 35.9 %copy-start.2 = (bf16[27,128,256]{2,1,0:T(8,128)(2,1)S(1)}, bf16[27,128,256]{2,1,0:T(8,128)(2,1)}, u32[]{:S(2)}) copy-start(bf16[27,128,256]{2,1,0:T(8,128)(2,1)} %param.11) | copy-start | bytes 5308420
  86.7 24.1 %collective-permute-start.8 = (bf16[1,32,16,128]{3,2,1,0:T(8,128)(2,1)S(1)}, bf16[1,32,16,128]{3,2,1,0:T(8,128)(2,1)S(1)}, u32[]{:S(2)}, u32[]{:S(2)}) collective-permute-start(bf16[1,32,16,128]{3,2,1,0:T(8,128)(2,1)S(1)} %get-tuple-element.24), channel_id=1, source_target_pairs={{0,1},{1,2},{2,3},{4,5},{5,6},{6,7},{8,9},{9,10},{10,11},{12,13},{... | collective-permute-start | bytes 393224 | tf_op jit(solution)/shard_map/ppermute | solution.py:474
  88.6 22.1 %collective-permute-start.9 = (bf16[16,1,16,128]{3,2,1,0:T(8,128)(2,1)S(1)}, bf16[16,1,16,128]{3,2,1,0:T(8,128)(2,1)S(1)}, u32[]{:S(2)}, u32[]{:S(2)}) collective-permute-start(bf16[16,1,16,128]{3,2,1,0:T(8,128)(2,1)S(1)} %get-tuple-element.25), channel_id=1, source_target_pairs={{0,4},{1,5},{2,6},{3,7},{4,8},{5,9},{6,10},{7,11},{8,12},{9,13},{1... | collective-permute-start | bytes 196616 | tf_op jit(solution)/shard_map/ppermute | solution.py:474
  104.0 6.7 %collective-permute-start.10 = (bf16[1,1,16,128]{3,2,1,0:T(8,128)(2,1)S(1)}, bf16[1,1,16,128]{3,2,1,0:T(8,128)(2,1)S(1)}, u32[]{:S(2)}, u32[]{:S(2)}) collective-permute-start(bf16[1,1,16,128]{3,2,1,0:T(8,128)(2,1)S(1)} %get-tuple-element.26), channel_id=1, source_target_pairs={{0,5},{1,6},{2,7},{4,9},{5,10},{6,11},{8,13},{9,14},{10,15},{12,17... | collective-permute-start | bytes 12296 | tf_op jit(solution)/shard_map/ppermute | solution.py:474

commit v8 on v7

--- a/solution.py
+++ b/solution.py
@@ -400,49 +400,122 @@
     )(ends, edges, *own, *faces, w_res)
 
 
-def lower_kernel(joined_ref, front_ref, side_ref, corner_ref, w_ref, out_ref, planes, taps):
+def fill_taps(plane, store, zero, half_y, half_z):
+    channels = plane.shape[-1]
+    span_y = 2 * half_y
+    rows = (span_y + 1) * half_z
+    low = jnp.where(zero, 0.0, plane[pl.ds(7, rows, stride=2), :])
+    for c, value in enumerate((low, plane[pl.ds(8, rows, stride=2), :],
+                               plane[pl.ds(9, rows, stride=2), :])):
+        value = value.reshape(span_y + 1, half_z, channels)
+        evens = value[0:span_y].reshape(half_y, 2, half_z, channels)
+        odds = value[1:].reshape(half_y, 2, half_z, channels)
+        for b, piece in enumerate((evens[:, 0], evens[:, 1], odds[:, 1])):
+            at = (b * 3 + c) * channels
+            store(at, piece.reshape(half_y * half_z, channels).astype(jnp.bfloat16))
+
+
+def taps_kernel(joined_ref, taps_ref, planes):
     span_x, span_y, span_z, channels = joined_ref.shape
     half_y, half_z = span_y // 2, span_z // 2
-    lines = half_y * half_z
+    count = (span_y + 1) * span_z
+    rows = (span_y + 1) * half_z
+    zero = lax.broadcasted_iota(jnp.int32, (rows, channels), 0) % half_z == 0
+    for k in range(2):
+        planes[k, 0:8 + span_z, :] = jnp.zeros((8 + span_z, channels), jnp.float32)
+    for x in range(span_x):
+        plane = planes.at[x % 2]
+        plane[8 + span_z:8 + count, :] = joined_ref[x].reshape(
+            span_y * span_z, channels).astype(jnp.float32)
+
+        def store(at, value):
+            taps_ref[x % 2, x // 2, :, at:at + channels] = value
+
+        fill_taps(plane, store, zero, half_y, half_z)
+
+
+def local_taps(joined):
+    span_x, span_y, span_z, channels = joined.shape
+    vm = pl.BlockSpec(memory_space=pltpu.VMEM)
+    return pl.pallas_call(
+        taps_kernel,
+        out_shape=jax.ShapeDtypeStruct(
+            (2, span_x // 2, span_y * span_z // 4, 9 * channels), jnp.bfloat16),
+        in_specs=[vm],
+        out_specs=vm,
+        scratch_shapes=[pltpu.VMEM((2, (span_y + 1) * span_z + 16, channels), jnp.float32)],
+        compiler_params=pltpu.CompilerParams(vmem_limit_bytes=8 * 2**20),
+        name="local_taps",
+        cost_estimate=pl.CostEstimate(flops=10**7, bytes_accessed=7 * 10**6, transcendentals=0),
+    )(joined)
+
+
+GROUPS = 2
+
+
+def lower_kernel(taps_ref, front_ref, side_ref, corner_ref, w_ref, out_ref, plane, front_taps,
+                 side_taps):
+    _, span_y, span_z, channels = front_ref.shape
+    span_x = side_ref.shape[0]
+    half_x, half_y, half_z = span_x // 2, span_y // 2, span_z // 2
     count = (span_y + 1) * span_z
     rows = (span_y + 1) * half_z
     depth = 9 * channels
+    wide = w_ref.shape[-1]
     zero = lax.broadcasted_iota(jnp.int32, (rows, channels), 0) % half_z == 0
-    for k in range(2):
-        planes[k, 0:8, :] = jnp.zeros((8, channels), jnp.float32)
-
-    def fill(x, first, rest):
-        plane = planes.at[x % 2]
-        plane[8:8 + span_z, :] = first.reshape(span_z, channels).astype(jnp.float32)
-        plane[8 + span_z:8 + count, :] = rest.reshape(
-            span_y * span_z, channels).astype(jnp.float32)
-        low = jnp.where(zero, 0.0, plane[pl.ds(7, rows, stride=2), :])
-        for c, value in enumerate((low, plane[pl.ds(8, rows, stride=2), :],
-                                   plane[pl.ds(9, rows, stride=2), :])):
-            value = value.reshape(span_y + 1, half_z, channels)
-            evens = value[0:span_y].reshape(half_y, 2, half_z, channels)
-            odds = value[1:].reshape(half_y, 2, half_z, channels)
-            for b, piece in enumerate((evens[:, 0], evens[:, 1], odds[:, 1])):
-                at = (b * 3 + c) * channels
-                taps[x, :, at:at + channels] = piece.reshape(lines, channels).astype(jnp.bfloat16)
-
-    def multiply(i):
-        total = None
-        for a in range(3):
-            part = jnp.dot(taps[2 * i + a], w_ref[a * depth:(a + 1) * depth, :],
-                           preferred_element_type=jnp.float32)
-            total = part if total is None else total + part
-        out_ref[i] = total.reshape(half_y, half_z, w_ref.shape[-1]).astype(jnp.bfloat16)
-
-    fill(0, corner_ref[...], front_ref[...])
-    for x in range(1, span_x + 1):
-        fill(x, side_ref[x - 1], joined_ref[x - 1])
-        if x % 2 == 0:
-            multiply(x // 2 - 1)
-
-
-def lower(joined, front, side, corner, w_down):
-    span_x, span_y, span_z, channels = joined.shape
+    plane[0:8, :] = jnp.zeros((8, channels), jnp.float32)
+    plane[8:8 + span_x * span_z, :] = side_ref[...].reshape(
+        span_x * span_z, channels).astype(jnp.float32)
+    lines = span_x * half_z
+    low = jnp.where(zero[0:lines], 0.0, plane[pl.ds(7, lines, stride=2), :])
+    for c, value in enumerate((low, plane[pl.ds(8, lines, stride=2), :],
+                               plane[pl.ds(9, lines, stride=2), :])):
+        value = value.reshape(half_x, 2, half_z, channels)
+        even = value[:, 0].reshape(half_x * half_z, channels)
+        odd = value[:, 1].reshape(half_x * half_z, channels)
+        before = jnp.concatenate(
+            [jnp.zeros((half_z, channels), jnp.float32), odd[:(half_x - 1) * half_z]], axis=0)
+        for a, piece in enumerate((before, even, odd)):
+            side_taps[a, :, c * channels:(c + 1) * channels] = piece.astype(jnp.bfloat16)
+    change = None
+    for a in range(3):
+        part = jnp.dot(side_taps[a], w_ref[a * depth:a * depth + 3 * channels, :],
+                       preferred_element_type=jnp.float32)
+        change = part if change is None else change + part
+    change = change.reshape(half_x, half_z, wide)
+    plane[8:8 + span_z, :] = corner_ref[...].reshape(span_z, channels).astype(jnp.float32)
+    plane[8 + span_z:8 + count, :] = front_ref[...].reshape(
+        span_y * span_z, channels).astype(jnp.float32)
+
+    def store(at, value):
+        front_taps[:, at:at + channels] = value
+
+    fill_taps(plane, store, zero, half_y, half_z)
+    lines = half_y * half_z
+    group = half_x // GROUPS
+
+    def product(piece, a):
+        return jnp.dot(piece.reshape(-1, depth), w_ref[a * depth:(a + 1) * depth, :],
+                       preferred_element_type=jnp.float32)
+
+    for g in range(GROUPS):
+        first = g * group
+        total = (product(taps_ref[0, first:first + group], 1)
+                 + product(taps_ref[1, first:first + group], 2))
+        if g == 0:
+            total = total + jnp.concatenate(
+                [product(front_taps[...], 0), product(taps_ref[1, 0:group - 1], 0)], axis=0)
+        else:
+            total = total + product(taps_ref[1, first - 1:first + group - 1], 0)
+        total = total.reshape(group, half_y, half_z, wide)
+        out_ref[first:first + group, 1:] = total[:, 1:].astype(jnp.bfloat16)
+        out_ref[first:first + group, 0] = (
+            total[:, 0] + change[first:first + group]).astype(jnp.bfloat16)
+
+
+def lower(taps, front, side, corner, w_down):
+    span_x = side.shape[0]
+    _, span_y, span_z, channels = front.shape
     wide = w_down.shape[-1]
     vm = pl.BlockSpec(memory_space=pltpu.VMEM)
     flops = 2 * span_x * span_y * span_z // 8 * 27 * channels * wide
@@ -453,13 +526,14 @@
         in_specs=[vm] * 5,
         out_specs=vm,
         scratch_shapes=[
-            pltpu.VMEM((2, (span_y + 1) * span_z + 16, channels), jnp.float32),
-            pltpu.VMEM((span_x + 1, span_y * span_z // 4, 9 * channels), jnp.bfloat16),
+            pltpu.VMEM((max(span_y + 1, span_x) * span_z + 16, channels), jnp.float32),
+            pltpu.VMEM((span_y * span_z // 4, 9 * channels), jnp.bfloat16),
+            pltpu.VMEM((3, span_x * span_z // 4, 3 * channels), jnp.bfloat16),
         ],
         compiler_params=pltpu.CompilerParams(vmem_limit_bytes=28 * 2**20),
         name="lower",
         cost_estimate=pl.CostEstimate(flops=flops, bytes_accessed=5 * 10**6, transcendentals=0),
-    )(joined, front, side, corner, w_down.reshape(-1, wide))
+    )(taps, front, side, corner, w_down.reshape(-1, wide))
 
 
 def shifted(array, by_pts, by_nbr):
@@ -512,7 +586,7 @@
     front = shifted(front, 0, 1)
     side = shifted(side, 1, 0)
     corner = shifted(corner, 1, 1)
-    return lower(joined, front, side, corner, w_down)
+    return lower(local_taps(joined), front, side, corner, w_down)
 
 
 def solution(mesh):

time: 116 us -> 116 us (level)
  transfers between devices with their start and end apart: 12 -> 12, of which waited for: 3 -> 3; matrix products, arithmetic and copies ran while one was open for 2% -> 2% of each run, Pallas kernels for 13% -> 14%
where the time goes in v8:
time: 116 us; the launch traced here: 114 us
  starting transfers between devices  49.5 us (43%)
  Pallas kernels  38.2 us (33%)
  waiting for transfers between devices  19.7 us (17%)
  local copies, waits for them, and re-layouts  6.15 us (5%)
    ppermute x11, starting transfers between devices, shifted(): return lax.ppermute(array, ('pts', 'nbr'), pairs)  43.5 us
    ppermute x11, waiting for transfers between devices, shifted(): return lax.ppermute(array, ('pts', 'nbr'), pairs)  19.7 us
    pallas_call x1, Pallas kernels, residual_base(): pl.pallas_call(functools.partial(residual_kernel, group), out_shape=[jax....  13.6 us
    pallas_call x1, Pallas kernels, add_rows(): pl.pallas_call(functools.partial(add_kernel, capacity), out_shape=[jax.Sh...  11.7 us
    pallas_call x1, Pallas kernels, pack(): pl.pallas_call(functools.partial(pack_kernel, devices, cap), out_shape=ja...  7.5 us
    all_to_all x1, starting transfers between devices, exchanged(): lax.all_to_all(array.reshape(devices, -1, array.shape[-1]), ('pts', 'nbr'...  6 us
    unnamed x10, local copies, waits for them, and re-layouts  3.53 us
    pallas_call x1, Pallas kernels, lower(): pl.pallas_call(lower_kernel, out_shape=jax.ShapeDtypeStruct((span_x // 2,...  3.13 us
  transfers between devices with their start and end apart: 12, of which 3 were waited for; matrix products, arithmetic and copies ran while one was open for 2% of the time, Pallas kernels for 14%

profile of v8, /device:TPU:12, one launch (start us, length us, event | category | flops | bytes accessed | tf_op | source)
XLA Modules:
  0.0 113.7 jit_solution(4701897878876095966)
XLA Ops:
  0.0 7.5 %pack.1 = bf16[8448,128]{1,0:T(8,128)(2,1)} custom-call(s32[32,128]{1,0:T(8,128)} %bitcast.12, s32[32,128]{1,0:T(8,128)} %bitcast.13, bf16[4096,128]{1,0:T(8,128)(2,1)} %bitcast.11), custom_call_target="tpu_custom_call" | custom-call | flops 100000000 | bytes 4000000 | tf_op jit(solution)/shard_map/pack/pallas_call | solution.py:91
  7.5 0.0 copy-start.3
  7.5 6.0 %all-to-all-start = ((bf16[32,264,128]{2,1,0:T(8,128)(2,1)}), bf16[32,264,128]{2,1,0:T(8,128)(2,1)S(1)}, u32[]{:S(2)}, u32[]{:S(2)}) async-start(bf16[32,264,128]{2,1,0:T(8,128)(2,1)} %bitcast.10), calls=%async_computation | async-start | bytes 4325376 | tf_op jit(solution)/shard_map/all_to_all | solution.py:552
  13.5 0.7 fusion
  14.3 3.1 %collective-permute-start.7 = (bf16[1,1,16,128]{3,2,1,0:T(8,128)(2,1)S(1)}, bf16[1,1,16,128]{3,2,1,0:T(8,128)(2,1)S(1)}, u32[]{:S(2)}, u32[]{:S(2)}) collective-permute-start(bf16[1,1,16,128]{3,2,1,0:T(8,128)(2,1)S(1)} %get-tuple-element.27), channel_id=1, source_target_pairs={{5,0},{6,1},{7,2},{9,4},{10,5},{11,6},{13,8},{14,9},{15,10},{17,12... | collective-permute-start | bytes 12296 | tf_op jit(solution)/shard_map/ppermute | solution.py:548
  17.3 2.5 %collective-permute-start.6 = (bf16[1,1,16,128]{3,2,1,0:T(8,128)(2,1)S(1)}, bf16[1,1,16,128]{3,2,1,0:T(8,128)(2,1)S(1)}, u32[]{:S(2)}, u32[]{:S(2)}) collective-permute-start(bf16[1,1,16,128]{3,2,1,0:T(8,128)(2,1)S(1)} %get-tuple-element.28), channel_id=1, source_target_pairs={{1,4},{2,5},{3,6},{5,8},{6,9},{7,10},{9,12},{10,13},{11,14},{13,16... | collective-permute-start | bytes 12296 | tf_op jit(solution)/shard_map/ppermute | solution.py:548
  19.8 4.0 %collective-permute-start.5 = (bf16[1,1,16,128]{3,2,1,0:T(8,128)(2,1)S(1)}, bf16[1,1,16,128]{3,2,1,0:T(8,128)(2,1)S(1)}, u32[]{:S(2)}, u32[]{:S(2)}) collective-permute-start(bf16[1,1,16,128]{3,2,1,0:T(8,128)(2,1)S(1)} %get-tuple-element.29), channel_id=1, source_target_pairs={{4,1},{5,2},{6,3},{8,5},{9,6},{10,7},{12,9},{13,10},{14,11},{16,13... | collective-permute-start | bytes 12296 | tf_op jit(solution)/shard_map/ppermute | solution.py:548
  23.8 1.9 %collective-permute-start.4 = (bf16[1,1,16,128]{3,2,1,0:T(8,128)(2,1)S(1)}, bf16[1,1,16,128]{3,2,1,0:T(8,128)(2,1)S(1)}, u32[]{:S(2)}, u32[]{:S(2)}) collective-permute-start(bf16[1,1,16,128]{3,2,1,0:T(8,128)(2,1)S(1)} %get-tuple-element.30), channel_id=1, source_target_pairs={{0,5},{1,6},{2,7},{4,9},{5,10},{6,11},{8,13},{9,14},{10,15},{12,17... | collective-permute-start | bytes 12296 | tf_op jit(solution)/shard_map/ppermute | solution.py:548
  25.7 0.9 fusion.1
  26.6 2.2 %collective-permute-start.2 = (bf16[16,1,16,128]{3,2,1,0:T(8,128)(2,1)S(1)}, bf16[16,1,16,128]{3,2,1,0:T(8,128)(2,1)S(1)}, u32[]{:S(2)}, u32[]{:S(2)}) collective-permute-start(bf16[16,1,16,128]{3,2,1,0:T(8,128)(2,1)S(1)} %get-tuple-element.31.ylast_ref), channel_id=1, source_target_pairs={{0,4},{1,5},{2,6},{3,7},{4,8},{5,9},{6,10},{7,11},{8,12},{9,13},{1... | collective-permute-start | bytes 196616 | tf_op jit(solution)/shard_map/ppermute | solution.py:548
  28.9 1.0 fusion.2
  29.9 7.3 %collective-permute-done.7.hh_ref = bf16[1,1,16,128]{3,2,1,0:T(8,128)(2,1)S(1)} collective-permute-done((bf16[1,1,16,128]{3,2,1,0:T(8,128)(2,1)S(1)}, bf16[1,1,16,128]{3,2,1,0:T(8,128)(2,1)S(1)}, u32[]{:S(2)}, u32[]{:S(2)}) %collective-permute-start.7) | collective-permute-done | bytes 4128 | tf_op jit(solution)/shard_map/ppermute | solution.py:548
  37.1 4.5 %collective-permute-start.3 = (bf16[16,1,16,128]{3,2,1,0:T(8,128)(2,1)S(1)}, bf16[16,1,16,128]{3,2,1,0:T(8,128)(2,1)S(1)}, u32[]{:S(2)}, u32[]{:S(2)}) collective-permute-start(bf16[16,1,16,128]{3,2,1,0:T(8,128)(2,1)S(1)} %get-tuple-element.32.yfirst_ref), channel_id=1, source_target_pairs={{4,0},{5,1},{6,2},{7,3},{8,4},{9,5},{10,6},{11,7},{12,8},{13,9},{1... | collective-permute-start | bytes 196616 | tf_op jit(solution)/shard_map/ppermute | solution.py:548
  41.6 8.8 %collective-permute-done.6.hl_ref = bf16[1,1,16,128]{3,2,1,0:T(8,128)(2,1)S(1)} collective-permute-done((bf16[1,1,16,128]{3,2,1,0:T(8,128)(2,1)S(1)}, bf16[1,1,16,128]{3,2,1,0:T(8,128)(2,1)S(1)}, u32[]{:S(2)}, u32[]{:S(2)}) %collective-permute-start.6) | collective-permute-done | bytes 4128 | tf_op jit(solution)/shard_map/ppermute | solution.py:548
  50.5 1.9 %collective-permute-start = (bf16[1,32,16,128]{3,2,1,0:T(8,128)(2,1)S(1)}, bf16[1,32,16,128]{3,2,1,0:T(8,128)(2,1)S(1)}, u32[]{:S(2)}, u32[]{:S(2)}) collective-permute-start(bf16[1,32,16,128]{3,2,1,0:T(8,128)(2,1)S(1)} %get-tuple-element.33.xlast_ref), channel_id=1, source_target_pairs={{0,1},{1,2},{2,3},{4,5},{5,6},{6,7},{8,9},{9,10},{10,11},{12,13},{... | collective-permute-start | bytes 393224 | tf_op jit(solution)/shard_map/ppermute | solution.py:548
  52.4 3.9 %collective-permute-start.1 = (bf16[1,32,16,128]{3,2,1,0:T(8,128)(2,1)S(1)}, bf16[1,32,16,128]{3,2,1,0:T(8,128)(2,1)S(1)}, u32[]{:S(2)}, u32[]{:S(2)}) collective-permute-start(bf16[1,32,16,128]{3,2,1,0:T(8,128)(2,1)S(1)} %get-tuple-element.34.xfirst_ref), channel_id=1, source_target_pairs={{1,0},{2,1},{3,2},{5,4},{6,5},{7,6},{9,8},{10,9},{11,10},{13,12},{... | collective-permute-start | bytes 393224 | tf_op jit(solution)/shard_map/ppermute | solution.py:548
  56.3 0.0 copy-start.2
  56.4 1.6 %copy-done.2 = bf16[16,32,16,128]{3,2,1,0:T(8,128)(2,1)S(1)} copy-done((bf16[16,32,16,128]{3,2,1,0:T(8,128)(2,1)S(1)}, bf16[16,32,16,128]{3,2,1,0:T(8,128)(2,1)}, u32[]{:S(2)}) %copy-start.2) | copy-done | bytes 2097176
  57.9 13.6 %residual.1 = (f32[16,16,2,16,128]{4,3,2,1,0:T(8,128)S(1)}, f32[2,16,2,16,128]{4,3,2,1,0:T(8,128)S(1)}, f32[2,16,16,128]{3,2,1,0:T(8,128)S(1)}) custom-call(bf16[16,32,16,128]{3,2,1,0:T(8,128)(2,1)S(1)} %copy-done.2, bf16[27,128,128]{2,1,0:T(8,128)(2,1)S(1)} %copy-done.3), custom_call_target="tpu_custom_call" | custom-call | flops 7247757312 | bytes 8000000 | tf_op jit(solution)/shard_map/residual/pallas_call | solution.py:306
  71.6 1.9 %copy-done = f32[16,16,2,16,128]{4,3,2,1,0:T(8,128)} copy-done((f32[16,16,2,16,128]{4,3,2,1,0:T(8,128)}, f32[16,16,2,16,128]{4,3,2,1,0:T(8,128)S(1)}, u32[]{:S(2)}) %copy-start) | copy-done | bytes 4194328
  73.5 0.0 collective-permute-done.xlow_ref
  73.5 0.0 collective-permute-done.1.xhigh_ref
  73.5 1.3 %border.1 = (f32[2,16,2,16,128]{4,3,2,1,0:T(8,128)S(1)}, f32[2,16,16,128]{3,2,1,0:T(8,128)S(1)}) custom-call(f32[2,16,2,16,128]{4,3,2,1,0:T(8,128)S(1)} %get-tuple-element.19.ends_ref, f32[2,16,16,128]{3,2,1,0:T(8,128)S(1)} %get-tuple-element.20.edges_ref, bf16[1,32,16,128]{3,2,1,0:T(8,128)(2,1)S(1)} %get-tuple-element.34.xfirst_ref, ...), custom_call_target="tpu_custom_call" | custom-call | flops 1000000000 | bytes 3000000 | tf_op jit(solution)/shard_map/border/pallas_call | solution.py:386
  74.8 0.0 all-to-all-done
  74.9 11.7 %add_rows.1 = (bf16[16,32,16,128]{3,2,1,0:T(8,128)(2,1)S(1)}, bf16[1,32,16,128]{3,2,1,0:T(8,128)(2,1)S(1)}, bf16[16,1,16,128]{3,2,1,0:T(8,128)(2,1)S(1)}, bf16[1,1,16,128]{3,2,1,0:T(8,128)(2,1)S(1)}) custom-call(bf16[8448,128]{1,0:T(8,128)(2,1)S(1)} %bitcast.7, f32[8192,128]{1,0:T(8,128)} %bitcast.8, f32[2,16,2,16,128]{4,3,2,1,0:T(8,128)S(1)} %get-tuple-element.21.ends_ref, ...), custom_call_target="tpu_custom_call" | custom-call | flops 100000000 | bytes 8000000 | tf_op jit(solution)/shard_map/add_rows/pallas_call | solution.py:185
  86.5 1.9 %collective-permute-start.8 = (bf16[1,32,16,128]{3,2,1,0:T(8,128)(2,1)S(1)}, bf16[1,32,16,128]{3,2,1,0:T(8,128)(2,1)S(1)}, u32[]{:S(2)}, u32[]{:S(2)}) collective-permute-start(bf16[1,32,16,128]{3,2,1,0:T(8,128)(2,1)S(1)} %get-tuple-element.24), channel_id=1, source_target_pairs={{0,1},{1,2},{2,3},{4,5},{5,6},{6,7},{8,9},{9,10},{10,11},{12,13},{... | collective-permute-start | bytes 393224 | tf_op jit(solution)/shard_map/ppermute | solution.py:548
  88.5 15.4 %collective-permute-start.9 = (bf16[16,1,16,128]{3,2,1,0:T(8,128)(2,1)S(1)}, bf16[16,1,16,128]{3,2,1,0:T(8,128)(2,1)S(1)}, u32[]{:S(2)}, u32[]{:S(2)}) collective-permute-start(bf16[16,1,16,128]{3,2,1,0:T(8,128)(2,1)S(1)} %get-tuple-element.25), channel_id=1, source_target_pairs={{0,4},{1,5},{2,6},{3,7},{4,8},{5,9},{6,10},{7,11},{8,12},{9,13},{1... | collective-permute-start | bytes 196616 | tf_op jit(solution)/shard_map/ppermute | solution.py:548
  103.9 2.1 %collective-permute-start.10 = (bf16[1,1,16,128]{3,2,1,0:T(8,128)(2,1)S(1)}, bf16[1,1,16,128]{3,2,1,0:T(8,128)(2,1)S(1)}, u32[]{:S(2)}, u32[]{:S(2)}) collective-permute-start(bf16[1,1,16,128]{3,2,1,0:T(8,128)(2,1)S(1)} %get-tuple-element.26), channel_id=1, source_target_pairs={{0,5},{1,6},{2,7},{4,9},{5,10},{6,11},{8,13},{9,14},{10,15},{12,17... | collective-permute-start | bytes 12296 | tf_op jit(solution)/shard_map/ppermute | solution.py:548
  106.0 0.0 copy-start.1
  106.0 1.0 local_taps.1.taps_ref
  107.1 3.5 %collective-permute-done.10.corner_ref = bf16[1,1,16,128]{3,2,1,0:T(8,128)(2,1)S(1)} collective-permute-done((bf16[1,1,16,128]{3,2,1,0:T(8,128)(2,1)S(1)}, bf16[1,1,16,128]{3,2,1,0:T(8,128)(2,1)S(1)}, u32[]{:S(2)}, u32[]{:S(2)}) %collective-permute-start.10) | collective-permute-done | bytes 4128 | tf_op jit(solution)/shard_map/ppermute | solution.py:548
  110.6 3.1 %lower.1 = bf16[8,16,8,256]{3,2,1,0:T(8,128)(2,1)} custom-call(bf16[2,8,128,1152]{3,2,1,0:T(8,128)(2,1)S(1)} %local_taps.1.taps_ref, bf16[1,32,16,128]{3,2,1,0:T(8,128)(2,1)S(1)} %collective-permute-done.8.front_ref, bf16[16,1,16,128]{3,2,1,0:T(8,128)(2,1)S(1)} %collective-permute-done.9.side_ref, ...), custom_call_target="tpu_custom_call" | custom-call | flops 1811939328 | bytes 5000000 | tf_op jit(solution)/shard_map/lower/pallas_call | solution.py:522
  (11 shorter events, 0.0 us)
Async XLA Ops:
  7.5 48.8 %copy-start.3 = (bf16[27,128,128]{2,1,0:T(8,128)(2,1)S(1)}, bf16[27,128,128]{2,1,0:T(8,128)(2,1)}, u32[]{:S(2)}) copy-start(bf16[27,128,128]{2,1,0:T(8,128)(2,1)} %w_ref.3) | copy-start | bytes 2654212
  7.5 67.3 %all-to-all-start = ((bf16[32,264,128]{2,1,0:T(8,128)(2,1)}), bf16[32,264,128]{2,1,0:T(8,128)(2,1)S(1)}, u32[]{:S(2)}, u32[]{:S(2)}) async-start(bf16[32,264,128]{2,1,0:T(8,128)(2,1)} %bitcast.10), calls=%async_computation | async-start | bytes 4325376 | tf_op jit(solution)/shard_map/all_to_all | solution.py:552
  14.3 22.9 %collective-permute-start.7 = (bf16[1,1,16,128]{3,2,1,0:T(8,128)(2,1)S(1)}, bf16[1,1,16,128]{3,2,1,0:T(8,128)(2,1)S(1)}, u32[]{:S(2)}, u32[]{:S(2)}) collective-permute-start(bf16[1,1,16,128]{3,2,1,0:T(8,128)(2,1)S(1)} %get-tuple-element.27), channel_id=1, source_target_pairs={{5,0},{6,1},{7,2},{9,4},{10,5},{11,6},{13,8},{14,9},{15,10},{17,12... | collective-permute-start | bytes 12296 | tf_op jit(solution)/shard_map/ppermute | solution.py:548
  17.3 33.1 %collective-permute-start.6 = (bf16[1,1,16,128]{3,2,1,0:T(8,128)(2,1)S(1)}, bf16[1,1,16,128]{3,2,1,0:T(8,128)(2,1)S(1)}, u32[]{:S(2)}, u32[]{:S(2)}) collective-permute-start(bf16[1,1,16,128]{3,2,1,0:T(8,128)(2,1)S(1)} %get-tuple-element.28), channel_id=1, source_target_pairs={{1,4},{2,5},{3,6},{5,8},{6,9},{7,10},{9,12},{10,13},{11,14},{13,16... | collective-permute-start | bytes 12296 | tf_op jit(solution)/shard_map/ppermute | solution.py:548
  19.8 32.5 %collective-permute-start.5 = (bf16[1,1,16,128]{3,2,1,0:T(8,128)(2,1)S(1)}, bf16[1,1,16,128]{3,2,1,0:T(8,128)(2,1)S(1)}, u32[]{:S(2)}, u32[]{:S(2)}) collective-permute-start(bf16[1,1,16,128]{3,2,1,0:T(8,128)(2,1)S(1)} %get-tuple-element.29), channel_id=1, source_target_pairs={{4,1},{5,2},{6,3},{8,5},{9,6},{10,7},{12,9},{13,10},{14,11},{16,13... | collective-permute-start | bytes 12296 | tf_op jit(solution)/shard_map/ppermute | solution.py:548
  23.8 49.7 %collective-permute-start.4 = (bf16[1,1,16,128]{3,2,1,0:T(8,128)(2,1)S(1)}, bf16[1,1,16,128]{3,2,1,0:T(8,128)(2,1)S(1)}, u32[]{:S(2)}, u32[]{:S(2)}) collective-permute-start(bf16[1,1,16,128]{3,2,1,0:T(8,128)(2,1)S(1)} %get-tuple-element.30), channel_id=1, source_target_pairs={{0,5},{1,6},{2,7},{4,9},{5,10},{6,11},{8,13},{9,14},{10,15},{12,17... | collective-permute-start | bytes 12296 | tf_op jit(solution)/shard_map/ppermute | solution.py:548
  26.6 46.9 %collective-permute-start.2 = (bf16[16,1,16,128]{3,2,1,0:T(8,128)(2,1)S(1)}, bf16[16,1,16,128]{3,2,1,0:T(8,128)(2,1)S(1)}, u32[]{:S(2)}, u32[]{:S(2)}) collective-permute-start(bf16[16,1,16,128]{3,2,1,0:T(8,128)(2,1)S(1)} %get-tuple-element.31.ylast_ref), channel_id=1, source_target_pairs={{0,4},{1,5},{2,6},{3,7},{4,8},{5,9},{6,10},{7,11},{8,12},{9,13},{1... | collective-permute-start | bytes 196616 | tf_op jit(solution)/shard_map/ppermute | solution.py:548
  37.1 36.4 %collective-permute-start.3 = (bf16[16,1,16,128]{3,2,1,0:T(8,128)(2,1)S(1)}, bf16[16,1,16,128]{3,2,1,0:T(8,128)(2,1)S(1)}, u32[]{:S(2)}, u32[]{:S(2)}) collective-permute-start(bf16[16,1,16,128]{3,2,1,0:T(8,128)(2,1)S(1)} %get-tuple-element.32.yfirst_ref), channel_id=1, source_target_pairs={{4,0},{5,1},{6,2},{7,3},{8,4},{9,5},{10,6},{11,7},{12,8},{13,9},{1... | collective-permute-start | bytes 196616 | tf_op jit(solution)/shard_map/ppermute | solution.py:548
  50.5 23.0 %collective-permute-start = (bf16[1,32,16,128]{3,2,1,0:T(8,128)(2,1)S(1)}, bf16[1,32,16,128]{3,2,1,0:T(8,128)(2,1)S(1)}, u32[]{:S(2)}, u32[]{:S(2)}) collective-permute-start(bf16[1,32,16,128]{3,2,1,0:T(8,128)(2,1)S(1)} %get-tuple-element.33.xlast_ref), channel_id=1, source_target_pairs={{0,1},{1,2},{2,3},{4,5},{5,6},{6,7},{8,9},{9,10},{10,11},{12,13},{... | collective-permute-start | bytes 393224 | tf_op jit(solution)/shard_map/ppermute | solution.py:548
  52.4 21.1 %collective-permute-start.1 = (bf16[1,32,16,128]{3,2,1,0:T(8,128)(2,1)S(1)}, bf16[1,32,16,128]{3,2,1,0:T(8,128)(2,1)S(1)}, u32[]{:S(2)}, u32[]{:S(2)}) collective-permute-start(bf16[1,32,16,128]{3,2,1,0:T(8,128)(2,1)S(1)} %get-tuple-element.34.xfirst_ref), channel_id=1, source_target_pairs={{1,0},{2,1},{3,2},{5,4},{6,5},{7,6},{9,8},{10,9},{11,10},{13,12},{... | collective-permute-start | bytes 393224 | tf_op jit(solution)/shard_map/ppermute | solution.py:548
  56.3 1.6 %copy-start.2 = (bf16[16,32,16,128]{3,2,1,0:T(8,128)(2,1)S(1)}, bf16[16,32,16,128]{3,2,1,0:T(8,128)(2,1)}, u32[]{:S(2)}) copy-start(bf16[16,32,16,128]{3,2,1,0:T(8,128)(2,1)} %level_ref) | copy-start | bytes 6291460
  57.9 15.6 %copy-start.4 = (bf16[27,128,128]{2,1,0:T(8,128)(2,1)S(1)}, bf16[27,128,128]{2,1,0:T(8,128)(2,1)}, u32[]{:S(2)}) copy-start(bf16[27,128,128]{2,1,0:T(8,128)(2,1)} %w_ref.3) | copy-start | bytes 2654212
  71.6 1.9 %copy-start = (f32[16,16,2,16,128]{4,3,2,1,0:T(8,128)}, f32[16,16,2,16,128]{4,3,2,1,0:T(8,128)S(1)}, u32[]{:S(2)}) copy-start(f32[16,16,2,16,128]{4,3,2,1,0:T(8,128)S(1)} %get-tuple-element.18) | copy-start | bytes 12582916
  86.5 24.1 %collective-permute-start.8 = (bf16[1,32,16,128]{3,2,1,0:T(8,128)(2,1)S(1)}, bf16[1,32,16,128]{3,2,1,0:T(8,128)(2,1)S(1)}, u32[]{:S(2)}, u32[]{:S(2)}) collective-permute-start(bf16[1,32,16,128]{3,2,1,0:T(8,128)(2,1)S(1)} %get-tuple-element.24), channel_id=1, source_target_pairs={{0,1},{1,2},{2,3},{4,5},{5,6},{6,7},{8,9},{9,10},{10,11},{12,13},{... | collective-permute-start | bytes 393224 | tf_op jit(solution)/shard_map/ppermute | solution.py:548
  88.5 22.1 %collective-permute-start.9 = (bf16[16,1,16,128]{3,2,1,0:T(8,128)(2,1)S(1)}, bf16[16,1,16,128]{3,2,1,0:T(8,128)(2,1)S(1)}, u32[]{:S(2)}, u32[]{:S(2)}) collective-permute-start(bf16[16,1,16,128]{3,2,1,0:T(8,128)(2,1)S(1)} %get-tuple-element.25), channel_id=1, source_target_pairs={{0,4},{1,5},{2,6},{3,7},{4,8},{5,9},{6,10},{7,11},{8,12},{9,13},{1... | collective-permute-start | bytes 196616 | tf_op jit(solution)/shard_map/ppermute | solution.py:548
  103.9 6.7 %collective-permute-start.10 = (bf16[1,1,16,128]{3,2,1,0:T(8,128)(2,1)S(1)}, bf16[1,1,16,128]{3,2,1,0:T(8,128)(2,1)S(1)}, u32[]{:S(2)}, u32[]{:S(2)}) collective-permute-start(bf16[1,1,16,128]{3,2,1,0:T(8,128)(2,1)S(1)} %get-tuple-element.26), channel_id=1, source_target_pairs={{0,5},{1,6},{2,7},{4,9},{5,10},{6,11},{8,13},{9,14},{10,15},{12,17... | collective-permute-start | bytes 12296 | tf_op jit(solution)/shard_map/ppermute | solution.py:548
  106.0 4.6 %copy-start.1 = (bf16[27,128,256]{2,1,0:T(8,128)(2,1)S(1)}, bf16[27,128,256]{2,1,0:T(8,128)(2,1)}, u32[]{:S(2)}) copy-start(bf16[27,128,256]{2,1,0:T(8,128)(2,1)} %param.11) | copy-start | bytes 5308420

commit v9 on v8

--- a/solution.py
+++ b/solution.py
@@ -11,6 +11,7 @@
 EXTRA = 8
 PIECES = 4
 LINES = 4
+MOVED = 8
 
 
 def pack_kernel(devices, cap, owner_ref, cell_ref, rows_hbm, out_hbm,
@@ -39,8 +40,13 @@
         low = jnp.where(hit, (cell % LANES).astype(jnp.float32), 0.0)
         left = jnp.concatenate([high, low], axis=0).astype(jnp.bfloat16)
         right = (spots == place).astype(jnp.float32).astype(jnp.bfloat16)
-        table = table + lax.dot_general(left, right, (((1,), (1,)), ((), ())),
-                                        preferred_element_type=jnp.float32)
+        if b % 2 == 0:
+            left_even, right_even = left, right
+        else:
+            table = table + lax.dot_general(
+                jnp.concatenate([left_even, left], axis=1),
+                jnp.concatenate([right_even, right], axis=1),
+                (((1,), (1,)), ((), ())), preferred_element_type=jnp.float32)
     copy = pltpu.make_async_copy(slot_vmem, slot_smem, sems.at[PIECES])
     copy.start()
     fetch.wait()
@@ -63,14 +69,14 @@
     copy.wait()
 
     def step(b, carry):
-        lines = [slot_smem.at[b * LINES + i] for i in range(LINES)]
+        lines = [slot_smem.at[b * MOVED + i] for i in range(MOVED)]
         for u in range(LANES):
-            for i in range(LINES):
+            for i in range(MOVED):
                 spread[pl.ds(lines[i][u], 1), :] = wide[
-                    pl.ds((b * LINES + i) * LANES + u, 1), :]
+                    pl.ds((b * MOVED + i) * LANES + u, 1), :]
         return carry
 
-    lax.fori_loop(0, blocks // LINES, step, 0)
+    lax.fori_loop(0, blocks // MOVED, step, 0)
     piece = staged.shape[0] // PIECES
     sends = []
     for i in range(PIECES):

time: 116 us -> 115 us (level)
  no operation moved by 1% of the time
where the time goes in v9:
time: 115 us; the launch traced here: 113 us
  starting transfers between devices  49.5 us (43%)
  Pallas kernels  37.6 us (33%)
  waiting for transfers between devices  19.7 us (17%)
  local copies, waits for them, and re-layouts  6.15 us (5%)
    ppermute x11, starting transfers between devices, shifted(): return lax.ppermute(array, ('pts', 'nbr'), pairs)  43.5 us
    ppermute x11, waiting for transfers between devices, shifted(): return lax.ppermute(array, ('pts', 'nbr'), pairs)  19.7 us
    pallas_call x1, Pallas kernels, residual_base(): pl.pallas_call(functools.partial(residual_kernel, group), out_shape=[jax....  13.6 us
    pallas_call x1, Pallas kernels, add_rows(): pl.pallas_call(functools.partial(add_kernel, capacity), out_shape=[jax.Sh...  11.7 us
    pallas_call x1, Pallas kernels, pack(): pl.pallas_call(functools.partial(pack_kernel, devices, cap), out_shape=ja...  6.92 us
    all_to_all x1, starting transfers between devices, exchanged(): lax.all_to_all(array.reshape(devices, -1, array.shape[-1]), ('pts', 'nbr'...  6 us
    unnamed x10, local copies, waits for them, and re-layouts  3.53 us
    pallas_call x1, Pallas kernels, lower(): pl.pallas_call(lower_kernel, out_shape=jax.ShapeDtypeStruct((span_x // 2,...  3.13 us
  transfers between devices with their start and end apart: 12, of which 3 were waited for; matrix products, arithmetic and copies ran while one was open for 2% of the time, Pallas kernels for 14%

profile of v9, /device:TPU:12, one launch (start us, length us, event | category | flops | bytes accessed | tf_op | source)
XLA Modules:
  0.0 113.2 jit_solution(8700575579358215795)
XLA Ops:
  0.0 6.9 %pack.1 = bf16[8448,128]{1,0:T(8,128)(2,1)} custom-call(s32[32,128]{1,0:T(8,128)} %bitcast.12, s32[32,128]{1,0:T(8,128)} %bitcast.13, bf16[4096,128]{1,0:T(8,128)(2,1)} %bitcast.11), custom_call_target="tpu_custom_call" | custom-call | flops 100000000 | bytes 4000000 | tf_op jit(solution)/shard_map/pack/pallas_call | solution.py:97
  6.9 0.0 copy-start.3
  6.9 6.0 %all-to-all-start = ((bf16[32,264,128]{2,1,0:T(8,128)(2,1)}), bf16[32,264,128]{2,1,0:T(8,128)(2,1)S(1)}, u32[]{:S(2)}, u32[]{:S(2)}) async-start(bf16[32,264,128]{2,1,0:T(8,128)(2,1)} %bitcast.10), calls=%async_computation | async-start | bytes 4325376 | tf_op jit(solution)/shard_map/all_to_all | solution.py:558
  12.9 0.7 fusion
  13.7 3.1 %collective-permute-start.7 = (bf16[1,1,16,128]{3,2,1,0:T(8,128)(2,1)S(1)}, bf16[1,1,16,128]{3,2,1,0:T(8,128)(2,1)S(1)}, u32[]{:S(2)}, u32[]{:S(2)}) collective-permute-start(bf16[1,1,16,128]{3,2,1,0:T(8,128)(2,1)S(1)} %get-tuple-element.27), channel_id=1, source_target_pairs={{5,0},{6,1},{7,2},{9,4},{10,5},{11,6},{13,8},{14,9},{15,10},{17,12... | collective-permute-start | bytes 12296 | tf_op jit(solution)/shard_map/ppermute | solution.py:554
  16.8 2.5 %collective-permute-start.6 = (bf16[1,1,16,128]{3,2,1,0:T(8,128)(2,1)S(1)}, bf16[1,1,16,128]{3,2,1,0:T(8,128)(2,1)S(1)}, u32[]{:S(2)}, u32[]{:S(2)}) collective-permute-start(bf16[1,1,16,128]{3,2,1,0:T(8,128)(2,1)S(1)} %get-tuple-element.28), channel_id=1, source_target_pairs={{1,4},{2,5},{3,6},{5,8},{6,9},{7,10},{9,12},{10,13},{11,14},{13,16... | collective-permute-start | bytes 12296 | tf_op jit(solution)/shard_map/ppermute | solution.py:554
  19.3 4.0 %collective-permute-start.5 = (bf16[1,1,16,128]{3,2,1,0:T(8,128)(2,1)S(1)}, bf16[1,1,16,128]{3,2,1,0:T(8,128)(2,1)S(1)}, u32[]{:S(2)}, u32[]{:S(2)}) collective-permute-start(bf16[1,1,16,128]{3,2,1,0:T(8,128)(2,1)S(1)} %get-tuple-element.29), channel_id=1, source_target_pairs={{4,1},{5,2},{6,3},{8,5},{9,6},{10,7},{12,9},{13,10},{14,11},{16,13... | collective-permute-start | bytes 12296 | tf_op jit(solution)/shard_map/ppermute | solution.py:554
  23.2 1.9 %collective-permute-start.4 = (bf16[1,1,16,128]{3,2,1,0:T(8,128)(2,1)S(1)}, bf16[1,1,16,128]{3,2,1,0:T(8,128)(2,1)S(1)}, u32[]{:S(2)}, u32[]{:S(2)}) collective-permute-start(bf16[1,1,16,128]{3,2,1,0:T(8,128)(2,1)S(1)} %get-tuple-element.30), channel_id=1, source_target_pairs={{0,5},{1,6},{2,7},{4,9},{5,10},{6,11},{8,13},{9,14},{10,15},{12,17... | collective-permute-start | bytes 12296 | tf_op jit(solution)/shard_map/ppermute | solution.py:554
  25.2 0.9 fusion.1
  26.1 2.2 %collective-permute-start.2 = (bf16[16,1,16,128]{3,2,1,0:T(8,128)(2,1)S(1)}, bf16[16,1,16,128]{3,2,1,0:T(8,128)(2,1)S(1)}, u32[]{:S(2)}, u32[]{:S(2)}) collective-permute-start(bf16[16,1,16,128]{3,2,1,0:T(8,128)(2,1)S(1)} %get-tuple-element.31.ylast_ref), channel_id=1, source_target_pairs={{0,4},{1,5},{2,6},{3,7},{4,8},{5,9},{6,10},{7,11},{8,12},{9,13},{1... | collective-permute-start | bytes 196616 | tf_op jit(solution)/shard_map/ppermute | solution.py:554
  28.3 1.0 fusion.2
  29.3 7.3 %collective-permute-done.7.hh_ref = bf16[1,1,16,128]{3,2,1,0:T(8,128)(2,1)S(1)} collective-permute-done((bf16[1,1,16,128]{3,2,1,0:T(8,128)(2,1)S(1)}, bf16[1,1,16,128]{3,2,1,0:T(8,128)(2,1)S(1)}, u32[]{:S(2)}, u32[]{:S(2)}) %collective-permute-start.7) | collective-permute-done | bytes 4128 | tf_op jit(solution)/shard_map/ppermute | solution.py:554
  36.6 4.5 %collective-permute-start.3 = (bf16[16,1,16,128]{3,2,1,0:T(8,128)(2,1)S(1)}, bf16[16,1,16,128]{3,2,1,0:T(8,128)(2,1)S(1)}, u32[]{:S(2)}, u32[]{:S(2)}) collective-permute-start(bf16[16,1,16,128]{3,2,1,0:T(8,128)(2,1)S(1)} %get-tuple-element.32.yfirst_ref), channel_id=1, source_target_pairs={{4,0},{5,1},{6,2},{7,3},{8,4},{9,5},{10,6},{11,7},{12,8},{13,9},{1... | collective-permute-start | bytes 196616 | tf_op jit(solution)/shard_map/ppermute | solution.py:554
  41.1 8.8 %collective-permute-done.6.hl_ref = bf16[1,1,16,128]{3,2,1,0:T(8,128)(2,1)S(1)} collective-permute-done((bf16[1,1,16,128]{3,2,1,0:T(8,128)(2,1)S(1)}, bf16[1,1,16,128]{3,2,1,0:T(8,128)(2,1)S(1)}, u32[]{:S(2)}, u32[]{:S(2)}) %collective-permute-start.6) | collective-permute-done | bytes 4128 | tf_op jit(solution)/shard_map/ppermute | solution.py:554
  49.9 1.9 %collective-permute-start = (bf16[1,32,16,128]{3,2,1,0:T(8,128)(2,1)S(1)}, bf16[1,32,16,128]{3,2,1,0:T(8,128)(2,1)S(1)}, u32[]{:S(2)}, u32[]{:S(2)}) collective-permute-start(bf16[1,32,16,128]{3,2,1,0:T(8,128)(2,1)S(1)} %get-tuple-element.33.xlast_ref), channel_id=1, source_target_pairs={{0,1},{1,2},{2,3},{4,5},{5,6},{6,7},{8,9},{9,10},{10,11},{12,13},{... | collective-permute-start | bytes 393224 | tf_op jit(solution)/shard_map/ppermute | solution.py:554
  51.8 0.0 collective-permute-done.5.lh_ref
  51.8 3.9 %collective-permute-start.1 = (bf16[1,32,16,128]{3,2,1,0:T(8,128)(2,1)S(1)}, bf16[1,32,16,128]{3,2,1,0:T(8,128)(2,1)S(1)}, u32[]{:S(2)}, u32[]{:S(2)}) collective-permute-start(bf16[1,32,16,128]{3,2,1,0:T(8,128)(2,1)S(1)} %get-tuple-element.34.xfirst_ref), channel_id=1, source_target_pairs={{1,0},{2,1},{3,2},{5,4},{6,5},{7,6},{9,8},{10,9},{11,10},{13,12},{... | collective-permute-start | bytes 393224 | tf_op jit(solution)/shard_map/ppermute | solution.py:554
  55.8 0.0 copy-start.2
  55.8 1.6 %copy-done.2 = bf16[16,32,16,128]{3,2,1,0:T(8,128)(2,1)S(1)} copy-done((bf16[16,32,16,128]{3,2,1,0:T(8,128)(2,1)S(1)}, bf16[16,32,16,128]{3,2,1,0:T(8,128)(2,1)}, u32[]{:S(2)}) %copy-start.2) | copy-done | bytes 2097176
  57.4 13.6 %residual.1 = (f32[16,16,2,16,128]{4,3,2,1,0:T(8,128)S(1)}, f32[2,16,2,16,128]{4,3,2,1,0:T(8,128)S(1)}, f32[2,16,16,128]{3,2,1,0:T(8,128)S(1)}) custom-call(bf16[16,32,16,128]{3,2,1,0:T(8,128)(2,1)S(1)} %copy-done.2, bf16[27,128,128]{2,1,0:T(8,128)(2,1)S(1)} %copy-done.3), custom_call_target="tpu_custom_call" | custom-call | flops 7247757312 | bytes 8000000 | tf_op jit(solution)/shard_map/residual/pallas_call | solution.py:312
  71.0 1.9 %copy-done = f32[16,16,2,16,128]{4,3,2,1,0:T(8,128)} copy-done((f32[16,16,2,16,128]{4,3,2,1,0:T(8,128)}, f32[16,16,2,16,128]{4,3,2,1,0:T(8,128)S(1)}, u32[]{:S(2)}) %copy-start) | copy-done | bytes 4194328
  72.9 0.0 collective-permute-done.4.ll_ref
  72.9 0.0 collective-permute-done.2.ylow_ref
  73.0 1.3 %border.1 = (f32[2,16,2,16,128]{4,3,2,1,0:T(8,128)S(1)}, f32[2,16,16,128]{3,2,1,0:T(8,128)S(1)}) custom-call(f32[2,16,2,16,128]{4,3,2,1,0:T(8,128)S(1)} %get-tuple-element.19.ends_ref, f32[2,16,16,128]{3,2,1,0:T(8,128)S(1)} %get-tuple-element.20.edges_ref, bf16[1,32,16,128]{3,2,1,0:T(8,128)(2,1)S(1)} %get-tuple-element.34.xfirst_ref, ...), custom_call_target="tpu_custom_call" | custom-call | flops 1000000000 | bytes 3000000 | tf_op jit(solution)/shard_map/border/pallas_call | solution.py:392
  74.3 11.7 %add_rows.1 = (bf16[16,32,16,128]{3,2,1,0:T(8,128)(2,1)S(1)}, bf16[1,32,16,128]{3,2,1,0:T(8,128)(2,1)S(1)}, bf16[16,1,16,128]{3,2,1,0:T(8,128)(2,1)S(1)}, bf16[1,1,16,128]{3,2,1,0:T(8,128)(2,1)S(1)}) custom-call(bf16[8448,128]{1,0:T(8,128)(2,1)S(1)} %bitcast.7, f32[8192,128]{1,0:T(8,128)} %bitcast.8, f32[2,16,2,16,128]{4,3,2,1,0:T(8,128)S(1)} %get-tuple-element.21.ends_ref, ...), custom_call_target="tpu_custom_call" | custom-call | flops 100000000 | bytes 8000000 | tf_op jit(solution)/shard_map/add_rows/pallas_call | solution.py:191
  86.0 1.9 %collective-permute-start.8 = (bf16[1,32,16,128]{3,2,1,0:T(8,128)(2,1)S(1)}, bf16[1,32,16,128]{3,2,1,0:T(8,128)(2,1)S(1)}, u32[]{:S(2)}, u32[]{:S(2)}) collective-permute-start(bf16[1,32,16,128]{3,2,1,0:T(8,128)(2,1)S(1)} %get-tuple-element.24), channel_id=1, source_target_pairs={{0,1},{1,2},{2,3},{4,5},{5,6},{6,7},{8,9},{9,10},{10,11},{12,13},{... | collective-permute-start | bytes 393224 | tf_op jit(solution)/shard_map/ppermute | solution.py:554
  87.9 15.4 %collective-permute-start.9 = (bf16[16,1,16,128]{3,2,1,0:T(8,128)(2,1)S(1)}, bf16[16,1,16,128]{3,2,1,0:T(8,128)(2,1)S(1)}, u32[]{:S(2)}, u32[]{:S(2)}) collective-permute-start(bf16[16,1,16,128]{3,2,1,0:T(8,128)(2,1)S(1)} %get-tuple-element.25), channel_id=1, source_target_pairs={{0,4},{1,5},{2,6},{3,7},{4,8},{5,9},{6,10},{7,11},{8,12},{9,13},{1... | collective-permute-start | bytes 196616 | tf_op jit(solution)/shard_map/ppermute | solution.py:554
  103.3 2.1 %collective-permute-start.10 = (bf16[1,1,16,128]{3,2,1,0:T(8,128)(2,1)S(1)}, bf16[1,1,16,128]{3,2,1,0:T(8,128)(2,1)S(1)}, u32[]{:S(2)}, u32[]{:S(2)}) collective-permute-start(bf16[1,1,16,128]{3,2,1,0:T(8,128)(2,1)S(1)} %get-tuple-element.26), channel_id=1, source_target_pairs={{0,5},{1,6},{2,7},{4,9},{5,10},{6,11},{8,13},{9,14},{10,15},{12,17... | collective-permute-start | bytes 12296 | tf_op jit(solution)/shard_map/ppermute | solution.py:554
  105.4 0.0 copy-start.1
  105.5 1.0 local_taps.1.taps_ref
  106.5 3.5 %collective-permute-done.10.corner_ref = bf16[1,1,16,128]{3,2,1,0:T(8,128)(2,1)S(1)} collective-permute-done((bf16[1,1,16,128]{3,2,1,0:T(8,128)(2,1)S(1)}, bf16[1,1,16,128]{3,2,1,0:T(8,128)(2,1)S(1)}, u32[]{:S(2)}, u32[]{:S(2)}) %collective-permute-start.10) | collective-permute-done | bytes 4128 | tf_op jit(solution)/shard_map/ppermute | solution.py:554
  110.0 3.1 %lower.1 = bf16[8,16,8,256]{3,2,1,0:T(8,128)(2,1)} custom-call(bf16[2,8,128,1152]{3,2,1,0:T(8,128)(2,1)S(1)} %local_taps.1.taps_ref, bf16[1,32,16,128]{3,2,1,0:T(8,128)(2,1)S(1)} %collective-permute-done.8.front_ref, bf16[16,1,16,128]{3,2,1,0:T(8,128)(2,1)S(1)} %collective-permute-done.9.side_ref, ...), custom_call_target="tpu_custom_call" | custom-call | flops 1811939328 | bytes 5000000 | tf_op jit(solution)/shard_map/lower/pallas_call | solution.py:528
  (11 shorter events, 0.0 us)
Async XLA Ops:
  6.9 48.8 %copy-start.3 = (bf16[27,128,128]{2,1,0:T(8,128)(2,1)S(1)}, bf16[27,128,128]{2,1,0:T(8,128)(2,1)}, u32[]{:S(2)}) copy-start(bf16[27,128,128]{2,1,0:T(8,128)(2,1)} %w_ref.3) | copy-start | bytes 2654212
  6.9 67.3 %all-to-all-start = ((bf16[32,264,128]{2,1,0:T(8,128)(2,1)}), bf16[32,264,128]{2,1,0:T(8,128)(2,1)S(1)}, u32[]{:S(2)}, u32[]{:S(2)}) async-start(bf16[32,264,128]{2,1,0:T(8,128)(2,1)} %bitcast.10), calls=%async_computation | async-start | bytes 4325376 | tf_op jit(solution)/shard_map/all_to_all | solution.py:558
  13.7 22.9 %collective-permute-start.7 = (bf16[1,1,16,128]{3,2,1,0:T(8,128)(2,1)S(1)}, bf16[1,1,16,128]{3,2,1,0:T(8,128)(2,1)S(1)}, u32[]{:S(2)}, u32[]{:S(2)}) collective-permute-start(bf16[1,1,16,128]{3,2,1,0:T(8,128)(2,1)S(1)} %get-tuple-element.27), channel_id=1, source_target_pairs={{5,0},{6,1},{7,2},{9,4},{10,5},{11,6},{13,8},{14,9},{15,10},{17,12... | collective-permute-start | bytes 12296 | tf_op jit(solution)/shard_map/ppermute | solution.py:554
  16.8 33.1 %collective-permute-start.6 = (bf16[1,1,16,128]{3,2,1,0:T(8,128)(2,1)S(1)}, bf16[1,1,16,128]{3,2,1,0:T(8,128)(2,1)S(1)}, u32[]{:S(2)}, u32[]{:S(2)}) collective-permute-start(bf16[1,1,16,128]{3,2,1,0:T(8,128)(2,1)S(1)} %get-tuple-element.28), channel_id=1, source_target_pairs={{1,4},{2,5},{3,6},{5,8},{6,9},{7,10},{9,12},{10,13},{11,14},{13,16... | collective-permute-start | bytes 12296 | tf_op jit(solution)/shard_map/ppermute | solution.py:554
  19.3 32.5 %collective-permute-start.5 = (bf16[1,1,16,128]{3,2,1,0:T(8,128)(2,1)S(1)}, bf16[1,1,16,128]{3,2,1,0:T(8,128)(2,1)S(1)}, u32[]{:S(2)}, u32[]{:S(2)}) collective-permute-start(bf16[1,1,16,128]{3,2,1,0:T(8,128)(2,1)S(1)} %get-tuple-element.29), channel_id=1, source_target_pairs={{4,1},{5,2},{6,3},{8,5},{9,6},{10,7},{12,9},{13,10},{14,11},{16,13... | collective-permute-start | bytes 12296 | tf_op jit(solution)/shard_map/ppermute | solution.py:554
  23.2 49.7 %collective-permute-start.4 = (bf16[1,1,16,128]{3,2,1,0:T(8,128)(2,1)S(1)}, bf16[1,1,16,128]{3,2,1,0:T(8,128)(2,1)S(1)}, u32[]{:S(2)}, u32[]{:S(2)}) collective-permute-start(bf16[1,1,16,128]{3,2,1,0:T(8,128)(2,1)S(1)} %get-tuple-element.30), channel_id=1, source_target_pairs={{0,5},{1,6},{2,7},{4,9},{5,10},{6,11},{8,13},{9,14},{10,15},{12,17... | collective-permute-start | bytes 12296 | tf_op jit(solution)/shard_map/ppermute | solution.py:554
  26.1 46.9 %collective-permute-start.2 = (bf16[16,1,16,128]{3,2,1,0:T(8,128)(2,1)S(1)}, bf16[16,1,16,128]{3,2,1,0:T(8,128)(2,1)S(1)}, u32[]{:S(2)}, u32[]{:S(2)}) collective-permute-start(bf16[16,1,16,128]{3,2,1,0:T(8,128)(2,1)S(1)} %get-tuple-element.31.ylast_ref), channel_id=1, source_target_pairs={{0,4},{1,5},{2,6},{3,7},{4,8},{5,9},{6,10},{7,11},{8,12},{9,13},{1... | collective-permute-start | bytes 196616 | tf_op jit(solution)/shard_map/ppermute | solution.py:554
  36.6 36.4 %collective-permute-start.3 = (bf16[16,1,16,128]{3,2,1,0:T(8,128)(2,1)S(1)}, bf16[16,1,16,128]{3,2,1,0:T(8,128)(2,1)S(1)}, u32[]{:S(2)}, u32[]{:S(2)}) collective-permute-start(bf16[16,1,16,128]{3,2,1,0:T(8,128)(2,1)S(1)} %get-tuple-element.32.yfirst_ref), channel_id=1, source_target_pairs={{4,0},{5,1},{6,2},{7,3},{8,4},{9,5},{10,6},{11,7},{12,8},{13,9},{1... | collective-permute-start | bytes 196616 | tf_op jit(solution)/shard_map/ppermute | solution.py:554
  49.9 23.1 %collective-permute-start = (bf16[1,32,16,128]{3,2,1,0:T(8,128)(2,1)S(1)}, bf16[1,32,16,128]{3,2,1,0:T(8,128)(2,1)S(1)}, u32[]{:S(2)}, u32[]{:S(2)}) collective-permute-start(bf16[1,32,16,128]{3,2,1,0:T(8,128)(2,1)S(1)} %get-tuple-element.33.xlast_ref), channel_id=1, source_target_pairs={{0,1},{1,2},{2,3},{4,5},{5,6},{6,7},{8,9},{9,10},{10,11},{12,13},{... | collective-permute-start | bytes 393224 | tf_op jit(solution)/shard_map/ppermute | solution.py:554
  51.8 21.1 %collective-permute-start.1 = (bf16[1,32,16,128]{3,2,1,0:T(8,128)(2,1)S(1)}, bf16[1,32,16,128]{3,2,1,0:T(8,128)(2,1)S(1)}, u32[]{:S(2)}, u32[]{:S(2)}) collective-permute-start(bf16[1,32,16,128]{3,2,1,0:T(8,128)(2,1)S(1)} %get-tuple-element.34.xfirst_ref), channel_id=1, source_target_pairs={{1,0},{2,1},{3,2},{5,4},{6,5},{7,6},{9,8},{10,9},{11,10},{13,12},{... | collective-permute-start | bytes 393224 | tf_op jit(solution)/shard_map/ppermute | solution.py:554
  55.8 1.6 %copy-start.2 = (bf16[16,32,16,128]{3,2,1,0:T(8,128)(2,1)S(1)}, bf16[16,32,16,128]{3,2,1,0:T(8,128)(2,1)}, u32[]{:S(2)}) copy-start(bf16[16,32,16,128]{3,2,1,0:T(8,128)(2,1)} %level_ref) | copy-start | bytes 6291460
  57.4 15.6 %copy-start.4 = (bf16[27,128,128]{2,1,0:T(8,128)(2,1)S(1)}, bf16[27,128,128]{2,1,0:T(8,128)(2,1)}, u32[]{:S(2)}) copy-start(bf16[27,128,128]{2,1,0:T(8,128)(2,1)} %w_ref.3) | copy-start | bytes 2654212
  71.0 1.9 %copy-start = (f32[16,16,2,16,128]{4,3,2,1,0:T(8,128)}, f32[16,16,2,16,128]{4,3,2,1,0:T(8,128)S(1)}, u32[]{:S(2)}) copy-start(f32[16,16,2,16,128]{4,3,2,1,0:T(8,128)S(1)} %get-tuple-element.18) | copy-start | bytes 12582916
  86.0 24.1 %collective-permute-start.8 = (bf16[1,32,16,128]{3,2,1,0:T(8,128)(2,1)S(1)}, bf16[1,32,16,128]{3,2,1,0:T(8,128)(2,1)S(1)}, u32[]{:S(2)}, u32[]{:S(2)}) collective-permute-start(bf16[1,32,16,128]{3,2,1,0:T(8,128)(2,1)S(1)} %get-tuple-element.24), channel_id=1, source_target_pairs={{0,1},{1,2},{2,3},{4,5},{5,6},{6,7},{8,9},{9,10},{10,11},{12,13},{... | collective-permute-start | bytes 393224 | tf_op jit(solution)/shard_map/ppermute | solution.py:554
  87.9 22.1 %collective-permute-start.9 = (bf16[16,1,16,128]{3,2,1,0:T(8,128)(2,1)S(1)}, bf16[16,1,16,128]{3,2,1,0:T(8,128)(2,1)S(1)}, u32[]{:S(2)}, u32[]{:S(2)}) collective-permute-start(bf16[16,1,16,128]{3,2,1,0:T(8,128)(2,1)S(1)} %get-tuple-element.25), channel_id=1, source_target_pairs={{0,4},{1,5},{2,6},{3,7},{4,8},{5,9},{6,10},{7,11},{8,12},{9,13},{1... | collective-permute-start | bytes 196616 | tf_op jit(solution)/shard_map/ppermute | solution.py:554
  103.3 6.7 %collective-permute-start.10 = (bf16[1,1,16,128]{3,2,1,0:T(8,128)(2,1)S(1)}, bf16[1,1,16,128]{3,2,1,0:T(8,128)(2,1)S(1)}, u32[]{:S(2)}, u32[]{:S(2)}) collective-permute-start(bf16[1,1,16,128]{3,2,1,0:T(8,128)(2,1)S(1)} %get-tuple-element.26), channel_id=1, source_target_pairs={{0,5},{1,6},{2,7},{4,9},{5,10},{6,11},{8,13},{9,14},{10,15},{12,17... | collective-permute-start | bytes 12296 | tf_op jit(solution)/shard_map/ppermute | solution.py:554
  105.4 4.6 %copy-start.1 = (bf16[27,128,256]{2,1,0:T(8,128)(2,1)S(1)}, bf16[27,128,256]{2,1,0:T(8,128)(2,1)}, u32[]{:S(2)}) copy-start(bf16[27,128,256]{2,1,0:T(8,128)(2,1)} %param.11) | copy-start | bytes 5308420

commit v10 on v9

--- a/solution.py
+++ b/solution.py
@@ -27,6 +27,7 @@
     spots = lax.broadcasted_iota(jnp.int32, (cap, LANES), 0)
     base = jnp.zeros((devices, 1), jnp.float32)
     table = jnp.zeros((2 * devices, cap), jnp.float32)
+    lefts, rights = [], []
     for b in range(blocks):
         own = owner_ref[b:b + 1, :]
         cell = cell_ref[b:b + 1, :]
@@ -40,13 +41,13 @@
         low = jnp.where(hit, (cell % LANES).astype(jnp.float32), 0.0)
         left = jnp.concatenate([high, low], axis=0).astype(jnp.bfloat16)
         right = (spots == place).astype(jnp.float32).astype(jnp.bfloat16)
-        if b % 2 == 0:
-            left_even, right_even = left, right
-        else:
+        lefts.append(left)
+        rights.append(right)
+        if len(lefts) == 4 or b == blocks - 1:
             table = table + lax.dot_general(
-                jnp.concatenate([left_even, left], axis=1),
-                jnp.concatenate([right_even, right], axis=1),
+                jnp.concatenate(lefts, axis=1), jnp.concatenate(rights, axis=1),
                 (((1,), (1,)), ((), ())), preferred_element_type=jnp.float32)
+            lefts, rights = [], []
     copy = pltpu.make_async_copy(slot_vmem, slot_smem, sems.at[PIECES])
     copy.start()
     fetch.wait()

time: 115 us -> 115 us (level)
  no operation moved by 1% of the time
where the time goes in v10:
time: 115 us; the launch traced here: 113 us
  starting transfers between devices  49.5 us (43%)
  Pallas kernels  37.4 us (33%)
  waiting for transfers between devices  19.7 us (17%)
  local copies, waits for them, and re-layouts  6.15 us (5%)
    ppermute x11, starting transfers between devices, shifted(): return lax.ppermute(array, ('pts', 'nbr'), pairs)  43.5 us
    ppermute x11, waiting for transfers between devices, shifted(): return lax.ppermute(array, ('pts', 'nbr'), pairs)  19.7 us
    pallas_call x1, Pallas kernels, residual_base(): pl.pallas_call(functools.partial(residual_kernel, group), out_shape=[jax....  13.6 us
    pallas_call x1, Pallas kernels, add_rows(): pl.pallas_call(functools.partial(add_kernel, capacity), out_shape=[jax.Sh...  11.7 us
    pallas_call x1, Pallas kernels, pack(): pl.pallas_call(functools.partial(pack_kernel, devices, cap), out_shape=ja...  6.71 us
    all_to_all x1, starting transfers between devices, exchanged(): lax.all_to_all(array.reshape(devices, -1, array.shape[-1]), ('pts', 'nbr'...  6 us
    unnamed x10, local copies, waits for them, and re-layouts  3.53 us
    pallas_call x1, Pallas kernels, lower(): pl.pallas_call(lower_kernel, out_shape=jax.ShapeDtypeStruct((span_x // 2,...  3.13 us
  transfers between devices with their start and end apart: 12, of which 3 were waited for; matrix products, arithmetic and copies ran while one was open for 2% of the time, Pallas kernels for 14%

profile of v10, /device:TPU:12, one launch (start us, length us, event | category | flops | bytes accessed | tf_op | source)
XLA Modules:
  0.0 112.9 jit_solution(3643773371740530263)
XLA Ops:
  0.0 6.7 %pack.1 = bf16[8448,128]{1,0:T(8,128)(2,1)} custom-call(s32[32,128]{1,0:T(8,128)} %bitcast.12, s32[32,128]{1,0:T(8,128)} %bitcast.13, bf16[4096,128]{1,0:T(8,128)(2,1)} %bitcast.11), custom_call_target="tpu_custom_call" | custom-call | flops 100000000 | bytes 4000000 | tf_op jit(solution)/shard_map/pack/pallas_call | solution.py:98
  6.7 0.0 copy-start.3
  6.7 6.0 %all-to-all-start = ((bf16[32,264,128]{2,1,0:T(8,128)(2,1)}), bf16[32,264,128]{2,1,0:T(8,128)(2,1)S(1)}, u32[]{:S(2)}, u32[]{:S(2)}) async-start(bf16[32,264,128]{2,1,0:T(8,128)(2,1)} %bitcast.10), calls=%async_computation | async-start | bytes 4325376 | tf_op jit(solution)/shard_map/all_to_all | solution.py:559
  12.7 0.7 fusion
  13.5 3.1 %collective-permute-start.7 = (bf16[1,1,16,128]{3,2,1,0:T(8,128)(2,1)S(1)}, bf16[1,1,16,128]{3,2,1,0:T(8,128)(2,1)S(1)}, u32[]{:S(2)}, u32[]{:S(2)}) collective-permute-start(bf16[1,1,16,128]{3,2,1,0:T(8,128)(2,1)S(1)} %get-tuple-element.27), channel_id=1, source_target_pairs={{5,0},{6,1},{7,2},{9,4},{10,5},{11,6},{13,8},{14,9},{15,10},{17,12... | collective-permute-start | bytes 12296 | tf_op jit(solution)/shard_map/ppermute | solution.py:555
  16.6 2.5 %collective-permute-start.6 = (bf16[1,1,16,128]{3,2,1,0:T(8,128)(2,1)S(1)}, bf16[1,1,16,128]{3,2,1,0:T(8,128)(2,1)S(1)}, u32[]{:S(2)}, u32[]{:S(2)}) collective-permute-start(bf16[1,1,16,128]{3,2,1,0:T(8,128)(2,1)S(1)} %get-tuple-element.28), channel_id=1, source_target_pairs={{1,4},{2,5},{3,6},{5,8},{6,9},{7,10},{9,12},{10,13},{11,14},{13,16... | collective-permute-start | bytes 12296 | tf_op jit(solution)/shard_map/ppermute | solution.py:555
  19.0 4.0 %collective-permute-start.5 = (bf16[1,1,16,128]{3,2,1,0:T(8,128)(2,1)S(1)}, bf16[1,1,16,128]{3,2,1,0:T(8,128)(2,1)S(1)}, u32[]{:S(2)}, u32[]{:S(2)}) collective-permute-start(bf16[1,1,16,128]{3,2,1,0:T(8,128)(2,1)S(1)} %get-tuple-element.29), channel_id=1, source_target_pairs={{4,1},{5,2},{6,3},{8,5},{9,6},{10,7},{12,9},{13,10},{14,11},{16,13... | collective-permute-start | bytes 12296 | tf_op jit(solution)/shard_map/ppermute | solution.py:555
  23.0 1.9 %collective-permute-start.4 = (bf16[1,1,16,128]{3,2,1,0:T(8,128)(2,1)S(1)}, bf16[1,1,16,128]{3,2,1,0:T(8,128)(2,1)S(1)}, u32[]{:S(2)}, u32[]{:S(2)}) collective-permute-start(bf16[1,1,16,128]{3,2,1,0:T(8,128)(2,1)S(1)} %get-tuple-element.30), channel_id=1, source_target_pairs={{0,5},{1,6},{2,7},{4,9},{5,10},{6,11},{8,13},{9,14},{10,15},{12,17... | collective-permute-start | bytes 12296 | tf_op jit(solution)/shard_map/ppermute | solution.py:555
  25.0 0.9 fusion.1
  25.9 2.2 %collective-permute-start.2 = (bf16[16,1,16,128]{3,2,1,0:T(8,128)(2,1)S(1)}, bf16[16,1,16,128]{3,2,1,0:T(8,128)(2,1)S(1)}, u32[]{:S(2)}, u32[]{:S(2)}) collective-permute-start(bf16[16,1,16,128]{3,2,1,0:T(8,128)(2,1)S(1)} %get-tuple-element.31.ylast_ref), channel_id=1, source_target_pairs={{0,4},{1,5},{2,6},{3,7},{4,8},{5,9},{6,10},{7,11},{8,12},{9,13},{1... | collective-permute-start | bytes 196616 | tf_op jit(solution)/shard_map/ppermute | solution.py:555
  28.1 1.0 fusion.2
  29.1 7.3 %collective-permute-done.7.hh_ref = bf16[1,1,16,128]{3,2,1,0:T(8,128)(2,1)S(1)} collective-permute-done((bf16[1,1,16,128]{3,2,1,0:T(8,128)(2,1)S(1)}, bf16[1,1,16,128]{3,2,1,0:T(8,128)(2,1)S(1)}, u32[]{:S(2)}, u32[]{:S(2)}) %collective-permute-start.7) | collective-permute-done | bytes 4128 | tf_op jit(solution)/shard_map/ppermute | solution.py:555
  36.4 4.5 %collective-permute-start.3 = (bf16[16,1,16,128]{3,2,1,0:T(8,128)(2,1)S(1)}, bf16[16,1,16,128]{3,2,1,0:T(8,128)(2,1)S(1)}, u32[]{:S(2)}, u32[]{:S(2)}) collective-permute-start(bf16[16,1,16,128]{3,2,1,0:T(8,128)(2,1)S(1)} %get-tuple-element.32.yfirst_ref), channel_id=1, source_target_pairs={{4,0},{5,1},{6,2},{7,3},{8,4},{9,5},{10,6},{11,7},{12,8},{13,9},{1... | collective-permute-start | bytes 196616 | tf_op jit(solution)/shard_map/ppermute | solution.py:555
  40.9 8.8 %collective-permute-done.6.hl_ref = bf16[1,1,16,128]{3,2,1,0:T(8,128)(2,1)S(1)} collective-permute-done((bf16[1,1,16,128]{3,2,1,0:T(8,128)(2,1)S(1)}, bf16[1,1,16,128]{3,2,1,0:T(8,128)(2,1)S(1)}, u32[]{:S(2)}, u32[]{:S(2)}) %collective-permute-start.6) | collective-permute-done | bytes 4128 | tf_op jit(solution)/shard_map/ppermute | solution.py:555
  49.7 1.9 %collective-permute-start = (bf16[1,32,16,128]{3,2,1,0:T(8,128)(2,1)S(1)}, bf16[1,32,16,128]{3,2,1,0:T(8,128)(2,1)S(1)}, u32[]{:S(2)}, u32[]{:S(2)}) collective-permute-start(bf16[1,32,16,128]{3,2,1,0:T(8,128)(2,1)S(1)} %get-tuple-element.33.xlast_ref), channel_id=1, source_target_pairs={{0,1},{1,2},{2,3},{4,5},{5,6},{6,7},{8,9},{9,10},{10,11},{12,13},{... | collective-permute-start | bytes 393224 | tf_op jit(solution)/shard_map/ppermute | solution.py:555
  51.6 3.9 %collective-permute-start.1 = (bf16[1,32,16,128]{3,2,1,0:T(8,128)(2,1)S(1)}, bf16[1,32,16,128]{3,2,1,0:T(8,128)(2,1)S(1)}, u32[]{:S(2)}, u32[]{:S(2)}) collective-permute-start(bf16[1,32,16,128]{3,2,1,0:T(8,128)(2,1)S(1)} %get-tuple-element.34.xfirst_ref), channel_id=1, source_target_pairs={{1,0},{2,1},{3,2},{5,4},{6,5},{7,6},{9,8},{10,9},{11,10},{13,12},{... | collective-permute-start | bytes 393224 | tf_op jit(solution)/shard_map/ppermute | solution.py:555
  55.5 0.0 copy-start.2
  55.6 1.6 %copy-done.2 = bf16[16,32,16,128]{3,2,1,0:T(8,128)(2,1)S(1)} copy-done((bf16[16,32,16,128]{3,2,1,0:T(8,128)(2,1)S(1)}, bf16[16,32,16,128]{3,2,1,0:T(8,128)(2,1)}, u32[]{:S(2)}) %copy-start.2) | copy-done | bytes 2097176
  57.1 13.6 %residual.1 = (f32[16,16,2,16,128]{4,3,2,1,0:T(8,128)S(1)}, f32[2,16,2,16,128]{4,3,2,1,0:T(8,128)S(1)}, f32[2,16,16,128]{3,2,1,0:T(8,128)S(1)}) custom-call(bf16[16,32,16,128]{3,2,1,0:T(8,128)(2,1)S(1)} %copy-done.2, bf16[27,128,128]{2,1,0:T(8,128)(2,1)S(1)} %copy-done.3), custom_call_target="tpu_custom_call" | custom-call | flops 7247757312 | bytes 8000000 | tf_op jit(solution)/shard_map/residual/pallas_call | solution.py:313
  70.8 1.9 %copy-done = f32[16,16,2,16,128]{4,3,2,1,0:T(8,128)} copy-done((f32[16,16,2,16,128]{4,3,2,1,0:T(8,128)}, f32[16,16,2,16,128]{4,3,2,1,0:T(8,128)S(1)}, u32[]{:S(2)}) %copy-start) | copy-done | bytes 4194328
  72.7 0.0 collective-permute-done.4.ll_ref
  72.7 0.0 collective-permute-done.2.ylow_ref
  72.7 0.0 collective-permute-done.3.yhigh_ref
  72.7 1.3 %border.1 = (f32[2,16,2,16,128]{4,3,2,1,0:T(8,128)S(1)}, f32[2,16,16,128]{3,2,1,0:T(8,128)S(1)}) custom-call(f32[2,16,2,16,128]{4,3,2,1,0:T(8,128)S(1)} %get-tuple-element.19.ends_ref, f32[2,16,16,128]{3,2,1,0:T(8,128)S(1)} %get-tuple-element.20.edges_ref, bf16[1,32,16,128]{3,2,1,0:T(8,128)(2,1)S(1)} %get-tuple-element.34.xfirst_ref, ...), custom_call_target="tpu_custom_call" | custom-call | flops 1000000000 | bytes 3000000 | tf_op jit(solution)/shard_map/border/pallas_call | solution.py:393
  74.1 11.7 %add_rows.1 = (bf16[16,32,16,128]{3,2,1,0:T(8,128)(2,1)S(1)}, bf16[1,32,16,128]{3,2,1,0:T(8,128)(2,1)S(1)}, bf16[16,1,16,128]{3,2,1,0:T(8,128)(2,1)S(1)}, bf16[1,1,16,128]{3,2,1,0:T(8,128)(2,1)S(1)}) custom-call(bf16[8448,128]{1,0:T(8,128)(2,1)S(1)} %bitcast.7, f32[8192,128]{1,0:T(8,128)} %bitcast.8, f32[2,16,2,16,128]{4,3,2,1,0:T(8,128)S(1)} %get-tuple-element.21.ends_ref, ...), custom_call_target="tpu_custom_call" | custom-call | flops 100000000 | bytes 8000000 | tf_op jit(solution)/shard_map/add_rows/pallas_call | solution.py:192
  85.7 1.9 %collective-permute-start.8 = (bf16[1,32,16,128]{3,2,1,0:T(8,128)(2,1)S(1)}, bf16[1,32,16,128]{3,2,1,0:T(8,128)(2,1)S(1)}, u32[]{:S(2)}, u32[]{:S(2)}) collective-permute-start(bf16[1,32,16,128]{3,2,1,0:T(8,128)(2,1)S(1)} %get-tuple-element.24), channel_id=1, source_target_pairs={{0,1},{1,2},{2,3},{4,5},{5,6},{6,7},{8,9},{9,10},{10,11},{12,13},{... | collective-permute-start | bytes 393224 | tf_op jit(solution)/shard_map/ppermute | solution.py:555
  87.7 15.4 %collective-permute-start.9 = (bf16[16,1,16,128]{3,2,1,0:T(8,128)(2,1)S(1)}, bf16[16,1,16,128]{3,2,1,0:T(8,128)(2,1)S(1)}, u32[]{:S(2)}, u32[]{:S(2)}) collective-permute-start(bf16[16,1,16,128]{3,2,1,0:T(8,128)(2,1)S(1)} %get-tuple-element.25), channel_id=1, source_target_pairs={{0,4},{1,5},{2,6},{3,7},{4,8},{5,9},{6,10},{7,11},{8,12},{9,13},{1... | collective-permute-start | bytes 196616 | tf_op jit(solution)/shard_map/ppermute | solution.py:555
  103.1 2.2 %collective-permute-start.10 = (bf16[1,1,16,128]{3,2,1,0:T(8,128)(2,1)S(1)}, bf16[1,1,16,128]{3,2,1,0:T(8,128)(2,1)S(1)}, u32[]{:S(2)}, u32[]{:S(2)}) collective-permute-start(bf16[1,1,16,128]{3,2,1,0:T(8,128)(2,1)S(1)} %get-tuple-element.26), channel_id=1, source_target_pairs={{0,5},{1,6},{2,7},{4,9},{5,10},{6,11},{8,13},{9,14},{10,15},{12,17... | collective-permute-start | bytes 12296 | tf_op jit(solution)/shard_map/ppermute | solution.py:555
  105.2 0.0 copy-start.1
  105.2 1.0 local_taps.1.taps_ref
  106.3 3.5 %collective-permute-done.10.corner_ref = bf16[1,1,16,128]{3,2,1,0:T(8,128)(2,1)S(1)} collective-permute-done((bf16[1,1,16,128]{3,2,1,0:T(8,128)(2,1)S(1)}, bf16[1,1,16,128]{3,2,1,0:T(8,128)(2,1)S(1)}, u32[]{:S(2)}, u32[]{:S(2)}) %collective-permute-start.10) | collective-permute-done | bytes 4128 | tf_op jit(solution)/shard_map/ppermute | solution.py:555
  109.8 3.1 %lower.1 = bf16[8,16,8,256]{3,2,1,0:T(8,128)(2,1)} custom-call(bf16[2,8,128,1152]{3,2,1,0:T(8,128)(2,1)S(1)} %local_taps.1.taps_ref, bf16[1,32,16,128]{3,2,1,0:T(8,128)(2,1)S(1)} %collective-permute-done.8.front_ref, bf16[16,1,16,128]{3,2,1,0:T(8,128)(2,1)S(1)} %collective-permute-done.9.side_ref, ...), custom_call_target="tpu_custom_call" | custom-call | flops 1811939328 | bytes 5000000 | tf_op jit(solution)/shard_map/lower/pallas_call | solution.py:529
  (11 shorter events, 0.0 us)
Async XLA Ops:
  6.7 48.8 %copy-start.3 = (bf16[27,128,128]{2,1,0:T(8,128)(2,1)S(1)}, bf16[27,128,128]{2,1,0:T(8,128)(2,1)}, u32[]{:S(2)}) copy-start(bf16[27,128,128]{2,1,0:T(8,128)(2,1)} %w_ref.3) | copy-start | bytes 2654212
  6.7 67.3 %all-to-all-start = ((bf16[32,264,128]{2,1,0:T(8,128)(2,1)}), bf16[32,264,128]{2,1,0:T(8,128)(2,1)S(1)}, u32[]{:S(2)}, u32[]{:S(2)}) async-start(bf16[32,264,128]{2,1,0:T(8,128)(2,1)} %bitcast.10), calls=%async_computation | async-start | bytes 4325376 | tf_op jit(solution)/shard_map/all_to_all | solution.py:559
  13.5 22.9 %collective-permute-start.7 = (bf16[1,1,16,128]{3,2,1,0:T(8,128)(2,1)S(1)}, bf16[1,1,16,128]{3,2,1,0:T(8,128)(2,1)S(1)}, u32[]{:S(2)}, u32[]{:S(2)}) collective-permute-start(bf16[1,1,16,128]{3,2,1,0:T(8,128)(2,1)S(1)} %get-tuple-element.27), channel_id=1, source_target_pairs={{5,0},{6,1},{7,2},{9,4},{10,5},{11,6},{13,8},{14,9},{15,10},{17,12... | collective-permute-start | bytes 12296 | tf_op jit(solution)/shard_map/ppermute | solution.py:555
  16.6 33.1 %collective-permute-start.6 = (bf16[1,1,16,128]{3,2,1,0:T(8,128)(2,1)S(1)}, bf16[1,1,16,128]{3,2,1,0:T(8,128)(2,1)S(1)}, u32[]{:S(2)}, u32[]{:S(2)}) collective-permute-start(bf16[1,1,16,128]{3,2,1,0:T(8,128)(2,1)S(1)} %get-tuple-element.28), channel_id=1, source_target_pairs={{1,4},{2,5},{3,6},{5,8},{6,9},{7,10},{9,12},{10,13},{11,14},{13,16... | collective-permute-start | bytes 12296 | tf_op jit(solution)/shard_map/ppermute | solution.py:555
  19.0 32.5 %collective-permute-start.5 = (bf16[1,1,16,128]{3,2,1,0:T(8,128)(2,1)S(1)}, bf16[1,1,16,128]{3,2,1,0:T(8,128)(2,1)S(1)}, u32[]{:S(2)}, u32[]{:S(2)}) collective-permute-start(bf16[1,1,16,128]{3,2,1,0:T(8,128)(2,1)S(1)} %get-tuple-element.29), channel_id=1, source_target_pairs={{4,1},{5,2},{6,3},{8,5},{9,6},{10,7},{12,9},{13,10},{14,11},{16,13... | collective-permute-start | bytes 12296 | tf_op jit(solution)/shard_map/ppermute | solution.py:555
  23.0 49.7 %collective-permute-start.4 = (bf16[1,1,16,128]{3,2,1,0:T(8,128)(2,1)S(1)}, bf16[1,1,16,128]{3,2,1,0:T(8,128)(2,1)S(1)}, u32[]{:S(2)}, u32[]{:S(2)}) collective-permute-start(bf16[1,1,16,128]{3,2,1,0:T(8,128)(2,1)S(1)} %get-tuple-element.30), channel_id=1, source_target_pairs={{0,5},{1,6},{2,7},{4,9},{5,10},{6,11},{8,13},{9,14},{10,15},{12,17... | collective-permute-start | bytes 12296 | tf_op jit(solution)/shard_map/ppermute | solution.py:555
  25.9 46.9 %collective-permute-start.2 = (bf16[16,1,16,128]{3,2,1,0:T(8,128)(2,1)S(1)}, bf16[16,1,16,128]{3,2,1,0:T(8,128)(2,1)S(1)}, u32[]{:S(2)}, u32[]{:S(2)}) collective-permute-start(bf16[16,1,16,128]{3,2,1,0:T(8,128)(2,1)S(1)} %get-tuple-element.31.ylast_ref), channel_id=1, source_target_pairs={{0,4},{1,5},{2,6},{3,7},{4,8},{5,9},{6,10},{7,11},{8,12},{9,13},{1... | collective-permute-start | bytes 196616 | tf_op jit(solution)/shard_map/ppermute | solution.py:555
  36.4 36.4 %collective-permute-start.3 = (bf16[16,1,16,128]{3,2,1,0:T(8,128)(2,1)S(1)}, bf16[16,1,16,128]{3,2,1,0:T(8,128)(2,1)S(1)}, u32[]{:S(2)}, u32[]{:S(2)}) collective-permute-start(bf16[16,1,16,128]{3,2,1,0:T(8,128)(2,1)S(1)} %get-tuple-element.32.yfirst_ref), channel_id=1, source_target_pairs={{4,0},{5,1},{6,2},{7,3},{8,4},{9,5},{10,6},{11,7},{12,8},{13,9},{1... | collective-permute-start | bytes 196616 | tf_op jit(solution)/shard_map/ppermute | solution.py:555
  49.7 23.1 %collective-permute-start = (bf16[1,32,16,128]{3,2,1,0:T(8,128)(2,1)S(1)}, bf16[1,32,16,128]{3,2,1,0:T(8,128)(2,1)S(1)}, u32[]{:S(2)}, u32[]{:S(2)}) collective-permute-start(bf16[1,32,16,128]{3,2,1,0:T(8,128)(2,1)S(1)} %get-tuple-element.33.xlast_ref), channel_id=1, source_target_pairs={{0,1},{1,2},{2,3},{4,5},{5,6},{6,7},{8,9},{9,10},{10,11},{12,13},{... | collective-permute-start | bytes 393224 | tf_op jit(solution)/shard_map/ppermute | solution.py:555
  51.6 21.1 %collective-permute-start.1 = (bf16[1,32,16,128]{3,2,1,0:T(8,128)(2,1)S(1)}, bf16[1,32,16,128]{3,2,1,0:T(8,128)(2,1)S(1)}, u32[]{:S(2)}, u32[]{:S(2)}) collective-permute-start(bf16[1,32,16,128]{3,2,1,0:T(8,128)(2,1)S(1)} %get-tuple-element.34.xfirst_ref), channel_id=1, source_target_pairs={{1,0},{2,1},{3,2},{5,4},{6,5},{7,6},{9,8},{10,9},{11,10},{13,12},{... | collective-permute-start | bytes 393224 | tf_op jit(solution)/shard_map/ppermute | solution.py:555
  55.5 1.6 %copy-start.2 = (bf16[16,32,16,128]{3,2,1,0:T(8,128)(2,1)S(1)}, bf16[16,32,16,128]{3,2,1,0:T(8,128)(2,1)}, u32[]{:S(2)}) copy-start(bf16[16,32,16,128]{3,2,1,0:T(8,128)(2,1)} %level_ref) | copy-start | bytes 6291460
  57.1 15.6 %copy-start.4 = (bf16[27,128,128]{2,1,0:T(8,128)(2,1)S(1)}, bf16[27,128,128]{2,1,0:T(8,128)(2,1)}, u32[]{:S(2)}) copy-start(bf16[27,128,128]{2,1,0:T(8,128)(2,1)} %w_ref.3) | copy-start | bytes 2654212
  70.8 1.9 %copy-start = (f32[16,16,2,16,128]{4,3,2,1,0:T(8,128)}, f32[16,16,2,16,128]{4,3,2,1,0:T(8,128)S(1)}, u32[]{:S(2)}) copy-start(f32[16,16,2,16,128]{4,3,2,1,0:T(8,128)S(1)} %get-tuple-element.18) | copy-start | bytes 12582916
  85.7 24.1 %collective-permute-start.8 = (bf16[1,32,16,128]{3,2,1,0:T(8,128)(2,1)S(1)}, bf16[1,32,16,128]{3,2,1,0:T(8,128)(2,1)S(1)}, u32[]{:S(2)}, u32[]{:S(2)}) collective-permute-start(bf16[1,32,16,128]{3,2,1,0:T(8,128)(2,1)S(1)} %get-tuple-element.24), channel_id=1, source_target_pairs={{0,1},{1,2},{2,3},{4,5},{5,6},{6,7},{8,9},{9,10},{10,11},{12,13},{... | collective-permute-start | bytes 393224 | tf_op jit(solution)/shard_map/ppermute | solution.py:555
  87.7 22.1 %collective-permute-start.9 = (bf16[16,1,16,128]{3,2,1,0:T(8,128)(2,1)S(1)}, bf16[16,1,16,128]{3,2,1,0:T(8,128)(2,1)S(1)}, u32[]{:S(2)}, u32[]{:S(2)}) collective-permute-start(bf16[16,1,16,128]{3,2,1,0:T(8,128)(2,1)S(1)} %get-tuple-element.25), channel_id=1, source_target_pairs={{0,4},{1,5},{2,6},{3,7},{4,8},{5,9},{6,10},{7,11},{8,12},{9,13},{1... | collective-permute-start | bytes 196616 | tf_op jit(solution)/shard_map/ppermute | solution.py:555
  103.1 6.7 %collective-permute-start.10 = (bf16[1,1,16,128]{3,2,1,0:T(8,128)(2,1)S(1)}, bf16[1,1,16,128]{3,2,1,0:T(8,128)(2,1)S(1)}, u32[]{:S(2)}, u32[]{:S(2)}) collective-permute-start(bf16[1,1,16,128]{3,2,1,0:T(8,128)(2,1)S(1)} %get-tuple-element.26), channel_id=1, source_target_pairs={{0,5},{1,6},{2,7},{4,9},{5,10},{6,11},{8,13},{9,14},{10,15},{12,17... | collective-permute-start | bytes 12296 | tf_op jit(solution)/shard_map/ppermute | solution.py:555
  105.2 4.6 %copy-start.1 = (bf16[27,128,256]{2,1,0:T(8,128)(2,1)S(1)}, bf16[27,128,256]{2,1,0:T(8,128)(2,1)}, u32[]{:S(2)}) copy-start(bf16[27,128,256]{2,1,0:T(8,128)(2,1)} %param.11) | copy-start | bytes 5308420
